TPU v7x, 256 devices: a whole 4x4x8 slice. The times are simulated.
256 devices in a mesh: pipe: 2 (over core), dp: 128 (over x, y, z).
Axes of the slice: x: 4, y: 4, z: 8, core: 2. Of those that a mesh axis runs over, the one named last changes fastest.
Arguments:
- tokens: bfloat16 [4, 4096, 2048], P(None, 'dp'), may hold values from -40 to 40
- seg_ids: int32 [4, 4096], P(None, 'dp'), may hold values from 0 to 31, as said below
- cache_row: int32 [4, 4096], P(None, 'dp'), may hold values from 0 to 16383, as said below
- ln_gain: float32 [2, 2048], P('pipe'), may hold values from 0.1 to 1.9
- ln_bias: float32 [2, 2048], P('pipe'), may hold values from -2 to 2
- qkv_weight: bfloat16 [2, 2048, 3072], P('pipe', 'dp'), may hold values from -8 to 8
- qkv_bias: float32 [2, 3072], P('pipe'), may hold values from -3 to 3
- out_weight: bfloat16 [2, 1024, 2048], P('pipe', 'dp'), may hold values from -0.1875 to 0.1875
- out_bias: float32 [2, 2048], P('pipe'), may hold values from -2 to 2
Outputs:
- hidden: bfloat16 [2, 4, 4096, 2048], P('pipe', None, 'dp')
- kv_cache: bfloat16 [2, 16384, 2048], P('pipe', 'dp')
Inputs may be any that keep to these rules, and one draw needn't show every extreme that they name: `seg_ids`: each block of 32 tokens of a micro-batch holds whole prompts, numbered from 0 in order, never crossing the block's edges. In every micro-batch one block holds a single prompt of 32 tokens and another holds 32 prompts of one token. `cache_row`: over all micro-batches each cache row is named once. Rows d * 4 * 32 to (d + 1) * 4 * 32 - 1 belong to index d of dp, which gets 32 of them in each micro-batch. Of the 32 tokens of one index of dp in one micro-batch, each owner gets none or exactly 2.
All inputs are finite; a program needn't handle non-finite values.
Results may differ from a plain program's by a relative error of at most 0.0065.
Values may be sent and summed in bfloat16 or wider, within the bound.
No kernel may reach another device: no remote copies, remote signals or barrier semaphores. Data moves between devices by JAX's collectives and lax.ppermute only.
A program may use at most 128 MiB of HBM per device.

v0:
```python
import functools

import jax
import jax.numpy as jnp
from jax import lax
from jax.experimental import pallas as pl
from jax.experimental.pallas import tpu as pltpu
from jax.sharding import Mesh
from jax.sharding import PartitionSpec as P

HDIM = 256
ROT = 64
HALF = ROT // 2
EPS = 1e-05
META = 128
LANES = 128
TILE = 256
BF = jnp.bfloat16
F32 = jnp.float32
DP = ("x", "y", "z")
PLANE = ("x", "y")
CAP_Z = 48
CAP_P = 32


def swap(value):
    return lax.ppermute(value, "pipe", [(0, 1), (1, 0)])


def mm(a, b):
    return jnp.dot(a, b, preferred_element_type=F32)


def chooser(count, places):
    return (jnp.arange(count, dtype=jnp.int32)[:, None] == places[None, :]).astype(BF)


def slots_of(dest, valid, count, cap):
    rows = dest.shape[0]
    hits = ((dest[:, None] == jnp.arange(count, dtype=jnp.int32)[None, :]) & valid[:, None]).astype(BF)
    number = jnp.arange(rows, dtype=jnp.int32)
    before = mm((number[None, :] < number[:, None]).astype(BF), hits)
    rank = jnp.sum(before * hits.astype(F32), axis=1).astype(jnp.int32)
    fits = valid & (rank < cap)
    return jnp.where(fits, dest * cap + rank, -1), jnp.any(valid & (rank >= cap))


def across(filled, axes, cap):
    cols = filled.shape[1]
    arrived = lax.all_to_all(
        filled.reshape(-1, cap, cols), axes, split_axis=0, concat_axis=0, tiled=True
    )
    return arrived.reshape(-1, cols)


def turns_of(positions):
    lane = jnp.arange(LANES)
    inverse = 10000.0 ** (-2.0 * (lane % HALF).astype(F32) / ROT)
    angles = positions[:, None] * inverse[None, :]
    cosine, sine = jnp.cos(angles), jnp.sin(angles)
    rotated, first = (lane < ROT)[None, :], (lane < HALF)[None, :]
    return jnp.stack(
        [
            jnp.where(rotated, cosine, 1.0),
            jnp.where(first, -sine, 0.0),
            jnp.where(rotated & ~first, sine, 0.0),
        ]
    )


def layer_norm(layer_in, gain_row, shift_row):
    data = layer_in.astype(F32)
    centre = jnp.mean(data, axis=-1, keepdims=True)
    centred = data - centre
    variance = jnp.mean(centred * centred, axis=-1, keepdims=True)
    return (centred * lax.rsqrt(variance + EPS) * gain_row + shift_row).astype(BF)


def rotary(cols, turns):
    parts = []
    for first in range(0, cols.shape[1], HDIM):
        head = cols[:, first : first + LANES]
        parts.append(
            head * turns[0]
            + pltpu.roll(head, LANES - HALF, 1) * turns[1]
            + pltpu.roll(head, HALF, 1) * turns[2]
        )
        parts.append(cols[:, first + LANES : first + HDIM])
    return jnp.concatenate(parts, axis=1).astype(BF)


def attend(queries, key_rows, value_rows, allowed):
    parts = []
    for first in range(0, queries.shape[1], HDIM):
        one = slice(first, first + HDIM)
        scores = lax.dot_general(
            queries[:, one], key_rows[:, one], (((1,), (1,)), ((), ())), preferred_element_type=F32
        ) * HDIM ** (-0.5)
        scores = jnp.where(allowed > 0, scores, -1e30)
        exp_scores = jnp.exp(scores - jnp.max(scores, axis=-1, keepdims=True))
        probs = (exp_scores / jnp.sum(exp_scores, axis=-1, keepdims=True)).astype(BF)
        parts.append(mm(probs, value_rows[:, one]).astype(BF))
    return jnp.concatenate(parts, axis=1)


def conclude(projected, turns, allowed_ref, out_ref):
    turns = [turns[k] for k in range(3)]
    if allowed_ref is None:
        half = projected.shape[1] // 2
        out_ref[:, :half] = rotary(projected[:, :half], turns)
        out_ref[:, half:] = projected[:, half:].astype(BF)
    else:
        third = projected.shape[1] // 3
        queries = rotary(projected[:, :third], turns)
        key_rows = rotary(projected[:, third : 2 * third], turns)
        value_rows = projected[:, 2 * third :].astype(BF)
        out_ref[...] = attend(queries, key_rows, value_rows, allowed_ref[...])


NEAR = ((0, 0, 4), (1, 0, 4), (3, 0, 4))
FAR = ((2, 0, 2), (2, 2, 2))


def cut(whole, normed):
    for k in range(normed.shape[0]):
        normed[k] = whole[:, k * LANES : (k + 1) * LANES]


def add_pieces(place, normed, parts, pieces, base, total, skipped):
    def left_hand(which, k, first, count):
        blocks = []
        for j in range(first, first + count):
            x_step, y_step = (k, j) if which == 0 else (j, k)
            x = lax.rem(place[0] + x_step, 4)
            y = lax.rem(place[1] + y_step, 4)
            blocks.append(normed[x * 4 + y])
        return jnp.concatenate(blocks, axis=1)

    def tile(which, number):
        column = pl.ds(pl.multiple_of(number * TILE, TILE), TILE)
        of_ring = pieces[len(parts) * which : len(parts) * (which + 1)]
        target = pl.ds(pl.multiple_of((3 * which + number) * TILE - skipped, TILE), TILE)
        result = jnp.broadcast_to(base[:, target], (total.shape[0], TILE))
        for part, piece in zip(parts, of_ring):
            result = result + mm(left_hand(which, *part), piece[:, column])
        total[:, target] = result

    for which in range(2):
        pl.loop(0 if which else skipped // TILE, 3)(functools.partial(tile, which))


def near_kernel(place, layer_in, gain, shift, bias, *rest):
    pieces, total, normed = rest[:-2], rest[-2], rest[-1]
    cut(layer_norm(layer_in[...], gain[...], shift[...]), normed)
    add_pieces(place, normed, NEAR, pieces, bias, total, 0)


def far_kernel(place, normed, near, turns, allowed, *rest):
    pieces, out_ref, total = rest[:-2], rest[-2], rest[-1]
    add_pieces(place, normed, FAR, pieces, near, total, 0)
    conclude(total[...], turns, allowed, out_ref)


def own_kernel(place, layer_in, gain, shift, bias, turns, *rest):
    pieces, out_ref, normed, total = rest[:-3], rest[-3], rest[-2], rest[-1]
    cut(layer_norm(layer_in[...], gain[...], shift[...]), normed)
    add_pieces(place, normed, NEAR + FAR, pieces, bias, total, 2 * TILE)
    conclude(total[...], turns, None, out_ref)


def unpack_kernel(came, own, marks):
    blocks = came.shape[1] // LANES
    last = came[:, (blocks - 1) * LANES :].astype(F32)
    lane = lax.broadcasted_iota(jnp.int32, last.shape, 1)
    named = jnp.sum(jnp.where(lane == 0, last, 0.0), axis=1, keepdims=True)
    take = (lane.astype(F32) + 1.0 == named).astype(BF)
    for first in range(0, blocks * LANES, 4 * LANES):
        part = came[:, first : min(first + 4 * LANES, blocks * LANES)]
        own[:, first : first + part.shape[1]] = lax.dot_general(
            take, part, (((0,), (0,)), ((), ())), preferred_element_type=F32
        ).astype(BF)
    marks[...] = jnp.sum(came[:, 8 * LANES : 9 * LANES].astype(F32), axis=0, keepdims=True)


def whole_kernel(with_context, layer_in, gain, shift, bias, turns, *rest):
    allowed, rest = (rest[0], rest[1:]) if with_context else (None, rest)
    weights, out_ref, normed, total = rest[:-3], rest[-3], rest[-2], rest[-1]
    step = pl.program_id(0)
    depth = weights[0].shape[0]

    @pl.when(step == 0)
    def _():
        whole = layer_norm(layer_in[...], gain[...], shift[...])
        for k in range(normed.shape[0]):
            normed[k] = whole[:, k * depth : (k + 1) * depth]
        total[...] = jnp.broadcast_to(bias[...], total.shape)

    part = normed[step]
    first = 0
    for one in weights:
        width = one.shape[1]
        total[:, first : first + width] += mm(part, one[...])
        first += width

    @pl.when(step == pl.num_programs(0) - 1)
    def _():
        conclude(total[...], turns, allowed, out_ref)


def cost(rows, width, cols):
    return pl.CostEstimate(flops=rows * cols, bytes_accessed=rows * cols, transcendentals=0)


def call(kernel, place, operands, out_shape, scratch, columns):
    rows = 128
    in_specs = [pl.BlockSpec(memory_space=pltpu.VMEM)] * len(operands)
    if place is not None:
        operands = [place, *operands]
        in_specs = [pl.BlockSpec(memory_space=pltpu.SMEM), *in_specs]
    return pl.pallas_call(
        kernel,
        out_shape=out_shape,
        in_specs=in_specs,
        out_specs=jax.tree.map(lambda one: pl.BlockSpec(memory_space=pltpu.VMEM), out_shape),
        scratch_shapes=[pltpu.VMEM(*one) for one in scratch],
        cost_estimate=cost(rows, rows, columns),
        compiler_params=pltpu.CompilerParams(vmem_limit_bytes=24 << 20),
    )(*operands)


def of(shape, dtype):
    return jax.ShapeDtypeStruct(shape, dtype)


def context_by_pieces(place, layer_in, vectors, turns, allowed, pieces):
    rows = layer_in.shape[0]
    columns = vectors[2].shape[1]
    sums, blocks = of((rows, columns), F32), of((16, rows, LANES), BF)
    near = [*pieces[:3], *pieces[5:8]]
    far = [*pieces[3:5], *pieces[8:]]
    total, normed = call(near_kernel, place, [layer_in, *vectors, *near], (sums, blocks), [], columns)
    return call(
        far_kernel,
        place,
        [normed, total, turns, allowed, *far],
        of((rows, 512), BF),
        [((rows, columns), F32)],
        columns,
    )


def own_by_pieces(place, layer_in, vectors, turns, pieces):
    rows = layer_in.shape[0]
    gain, shift, bias = vectors
    bias = bias[:, 512:]
    return call(
        own_kernel,
        place,
        [layer_in, gain, shift, bias, turns, *pieces],
        of((rows, 1024), BF),
        [((16, rows, LANES), BF), ((rows, 1024), F32)],
        1024,
    )


def project_whole(layer_in, vectors, turns, allowed, gathered):
    rows, width = layer_in.shape
    gain, shift, bias = vectors
    with_context = allowed is not None
    out_cols = 512 if with_context else 1024
    if not with_context:
        bias = bias[:, 512:]
    operands = [layer_in, gain, shift, bias, turns, *((allowed,) if with_context else ())]
    depth = 512
    columns = (0, 1, 2) if with_context else (1, 2)
    return pl.pallas_call(
        functools.partial(whole_kernel, with_context),
        grid=(width // depth,),
        out_shape=jax.ShapeDtypeStruct((rows, out_cols), BF),
        in_specs=[
            pl.BlockSpec(one.shape, lambda k, rank=one.ndim: (0,) * rank) for one in operands
        ]
        + [pl.BlockSpec((depth, 512), lambda k, col=col: (k, col)) for col in columns],
        out_specs=pl.BlockSpec((rows, out_cols), lambda k: (0, 0)),
        scratch_shapes=[
            pltpu.VMEM((width // depth, rows, depth), BF),
            pltpu.VMEM((rows, bias.shape[1]), F32),
        ],
        cost_estimate=cost(rows, width, bias.shape[1]),
        compiler_params=pltpu.CompilerParams(vmem_limit_bytes=24 << 20),
    )(*operands, *[pltpu.with_memory_space_constraint(gathered, pltpu.HBM)] * len(columns))


def shifted(value, axis, by):
    size = lax.axis_size(axis)
    return lax.ppermute(value, axis, [(one, (one + by) % size) for one in range(size)])


def rings(blocks, axes, halves):
    size = lax.axis_size(axes[0])
    found = [{0: [block]} for block in blocks]
    ups = downs = list(blocks)
    for step in range(1, size // 2):
        ups = [shifted(up, axis, 1) for up, axis in zip(ups, axes)]
        downs = [shifted(down, axis, -1) for down, axis in zip(downs, axes)]
        ups, downs = lax.optimization_barrier((ups, downs))
        for one, up, down in zip(found, ups, downs):
            one[size - step], one[step] = [up], [down]
    for one, up, down, axis in zip(found, ups, downs, axes):
        rows = up.shape[0] // 2
        if halves:
            one[size // 2] = [shifted(up[:rows], axis, 1), shifted(down[rows:], axis, -1)]
        else:
            one[size // 2] = [shifted(up, axis, 1)]
    return [[one[k] for k in range(size)] for one in found]


def column_of(shard, later):
    size, index = lax.axis_size("z"), lax.axis_index("z")
    block, step = shard[None], size // 2
    while step:
        got = lax.ppermute(block, "z", [(one, one ^ step) for one in range(size)])
        upper = (index // step) % 2 == 1
        both = [jnp.where(upper, got, block), jnp.where(upper, block, got)]
        block = jnp.stack(both, axis=1).reshape(-1, *shard.shape)
        if step == size // 2:
            block, later = lax.optimization_barrier((block, later))
        step //= 2
    return block.reshape(-1, shard.shape[1]), later


def pieces_of(ring):
    half = ring.shape[1] // 2
    pair = rings([ring[:, :half], ring[:, half:]], ["y", "x"], False)
    pair = [jnp.concatenate([one[0] for one in each], axis=0) for each in pair]
    pair = lax.optimization_barrier(pair)
    order = []
    for each in rings(pair, ["x", "y"], True):
        order += [*each[0], *each[1], *each[3], *each[2]]
    return order


def shards(
    tokens, seg_ids, cache_row, ln_gain, ln_bias, qkv_weight, qkv_bias, out_weight, out_bias
):
    micro_count, row_count, width = tokens.shape
    device_count = lax.axis_size(DP)
    first_core = lax.axis_index("pipe") == 0
    cache_size = micro_count * row_count
    slot_cap = 2 * micro_count * ((row_count + device_count - 1) // device_count)
    head_width = qkv_weight.shape[2] // 3
    part = head_width // 2
    half_width = width // 2

    def pick(a, b):
        return jnp.where(first_core, a, b)

    def joined(piece):
        other = swap(piece)
        return jnp.concatenate([pick(piece, other), pick(other, piece)], axis=1)

    def packed(which):
        cuts = [
            qkv_weight[0][:, kind * head_width + which * part : kind * head_width + (which + 1) * part]
            for kind in range(3)
        ]
        begin = which * half_width
        out_cut = jnp.concatenate(
            [out_weight[0][:, begin : begin + part], out_weight[0][:, begin + part : begin + 2 * part]],
            axis=0,
        )
        return jnp.concatenate([*cuts, out_cut], axis=1)

    low, high = packed(0), packed(1)
    kept = pick(low, high)
    got = swap(pick(high, low))
    shard0, shard1 = pick(kept, got), pick(got, kept)
    bulk = jnp.concatenate([shard1, shard0[:, 3 * part :]], axis=1)
    gathered = lax.all_gather(bulk, DP, axis=0, tiled=True)
    column, (seg_ids, cache_row, ln_gain) = column_of(
        shard0[:, : 3 * part], (seg_ids, cache_row, ln_gain)
    )

    vectors = jnp.concatenate([ln_gain[0], ln_bias[0], qkv_bias[0], out_bias[0]])
    vectors_got = swap(vectors)

    def vectors_of(layer):
        vec = pick(vectors, vectors_got) if layer == 0 else pick(vectors_got, vectors)
        rest = vec[2 * width :]
        bias = [
            pick(
                rest[kind * head_width : kind * head_width + part],
                rest[kind * head_width + part : (kind + 1) * head_width],
            )
            for kind in range(3)
        ]
        out_b = rest[3 * head_width :]
        rows = (vec[None, :width], vec[None, width : 2 * width], jnp.concatenate(bias)[None, :])
        return rows, pick(out_b[:half_width], out_b[half_width:])

    (rows0, out_bias0), (rows1, out_bias1) = vectors_of(0), vectors_of(1)

    flat = tokens.reshape(cache_size, width)
    seg = seg_ids.reshape(cache_size)
    rows = cache_row.reshape(cache_size)
    order = jnp.arange(cache_size, dtype=jnp.int32)
    micro = order // row_count
    same_micro = micro[:, None] == micro[None, :]
    positions = (order % row_count) - jnp.sum(
        (same_micro & (seg[None, :] < seg[:, None])).astype(jnp.int32), axis=1
    )
    earlier = order[None, :] <= order[:, None]
    allowed = (same_micro & earlier & (seg[:, None] == seg[None, :])).astype(F32)
    owners = rows // cache_size
    rank = jnp.sum(
        (same_micro & earlier & (owners[:, None] == owners[None, :])).astype(jnp.int32), axis=1
    ) - 1
    slot = owners * slot_cap + micro * (slot_cap // micro_count) + rank
    depth = lax.axis_size("z")
    lane = jnp.arange(META, dtype=jnp.int32)[None, :]
    meta = jnp.where(
        lane == 0,
        (rows % cache_size + 1)[:, None],
        jnp.where(lane == 1, positions[:, None], jnp.where(lane == 2, (owners // depth)[:, None], 0)),
    ).astype(BF)
    half_tokens = pick(flat[:, :half_width], flat[:, half_width:])
    payload = jnp.concatenate([half_tokens, meta], axis=1)
    flag_at = half_width + 3

    def flagged(filled, flag, at):
        mark = (jnp.arange(filled.shape[1]) == at).astype(BF)[None, :]
        return filled + flag.astype(BF) * mark

    slot_z, out_z = slots_of(owners % depth, rows >= 0, depth, CAP_Z)
    send_z = chooser(depth * CAP_Z, slot_z)
    filled = flagged(mm(send_z, payload).astype(BF), out_z, flag_at)
    place = jnp.stack([lax.axis_index("x"), lax.axis_index("y")]).astype(jnp.int32)
    turns = turns_of(positions.astype(F32))
    filled, column, turns, allowed, send_z, place, rows0 = lax.optimization_barrier(
        (filled, column, turns, allowed, send_z, place, rows0)
    )
    middle = across(filled, "z", CAP_Z)
    pieces = pieces_of(column)
    slot_p, out_p = slots_of(
        middle[:, half_width + 2].astype(jnp.int32),
        middle[:, half_width] > 0,
        device_count // depth,
        CAP_P,
    )
    slots_p = device_count // depth * CAP_P
    send_p = chooser(slots_p, slot_p)
    ran_out = out_p | jnp.any(middle[:, flag_at] > 0)

    context0 = context_by_pieces(place, flat, rows0, turns, allowed, pieces)
    filled = jnp.where(ran_out, jnp.nan, mm(send_z, context0)).astype(BF)
    middle0 = across(filled, "z", CAP_Z)
    leg = jnp.concatenate([middle[:, :half_width], middle0, middle[:, half_width:]], axis=1)
    leg = mm(send_p, leg).astype(BF)
    wide = half_width + part
    arrived = across(leg, PLANE, CAP_P)
    gathered, leg_mark = lax.optimization_barrier((gathered, leg[0, half_width]))

    def finish(half, context, out, out_b):
        done = jnp.concatenate([mm(context, one) for one in out], axis=1)
        done = (half.astype(F32) + done + out_b).astype(BF)
        return done, joined(done)

    def out_of(begin):
        cut = gathered[:, begin : begin + part].reshape(device_count, 2, -1, part)
        return [cut[:, k].reshape(head_width, part) for k in range(2)]

    out0, out1 = out_of(4 * part), out_of(3 * part)
    hidden0_half, hidden0 = finish(half_tokens, joined(context0), out0, out_bias0)
    context1 = project_whole(hidden0, rows1, turns, allowed, gathered)
    arrived, context1 = lax.optimization_barrier((arrived, context1))
    _, hidden1 = finish(hidden0_half, joined(context1), out1, out_bias1)

    def places(came_meta):
        return came_meta[:, 0].astype(jnp.int32) - 1

    def straight():
        row = jnp.concatenate([half_tokens, context0, meta], axis=1)
        fill = chooser(device_count * slot_cap, slot)
        blocks = row.shape[1] // META

        def some_columns(step, state):
            take, own = state
            begin = (blocks - 1 - step) * META
            part_of = lax.dynamic_slice_in_dim(row, begin, META, 1)
            came = across(mm(fill, part_of).astype(BF), DP, slot_cap)
            take = jnp.where(step == 0, chooser(cache_size, places(came)), take)
            return take, lax.dynamic_update_slice(own, mm(take, came).astype(BF), (0, begin))

        state = (jnp.zeros((cache_size, device_count * slot_cap), BF), jnp.zeros_like(row))
        return lax.fori_loop(0, blocks, some_columns, state)[1]

    own, marks = call(
        unpack_kernel,
        None,
        [arrived],
        (of((cache_size, arrived.shape[1]), BF), of((1, LANES), F32)),
        [],
        arrived.shape[1],
    )
    ran_out = jnp.isnan(marks[0, 0]) | jnp.isnan(leg_mark.astype(F32))
    own = lax.cond(ran_out, straight, lambda: own)
    own_part, own_meta = own[:, :wide], own[:, wide:]
    own_turns = turns_of(own_meta[:, 1].astype(F32))
    other = swap(own_part)
    lower, upper = pick(own_part, other), pick(other, own_part)
    own_tokens = jnp.concatenate([lower[:, :half_width], upper[:, :half_width]], axis=1)
    own_context0 = jnp.concatenate([lower[:, half_width:], upper[:, half_width:]], axis=1)
    own_kv0 = own_by_pieces(place, own_tokens, rows0, own_turns, pieces)
    _, own_hidden0 = finish(own_part[:, :half_width], own_context0, out0, out_bias0)
    own_kv1 = project_whole(own_hidden0, rows1, own_turns, None, gathered)

    kept_kv = pick(own_kv0, own_kv1)
    got_kv = swap(pick(own_kv1, own_kv0))
    low_kv, high_kv = pick(kept_kv, got_kv), pick(got_kv, kept_kv)
    cache = jnp.concatenate(
        [low_kv[:, :part], high_kv[:, :part], low_kv[:, part:], high_kv[:, part:]], axis=1
    )
    hidden = pick(hidden0, hidden1).reshape(1, micro_count, row_count, width)
    return hidden, cache[None]


def solution(mesh):
    torus = Mesh(mesh.devices.reshape(2, 4, 4, 8), ("pipe", *DP))
    placed = (
        P(None, DP, None),
        P(None, DP),
        P(None, DP),
        P("pipe", None),
        P("pipe", None),
        P("pipe", DP, None),
        P("pipe", None),
        P("pipe", DP, None),
        P("pipe", None),
    )
    return jax.shard_map(
        shards,
        mesh=torus,
        in_specs=placed,
        out_specs=(P("pipe", None, DP, None), P("pipe", DP, None)),
        check_vma=False,
    )
```

profile of v0, /device:TPU:1, one launch (start us, length us, event | category | flops | bytes accessed | tf_op | source)
XLA Modules:
  0.0 207.5 jit_solution(4263310627907438268)
XLA Ops:
  7.3 0.8 fusion.80
  8.0 0.8 fusion.77
  8.9 3.3 %collective-permute-start = (bf16[16,2048]{1,0:T(8,128)(2,1)S(1)}, bf16[16,2048]{1,0:T(8,128)(2,1)S(1)}, u32[]{:S(2)}, u32[]{:S(2)}) collective-permute-start(bf16[16,2048]{1,0:T(8,128)(2,1)S(1)} %broadcast_select_fusion.18), channel_id=1, source_target_pairs={{0,128},{128,0},{1,129},{129,1},{2,130},{130,2},{3,131},{131,3},{4... | collective-permute-start | bytes 196616 | tf_op jit(solution)/shard_map/ppermute | solution.py:27
  12.2 0.9 collective-permute-done
  14.0 1.1 slice_select_fusion
  15.0 5.3 %collective-permute-start.1 = (bf16[1,16,1536]{2,1,0:T(8,128)(2,1)S(1)}, bf16[1,16,1536]{2,1,0:T(8,128)(2,1)S(1)}, u32[]{:S(2)}, u32[]{:S(2)}) collective-permute-start(bf16[1,16,1536]{2,1,0:T(8,128)(2,1)S(1)} %slice_bitcast_fusion.10), channel_id=1, source_target_pairs={{0,4},{1,5},{2,6},{3,7},{4,0},{5,1},{6,2},{7,3},{8,12},{9,13},{10,... | collective-permute-start | bytes 147464 | tf_op jit(solution)/shard_map/ppermute | solution.py:322
  20.4 1.7 collective-permute-done.1
  25.2 1.5 collective-permute-start.4
  26.7 2.4 %collective-permute-start.2 = (bf16[2,16,1536]{2,1,0:T(8,128)(2,1)S(1)}, bf16[2,16,1536]{2,1,0:T(8,128)(2,1)S(1)}, u32[]{:S(2)}, u32[]{:S(2)}) collective-permute-start(bf16[2,16,1536]{2,1,0:T(8,128)(2,1)S(1)} %maximum_bitcast_fusion.1), channel_id=1, source_target_pairs={{0,2},{1,3},{2,0},{3,1},{4,6},{5,7},{6,4},{7,5},{8,10},{9,11},{10,... | collective-permute-start | bytes 294920 | tf_op jit(solution)/shard_map/ppermute | solution.py:322
  30.4 0.7 and_convert_fusion
  31.5 1.4 fusion.12
  33.5 1.0 collective-permute-done.2
  34.7 6.2 %collective-permute-done.3 = bf16[4,16,1536]{2,1,0:T(8,128)(2,1)S(1)} collective-permute-done((bf16[4,16,1536]{2,1,0:T(8,128)(2,1)S(1)}, bf16[4,16,1536]{2,1,0:T(8,128)(2,1)S(1)}, u32[]{:S(2)}, u32[]{:S(2)}) %collective-permute-start.3) | collective-permute-done | bytes 196640 | tf_op jit(solution)/shard_map/ppermute | solution.py:322
  41.0 6.3 %all-to-all-start.1 = ((bf16[8,48,1152]{2,1,0:T(8,128)(2,1)}), bf16[8,48,1152]{2,1,0:T(8,128)(2,1)}, u32[]{:S(2)}, u32[]{:S(2)}) async-start(bf16[8,48,1152]{2,1,0:T(8,128)(2,1)} %bitcast.21), calls=%async_computation.1 | async-start | bytes 1769472 | tf_op jit(solution)/shard_map/all_to_all | solution.py:50
  47.4 3.0 %collective-permute-start.8 = (bf16[128,768]{1,0:T(8,128)(2,1)S(1)}, bf16[128,768]{1,0:T(8,128)(2,1)S(1)}, u32[]{:S(2)}, u32[]{:S(2)}) collective-permute-start(bf16[128,768]{1,0:T(8,128)(2,1)S(1)} %get-tuple-element.325), channel_id=1, source_target_pairs={{0,96},{32,0},{64,32},{96,64},{1,97},{33,1},{65,33},{97,65},{2,98}... | collective-permute-start | bytes 589832 | tf_op jit(solution)/shard_map/ppermute | solution.py:296
  50.4 3.0 %collective-permute-start.7 = (bf16[128,768]{1,0:T(8,128)(2,1)S(1)}, bf16[128,768]{1,0:T(8,128)(2,1)S(1)}, u32[]{:S(2)}, u32[]{:S(2)}) collective-permute-start(bf16[128,768]{1,0:T(8,128)(2,1)S(1)} %get-tuple-element.326), channel_id=1, source_target_pairs={{0,24},{8,0},{16,8},{24,16},{1,25},{9,1},{17,9},{25,17},{2,26},{10... | collective-permute-start | bytes 589832 | tf_op jit(solution)/shard_map/ppermute | solution.py:296
  53.4 3.1 %collective-permute-done.6 = bf16[128,768]{1,0:T(8,128)(2,1)S(1)} collective-permute-done((bf16[128,768]{1,0:T(8,128)(2,1)S(1)}, bf16[128,768]{1,0:T(8,128)(2,1)S(1)}, u32[]{:S(2)}, u32[]{:S(2)}) %collective-permute-start.6) | collective-permute-done | bytes 196640 | tf_op jit(solution)/shard_map/ppermute | solution.py:296
  56.5 3.0 %collective-permute-done.5 = bf16[128,768]{1,0:T(8,128)(2,1)S(1)} collective-permute-done((bf16[128,768]{1,0:T(8,128)(2,1)S(1)}, bf16[128,768]{1,0:T(8,128)(2,1)S(1)}, u32[]{:S(2)}, u32[]{:S(2)}) %collective-permute-start.5) | collective-permute-done | bytes 196640 | tf_op jit(solution)/shard_map/ppermute | solution.py:296
  59.8 5.9 %collective-permute-done.9 = bf16[128,768]{1,0:T(8,128)(2,1)S(1)} collective-permute-done((bf16[128,768]{1,0:T(8,128)(2,1)S(1)}, bf16[128,768]{1,0:T(8,128)(2,1)S(1)}, u32[]{:S(2)}, u32[]{:S(2)}) %collective-permute-start.9) | collective-permute-done | bytes 196640 | tf_op jit(solution)/shard_map/ppermute | solution.py:296
  65.8 2.8 %collective-permute-start.13 = (bf16[512,768]{1,0:T(8,128)(2,1)S(1)}, bf16[512,768]{1,0:T(8,128)(2,1)S(1)}, u32[]{:S(2)}, u32[]{:S(2)}) collective-permute-start(bf16[512,768]{1,0:T(8,128)(2,1)S(1)} %pad_maximum_fusion.1.rest_0_), channel_id=1, source_target_pairs={{0,96},{32,0},{64,32},{96,64},{1,97},{33,1},{65,33},{97,65},{2,98}... | collective-permute-start | bytes 2359304 | tf_op jit(solution)/shard_map/ppermute | solution.py:296
  68.6 1.4 collective-permute-start.14
  71.2 19.0 %collective-permute-done.13.rest_1_ = bf16[512,768]{1,0:T(8,128)(2,1)S(1)} collective-permute-done((bf16[512,768]{1,0:T(8,128)(2,1)S(1)}, bf16[512,768]{1,0:T(8,128)(2,1)S(1)}, u32[]{:S(2)}, u32[]{:S(2)}) %collective-permute-start.13) | collective-permute-done | bytes 786464 | tf_op jit(solution)/shard_map/ppermute | solution.py:296
  90.8 0.9 slice.257
  91.6 0.8 slice.256
  92.4 0.8 slice.259
  93.2 0.8 slice.258
  94.0 2.0 collective-permute-start.17
  96.7 2.7 %collective-permute-start.16 = (bf16[256,768]{1,0:T(8,128)(2,1)}, bf16[256,768]{1,0:T(8,128)(2,1)S(1)}, u32[]{:S(2)}, u32[]{:S(2)}) collective-permute-start(bf16[256,768]{1,0:T(8,128)(2,1)} %slice.257), channel_id=1, source_target_pairs={{0,96},{32,0},{64,32},{96,64},{1,97},{33,1},{65,33},{97,65},{2,98}... | collective-permute-start | bytes 1179656 | tf_op jit(solution)/shard_map/ppermute | solution.py:296
  99.4 2.7 %shard_map.104 = (f32[128,1536]{1,0:T(8,128)S(1)}, bf16[16,128,128]{2,1,0:T(8,128)(2,1)S(1)}) custom-call(s32[2]{0:T(128)S(1)} %pad_add_fusion.place, bf16[128,2048]{1,0:T(8,128)(2,1)S(1)} %bitcast.89, f32[1,2048]{1,0:T(1,128)S(1)} %bitcast.93, f32[1,2048]{1,0:T(1,128)S(1)} %bitcast.91, f32[1,1536]{1,0:T(1,128)S(1)} %broadcast_in_dim.183.bias, ...), custom_call_target="tpu_custom_call" | custom-call | flops 196608 | bytes 196608 | tf_op jit(solution)/shard_map/pallas_call | solution.py:220
  102.1 0.9 copy-done.18
  103.0 0.8 copy-done.22
  103.8 1.2 fusion.37
  105.0 1.9 compare_reduce_fusion
  109.1 1.6 copy-done.19
  110.7 1.0 copy-done.23
  111.8 3.3 %shard_map.105 = bf16[128,512]{1,0:T(8,128)(2,1)} custom-call(s32[2]{0:T(128)S(1)} %pad_add_fusion.place, bf16[16,128,128]{2,1,0:T(8,128)(2,1)S(1)} %copy-done.23, f32[128,1536]{1,0:T(8,128)S(1)} %copy-done.19, f32[3,128,128]{2,1,0:T(8,128)S(1)} %pad_maximum_fusion.11.turns, f32[128,128]{1,0:T(8,128)S(1)} %get-tuple-element.266.allowed.rest_0_, ...), custom_call_target="tpu_custom_call" | custom-call | flops 196608 | bytes 196608 | tf_op jit(solution)/shard_map/pallas_call | solution.py:220
  115.0 1.9 fusion.18
  117.0 7.4 %all-to-all-start.2 = ((bf16[8,48,512]{2,1,0:T(8,128)(2,1)}), bf16[8,48,512]{2,1,0:T(8,128)(2,1)}, u32[]{:S(2)}, u32[]{:S(2)}) async-start(bf16[8,48,512]{2,1,0:T(8,128)(2,1)} %bitcast.112), calls=%async_computation.2 | async-start | bytes 786432 | tf_op jit(solution)/shard_map/all_to_all | solution.py:50
  124.4 1.3 slice_select_fusion.1
  125.7 1.4 slice_select_fusion.5
  127.0 1.5 slice.327
  128.6 2.1 %slice.325 = bf16[384,1024]{1,0:T(8,128)(2,1)} slice(bf16[384,1152]{1,0:T(8,128)(2,1)} %bitcast.22), slice={[0:384], [0:1024]} | slice | bytes 1572864 | tf_op jit(solution)/shard_map/slice | solution.py:457
  130.7 8.5 %collective-permute-start.19 = (bf16[128,512]{1,0:T(8,128)(2,1)}, bf16[128,512]{1,0:T(8,128)(2,1)S(1)}, u32[]{:S(2)}, u32[]{:S(2)}) collective-permute-start(bf16[128,512]{1,0:T(8,128)(2,1)} %shard_map.105), channel_id=1, source_target_pairs={{0,128},{128,0},{1,129},{129,1},{2,130},{130,2},{3,131},{131,3},{4... | collective-permute-start | bytes 393224 | tf_op jit(solution)/shard_map/ppermute | solution.py:27
  140.4 1.6 broadcast_select_fusion.15
  142.0 2.4 %convolution_convert_fusion.2 = bf16[512,1664]{1,0:T(8,128)(2,1)S(1)} fusion(bf16[384,128]{1,0:T(8,128)(2,1)} %slice.327, bf16[384,512]{1,0:T(8,128)(2,1)} %bitcast.24, bf16[384,1024]{1,0:T(8,128)(2,1)} %slice.325, s32[384]{0:T(512)} %add_select_fusion), kind=kOutput, calls=%fused_computation.20 | convolution fusion | flops 659193856 | bytes 2983424 | tf_op jit(solution)/shard_map/dot_general | solution.py:31
  145.6 4.7 %all-to-all-start.3 = ((bf16[16,32,1664]{2,1,0:T(8,128)(2,1)}), bf16[16,32,1664]{2,1,0:T(8,128)(2,1)S(1)}, u32[]{:S(2)}, u32[]{:S(2)}) async-start(bf16[16,32,1664]{2,1,0:T(8,128)(2,1)} %bitcast.110), calls=%async_computation.3 | async-start | bytes 3407872 | tf_op jit(solution)/shard_map/all_to_all | solution.py:50
  150.3 6.9 %all-gather.2.cloned.1.call-done.rest_1_.rest_2_.rest_3_.rest_0_ = bf16[2048,2560]{1,0:T(8,128)(2,1)} async-done(((bf16[16,2560]{1,0:T(8,128)(2,1)}), bf16[2048,2560]{1,0:T(8,128)(2,1)}) %all-gather.2.cloned.1.call-update) | async-done | bytes 10485776 | tf_op jit(solution)/shard_map/all_gather | solution.py:379
  157.2 3.9 %fusion.73 = (bf16[2048,512]{1,0:T(8,128)(2,1)}, bf16[2048,512]{1,0:T(8,128)(2,1)S(1)}) fusion(bf16[2048,2560]{1,0:T(8,128)(2,1)} %all-gather.2.cloned.1.call-done.rest_1_.rest_2_.rest_3_.rest_0_), kind=kLoop, calls=%fused_computation.205 | loop fusion | bytes 8388608 | tf_op jit(solution)/shard_map/slice | solution.py:469
  162.5 0.8 fusion.28
  163.3 0.8 collective-permute-start.20
  164.8 1.3 fusion.78
  170.2 1.1 broadcast_select_fusion.11
  172.1 5.5 %shard_map.106 = bf16[128,512]{1,0:T(8,128)(2,1)S(1)} custom-call(bf16[128,2048]{1,0:T(8,128)(2,1)S(1)} %pad_maximum_fusion.3.layer_in, f32[1,2048]{1,0:T(1,128)S(1)} %bitcast.97, f32[1,2048]{1,0:T(1,128)S(1)} %bitcast.95, f32[1,1536]{1,0:T(1,128)S(1)} %copy-done.31, f32[3,128,128]{2,1,0:T(8,128)S(1)} %pad_maximum_fusion.11.turns, ...), custom_call_target="tpu_custom_call" | custom-call | flops 196608 | bytes 196608 | tf_op jit(solution)/shard_map/pallas_call | solution.py:276
  178.3 1.3 shard_map.107
  179.9 1.1 convert_reduce_fusion.1
  181.4 1.0 slice.345
  183.1 1.5 fusion.21
  185.0 1.2 broadcast_select_fusion.1
  187.0 1.0 fusion.32
  188.2 1.1 fusion.30
  191.4 2.4 %shard_map.108 = bf16[128,1024]{1,0:T(8,128)(2,1)S(1)} custom-call(s32[2]{0:T(128)S(1)} %copy-done.35, bf16[128,2048]{1,0:T(8,128)(2,1)S(1)} %pad_maximum_fusion.4.layer_in, f32[1,2048]{1,0:T(1,128)S(1)} %bitcast.94, f32[1,2048]{1,0:T(1,128)S(1)} %bitcast.92, f32[1,1024]{1,0:T(1,128)S(1)} %copy-done.32, f32[3,128,128]{2,1,0:T(8,128)S(1)} %pad_maximum_fusion.12.turns, ...), custom_call_target="tpu_custom_call" | custom-call | flops 131072 | bytes 131072 | tf_op jit(solution)/shard_map/pallas_call | solution.py:220
  193.8 4.1 %shard_map.109 = bf16[128,1024]{1,0:T(8,128)(2,1)S(1)} custom-call(bf16[128,2048]{1,0:T(8,128)(2,1)S(1)} %pad_maximum_fusion.5.layer_in, f32[1,2048]{1,0:T(1,128)S(1)} %bitcast.98, f32[1,2048]{1,0:T(1,128)S(1)} %bitcast.96, f32[1,1024]{1,0:T(1,128)S(1)} %copy-done.33, f32[3,128,128]{2,1,0:T(8,128)S(1)} %pad_maximum_fusion.12.turns, ...), custom_call_target="tpu_custom_call" | custom-call | flops 131072 | bytes 131072 | tf_op jit(solution)/shard_map/pallas_call | solution.py:276
  198.6 0.9 maximum_select_fusion
  199.8 0.8 maximum_bitcast_fusion
  (255 shorter events, 23.5 us)
Async XLA Ops:
  7.2 18.0 %copy-start.54 = (f32[1,2048]{1,0:T(1,128)S(1)}, f32[1,2048]{1,0:T(1,128)}, u32[]{:S(2)}) copy-start(f32[1,2048]{1,0:T(1,128)} %param.16) | copy-start | bytes 24580
  7.2 14.9 %copy-start.59 = (s32[4,32]{1,0:T(4,128)S(1)}, s32[4,32]{1,0:T(4,128)}, u32[]{:S(2)}) copy-start(s32[4,32]{1,0:T(4,128)} %param.15) | copy-start | bytes 1540
  7.2 15.0 %copy-start.69 = (s32[4,32]{1,0:T(4,128)S(1)}, s32[4,32]{1,0:T(4,128)}, u32[]{:S(2)}) copy-start(s32[4,32]{1,0:T(4,128)} %param.14) | copy-start | bytes 1540
  7.2 17.9 %copy-start.52 = (f32[1,2048]{1,0:T(1,128)S(1)}, f32[1,2048]{1,0:T(1,128)}, u32[]{:S(2)}) copy-start(f32[1,2048]{1,0:T(1,128)} %param.21) | copy-start | bytes 24580
  7.2 17.9 %copy-start.49 = (f32[1,3072]{1,0:T(1,128)S(1)}, f32[1,3072]{1,0:T(1,128)}, u32[]{:S(2)}) copy-start(f32[1,3072]{1,0:T(1,128)} %param.19) | copy-start | bytes 36868
  7.2 17.9 %copy-start.53 = (f32[1,2048]{1,0:T(1,128)S(1)}, f32[1,2048]{1,0:T(1,128)}, u32[]{:S(2)}) copy-start(f32[1,2048]{1,0:T(1,128)} %param.17) | copy-start | bytes 24580
  7.2 150.0 %all-gather.2.cloned.1.call-start = ((), (), s32[]{:S(2)}) async-start(), calls=%async_computation.4 | async-start | bytes 10567680 | tf_op jit(solution)/shard_map/all_gather | solution.py:379
  8.9 4.2 %collective-permute-start = (bf16[16,2048]{1,0:T(8,128)(2,1)S(1)}, bf16[16,2048]{1,0:T(8,128)(2,1)S(1)}, u32[]{:S(2)}, u32[]{:S(2)}) collective-permute-start(bf16[16,2048]{1,0:T(8,128)(2,1)S(1)} %broadcast_select_fusion.18), channel_id=1, source_target_pairs={{0,128},{128,0},{1,129},{129,1},{2,130},{130,2},{3,131},{131,3},{4... | collective-permute-start | bytes 196616 | tf_op jit(solution)/shard_map/ppermute | solution.py:27
  13.9 20.6 %copy-start.61 = (pred[128]{0:T(512)(128)(4,1)}, pred[128]{0:T(512)(128)(4,1)S(1)}, u32[]{:S(2)}) copy-start(pred[128]{0:T(512)(128)(4,1)S(1)} %iota_compare_fusion.15) | copy-start | bytes 388
  13.9 20.6 %copy-start.63 = (f32[128]{0:T(128)}, f32[128]{0:T(128)S(1)}, u32[]{:S(2)}) copy-start(f32[128]{0:T(128)S(1)} %multiply_power_fusion) | copy-start | bytes 1540
  13.9 20.6 %copy-start.65 = (pred[128]{0:T(512)(128)(4,1)}, pred[128]{0:T(512)(128)(4,1)S(1)}, u32[]{:S(2)}) copy-start(pred[128]{0:T(512)(128)(4,1)S(1)} %get-tuple-element.382) | copy-start | bytes 388
  13.9 20.6 %copy-start.67 = (pred[128]{0:T(512)(128)(4,1)}, pred[128]{0:T(512)(128)(4,1)S(1)}, u32[]{:S(2)}) copy-start(pred[128]{0:T(512)(128)(4,1)S(1)} %get-tuple-element.383) | copy-start | bytes 388
  15.0 17.8 %copy-start.36 = (bf16[128,1024]{1,0:T(8,128)(2,1)}, bf16[128,1024]{1,0:T(8,128)(2,1)S(1)}, u32[]{:S(2)}) copy-start(bf16[128,1024]{1,0:T(8,128)(2,1)S(1)} %slice_select_fusion) | copy-start | bytes 786436
  15.0 7.0 %collective-permute-start.1 = (bf16[1,16,1536]{2,1,0:T(8,128)(2,1)S(1)}, bf16[1,16,1536]{2,1,0:T(8,128)(2,1)S(1)}, u32[]{:S(2)}, u32[]{:S(2)}) collective-permute-start(bf16[1,16,1536]{2,1,0:T(8,128)(2,1)S(1)} %slice_bitcast_fusion.10), channel_id=1, source_target_pairs={{0,4},{1,5},{2,6},{3,7},{4,0},{5,1},{6,2},{7,3},{8,12},{9,13},{10,... | collective-permute-start | bytes 147464 | tf_op jit(solution)/shard_map/ppermute | solution.py:322
  20.4 88.7 %copy-start.34 = (s32[2]{0:T(128)}, s32[2]{0:T(128)S(1)}, u32[]{:S(2)}) copy-start(s32[2]{0:T(128)S(1)} %pad_add_fusion.place) | copy-start | bytes 28
  22.2 18.7 %copy-start.60 = (s32[128]{0:T(128)}, s32[128]{0:T(128)S(1)}, u32[]{:S(2)}) copy-start(s32[128]{0:T(128)S(1)} %reshape.853) | copy-start | bytes 1540
  25.2 7.7 %collective-permute-start.4 = (f32[9216]{0:T(1024)S(1)}, f32[9216]{0:T(1024)S(1)}, u32[]{:S(2)}, u32[]{:S(2)}) collective-permute-start(f32[9216]{0:T(1024)S(1)} %pad_maximum_fusion.20), channel_id=1, source_target_pairs={{0,128},{128,0},{1,129},{129,1},{2,130},{130,2},{3,131},{131,3},{4... | collective-permute-start | bytes 110600 | tf_op jit(solution)/shard_map/ppermute | solution.py:27
  26.7 7.8 %collective-permute-start.2 = (bf16[2,16,1536]{2,1,0:T(8,128)(2,1)S(1)}, bf16[2,16,1536]{2,1,0:T(8,128)(2,1)S(1)}, u32[]{:S(2)}, u32[]{:S(2)}) collective-permute-start(bf16[2,16,1536]{2,1,0:T(8,128)(2,1)S(1)} %maximum_bitcast_fusion.1), channel_id=1, source_target_pairs={{0,2},{1,3},{2,0},{3,1},{4,6},{5,7},{6,4},{7,5},{8,10},{9,11},{10,... | collective-permute-start | bytes 294920 | tf_op jit(solution)/shard_map/ppermute | solution.py:322
  29.7 3.1 %copy-start.46 = (bf16[128,128]{1,0:T(8,128)(2,1)}, bf16[128,128]{1,0:T(8,128)(2,1)S(1)}, u32[]{:S(2)}) copy-start(bf16[128,128]{1,0:T(8,128)(2,1)S(1)} %select_convert_fusion) | copy-start | bytes 98308
  33.5 65.9 %copy-start.28 = (f32[1,1536]{1,0:T(1,128)}, f32[1,1536]{1,0:T(1,128)S(1)}, u32[]{:S(2)}) copy-start(f32[1,1536]{1,0:T(1,128)S(1)} %broadcast_in_dim.183.bias) | copy-start | bytes 18436
  34.6 6.3 %collective-permute-start.3 = (bf16[4,16,1536]{2,1,0:T(8,128)(2,1)S(1)}, bf16[4,16,1536]{2,1,0:T(8,128)(2,1)S(1)}, u32[]{:S(2)}, u32[]{:S(2)}) collective-permute-start(bf16[4,16,1536]{2,1,0:T(8,128)(2,1)S(1)} %bitcast.115), channel_id=1, source_target_pairs={{0,1},{1,0},{2,3},{3,2},{4,5},{5,4},{6,7},{7,6},{8,9},{9,8},{10,11... | collective-permute-start | bytes 589832 | tf_op jit(solution)/shard_map/ppermute | solution.py:322
  41.0 62.8 %all-to-all-start.1 = ((bf16[8,48,1152]{2,1,0:T(8,128)(2,1)}), bf16[8,48,1152]{2,1,0:T(8,128)(2,1)}, u32[]{:S(2)}, u32[]{:S(2)}) async-start(bf16[8,48,1152]{2,1,0:T(8,128)(2,1)} %bitcast.21), calls=%async_computation.1 | async-start | bytes 1769472 | tf_op jit(solution)/shard_map/all_to_all | solution.py:50
  47.4 6.1 %collective-permute-start.8 = (bf16[128,768]{1,0:T(8,128)(2,1)S(1)}, bf16[128,768]{1,0:T(8,128)(2,1)S(1)}, u32[]{:S(2)}, u32[]{:S(2)}) collective-permute-start(bf16[128,768]{1,0:T(8,128)(2,1)S(1)} %get-tuple-element.325), channel_id=1, source_target_pairs={{0,96},{32,0},{64,32},{96,64},{1,97},{33,1},{65,33},{97,65},{2,98}... | collective-permute-start | bytes 589832 | tf_op jit(solution)/shard_map/ppermute | solution.py:296
  50.4 6.1 %collective-permute-start.6 = (bf16[128,768]{1,0:T(8,128)(2,1)S(1)}, bf16[128,768]{1,0:T(8,128)(2,1)S(1)}, u32[]{:S(2)}, u32[]{:S(2)}) collective-permute-start(bf16[128,768]{1,0:T(8,128)(2,1)S(1)} %get-tuple-element.325), channel_id=1, source_target_pairs={{0,32},{32,64},{64,96},{96,0},{1,33},{33,65},{65,97},{97,1},{2,34}... | collective-permute-start | bytes 589832 | tf_op jit(solution)/shard_map/ppermute | solution.py:296
  50.4 6.1 %collective-permute-start.7 = (bf16[128,768]{1,0:T(8,128)(2,1)S(1)}, bf16[128,768]{1,0:T(8,128)(2,1)S(1)}, u32[]{:S(2)}, u32[]{:S(2)}) collective-permute-start(bf16[128,768]{1,0:T(8,128)(2,1)S(1)} %get-tuple-element.326), channel_id=1, source_target_pairs={{0,24},{8,0},{16,8},{24,16},{1,25},{9,1},{17,9},{25,17},{2,26},{10... | collective-permute-start | bytes 589832 | tf_op jit(solution)/shard_map/ppermute | solution.py:296
  53.4 6.1 %collective-permute-start.5 = (bf16[128,768]{1,0:T(8,128)(2,1)S(1)}, bf16[128,768]{1,0:T(8,128)(2,1)S(1)}, u32[]{:S(2)}, u32[]{:S(2)}) collective-permute-start(bf16[128,768]{1,0:T(8,128)(2,1)S(1)} %get-tuple-element.326), channel_id=1, source_target_pairs={{0,8},{8,16},{16,24},{24,0},{1,9},{9,17},{17,25},{25,1},{2,10},{10... | collective-permute-start | bytes 589832 | tf_op jit(solution)/shard_map/ppermute | solution.py:296
  59.6 6.1 %collective-permute-start.9 = (bf16[128,768]{1,0:T(8,128)(2,1)S(1)}, bf16[128,768]{1,0:T(8,128)(2,1)S(1)}, u32[]{:S(2)}, u32[]{:S(2)}) collective-permute-start(bf16[128,768]{1,0:T(8,128)(2,1)S(1)} %collective-permute-done.5), channel_id=1, source_target_pairs={{0,8},{8,16},{16,24},{24,0},{1,9},{9,17},{17,25},{25,1},{2,10},{10... | collective-permute-start | bytes 589832 | tf_op jit(solution)/shard_map/ppermute | solution.py:296
  59.6 6.2 %collective-permute-start.10 = (bf16[128,768]{1,0:T(8,128)(2,1)S(1)}, bf16[128,768]{1,0:T(8,128)(2,1)S(1)}, u32[]{:S(2)}, u32[]{:S(2)}) collective-permute-start(bf16[128,768]{1,0:T(8,128)(2,1)S(1)} %collective-permute-done.6), channel_id=1, source_target_pairs={{0,32},{32,64},{64,96},{96,0},{1,33},{33,65},{65,97},{97,1},{2,34}... | collective-permute-start | bytes 589832 | tf_op jit(solution)/shard_map/ppermute | solution.py:296
  65.8 33.6 %copy-start.8 = (bf16[4,32,2048]{2,1,0:T(8,128)(2,1)S(1)}, bf16[4,32,2048]{2,1,0:T(8,128)(2,1)}, u32[]{:S(2)}) copy-start(bf16[4,32,2048]{2,1,0:T(8,128)(2,1)} %param.13) | copy-start | bytes 1572868
  65.8 24.4 %collective-permute-start.13 = (bf16[512,768]{1,0:T(8,128)(2,1)S(1)}, bf16[512,768]{1,0:T(8,128)(2,1)S(1)}, u32[]{:S(2)}, u32[]{:S(2)}) collective-permute-start(bf16[512,768]{1,0:T(8,128)(2,1)S(1)} %pad_maximum_fusion.1.rest_0_), channel_id=1, source_target_pairs={{0,96},{32,0},{64,32},{96,64},{1,97},{33,1},{65,33},{97,65},{2,98}... | collective-permute-start | bytes 2359304 | tf_op jit(solution)/shard_map/ppermute | solution.py:296
  68.6 22.1 %collective-permute-start.11 = (bf16[512,768]{1,0:T(8,128)(2,1)S(1)}, bf16[512,768]{1,0:T(8,128)(2,1)S(1)}, u32[]{:S(2)}, u32[]{:S(2)}) collective-permute-start(bf16[512,768]{1,0:T(8,128)(2,1)S(1)} %pad_maximum_fusion.1.rest_0_), channel_id=1, source_target_pairs={{0,32},{32,64},{64,96},{96,0},{1,33},{33,65},{65,97},{97,1},{2,34}... | collective-permute-start | bytes 2359304 | tf_op jit(solution)/shard_map/ppermute | solution.py:296
  68.6 22.1 %collective-permute-start.14 = (bf16[512,768]{1,0:T(8,128)(2,1)S(1)}, bf16[512,768]{1,0:T(8,128)(2,1)S(1)}, u32[]{:S(2)}, u32[]{:S(2)}) collective-permute-start(bf16[512,768]{1,0:T(8,128)(2,1)S(1)} %pad_maximum_fusion.2.rest_3_.rest_5_), channel_id=1, source_target_pairs={{0,24},{8,0},{16,8},{24,16},{1,25},{9,1},{17,9},{25,17},{2,26},{10... | collective-permute-start | bytes 2359304 | tf_op jit(solution)/shard_map/ppermute | solution.py:296
  70.0 20.8 %collective-permute-start.12 = (bf16[512,768]{1,0:T(8,128)(2,1)S(1)}, bf16[512,768]{1,0:T(8,128)(2,1)S(1)}, u32[]{:S(2)}, u32[]{:S(2)}) collective-permute-start(bf16[512,768]{1,0:T(8,128)(2,1)S(1)} %pad_maximum_fusion.2.rest_3_.rest_5_), channel_id=1, source_target_pairs={{0,8},{8,16},{16,24},{24,0},{1,9},{9,17},{17,25},{25,1},{2,10},{10... | collective-permute-start | bytes 2359304 | tf_op jit(solution)/shard_map/ppermute | solution.py:296
  90.2 9.1 %copy-start = (bf16[512,768]{1,0:T(8,128)(2,1)}, bf16[512,768]{1,0:T(8,128)(2,1)S(1)}, u32[]{:S(2)}) copy-start(bf16[512,768]{1,0:T(8,128)(2,1)S(1)} %collective-permute-done.13.rest_1_) | copy-start | bytes 2359300
  90.7 8.6 %copy-start.2 = (bf16[512,768]{1,0:T(8,128)(2,1)}, bf16[512,768]{1,0:T(8,128)(2,1)S(1)}, u32[]{:S(2)}) copy-start(bf16[512,768]{1,0:T(8,128)(2,1)S(1)} %collective-permute-done.11.rest_2_) | copy-start | bytes 2359300
  90.7 8.6 %copy-start.4 = (bf16[512,768]{1,0:T(8,128)(2,1)}, bf16[512,768]{1,0:T(8,128)(2,1)S(1)}, u32[]{:S(2)}) copy-start(bf16[512,768]{1,0:T(8,128)(2,1)S(1)} %collective-permute-done.14.rest_4_.rest_6_) | copy-start | bytes 2359300
  90.8 8.6 %copy-start.6 = (bf16[512,768]{1,0:T(8,128)(2,1)}, bf16[512,768]{1,0:T(8,128)(2,1)S(1)}, u32[]{:S(2)}) copy-start(bf16[512,768]{1,0:T(8,128)(2,1)S(1)} %collective-permute-done.12.rest_5_.rest_7_) | copy-start | bytes 2359300
  94.0 15.0 %collective-permute-start.17 = (bf16[256,768]{1,0:T(8,128)(2,1)}, bf16[256,768]{1,0:T(8,128)(2,1)S(1)}, u32[]{:S(2)}, u32[]{:S(2)}) collective-permute-start(bf16[256,768]{1,0:T(8,128)(2,1)} %slice.258), channel_id=1, source_target_pairs={{0,8},{8,16},{16,24},{24,0},{1,9},{9,17},{17,25},{25,1},{2,10},{10... | collective-permute-start | bytes 1179656 | tf_op jit(solution)/shard_map/ppermute | solution.py:296
  96.0 13.1 %collective-permute-start.18 = (bf16[256,768]{1,0:T(8,128)(2,1)}, bf16[256,768]{1,0:T(8,128)(2,1)S(1)}, u32[]{:S(2)}, u32[]{:S(2)}) collective-permute-start(bf16[256,768]{1,0:T(8,128)(2,1)} %slice.259), channel_id=1, source_target_pairs={{0,24},{8,0},{16,8},{24,16},{1,25},{9,1},{17,9},{25,17},{2,26},{10... | collective-permute-start | bytes 1179656 | tf_op jit(solution)/shard_map/ppermute | solution.py:296
  96.7 12.4 %collective-permute-start.15 = (bf16[256,768]{1,0:T(8,128)(2,1)}, bf16[256,768]{1,0:T(8,128)(2,1)S(1)}, u32[]{:S(2)}, u32[]{:S(2)}) collective-permute-start(bf16[256,768]{1,0:T(8,128)(2,1)} %slice.256), channel_id=1, source_target_pairs={{0,32},{32,64},{64,96},{96,0},{1,33},{33,65},{65,97},{97,1},{2,34}... | collective-permute-start | bytes 1179656 | tf_op jit(solution)/shard_map/ppermute | solution.py:296
  96.7 12.4 %collective-permute-start.16 = (bf16[256,768]{1,0:T(8,128)(2,1)}, bf16[256,768]{1,0:T(8,128)(2,1)S(1)}, u32[]{:S(2)}, u32[]{:S(2)}) collective-permute-start(bf16[256,768]{1,0:T(8,128)(2,1)} %slice.257), channel_id=1, source_target_pairs={{0,96},{32,0},{64,32},{96,64},{1,97},{33,1},{65,33},{97,65},{2,98}... | collective-permute-start | bytes 1179656 | tf_op jit(solution)/shard_map/ppermute | solution.py:296
  103.8 11.3 %copy-start.45 = (bf16[384,128]{1,0:T(8,128)(2,1)S(1)}, bf16[384,128]{1,0:T(8,128)(2,1)}, u32[]{:S(2)}) copy-start(bf16[384,128]{1,0:T(8,128)(2,1)} %fusion.38) | copy-start | bytes 294916
  109.0 7.9 %copy-start.10 = (bf16[256,768]{1,0:T(8,128)(2,1)}, bf16[256,768]{1,0:T(8,128)(2,1)S(1)}, u32[]{:S(2)}) copy-start(bf16[256,768]{1,0:T(8,128)(2,1)S(1)} %collective-permute-done.17.rest_2_.rest_8_) | copy-start | bytes 1179652
  109.0 7.9 %copy-start.12 = (bf16[256,768]{1,0:T(8,128)(2,1)}, bf16[256,768]{1,0:T(8,128)(2,1)S(1)}, u32[]{:S(2)}) copy-start(bf16[256,768]{1,0:T(8,128)(2,1)S(1)} %collective-permute-done.18.rest_3_.rest_9_) | copy-start | bytes 1179652
  109.1 7.9 %copy-start.14 = (bf16[256,768]{1,0:T(8,128)(2,1)}, bf16[256,768]{1,0:T(8,128)(2,1)S(1)}, u32[]{:S(2)}) copy-start(bf16[256,768]{1,0:T(8,128)(2,1)S(1)} %collective-permute-done.15.rest_0_.rest_3_) | copy-start | bytes 1179652
  109.1 7.9 %copy-start.16 = (bf16[256,768]{1,0:T(8,128)(2,1)}, bf16[256,768]{1,0:T(8,128)(2,1)S(1)}, u32[]{:S(2)}) copy-start(bf16[256,768]{1,0:T(8,128)(2,1)S(1)} %collective-permute-done.16.rest_1_.rest_4_) | copy-start | bytes 1179652
  117.0 25.1 %all-to-all-start.2 = ((bf16[8,48,512]{2,1,0:T(8,128)(2,1)}), bf16[8,48,512]{2,1,0:T(8,128)(2,1)}, u32[]{:S(2)}, u32[]{:S(2)}) async-start(bf16[8,48,512]{2,1,0:T(8,128)(2,1)} %bitcast.112), calls=%async_computation.2 | async-start | bytes 786432 | tf_op jit(solution)/shard_map/all_to_all | solution.py:50
  130.7 9.7 %collective-permute-start.19 = (bf16[128,512]{1,0:T(8,128)(2,1)}, bf16[128,512]{1,0:T(8,128)(2,1)S(1)}, u32[]{:S(2)}, u32[]{:S(2)}) collective-permute-start(bf16[128,512]{1,0:T(8,128)(2,1)} %shard_map.105), channel_id=1, source_target_pairs={{0,128},{128,0},{1,129},{129,1},{2,130},{130,2},{3,131},{131,3},{4... | collective-permute-start | bytes 393224 | tf_op jit(solution)/shard_map/ppermute | solution.py:27
  145.6 32.6 %all-to-all-start.3 = ((bf16[16,32,1664]{2,1,0:T(8,128)(2,1)}), bf16[16,32,1664]{2,1,0:T(8,128)(2,1)S(1)}, u32[]{:S(2)}, u32[]{:S(2)}) async-start(bf16[16,32,1664]{2,1,0:T(8,128)(2,1)} %bitcast.110), calls=%async_computation.3 | async-start | bytes 3407872 | tf_op jit(solution)/shard_map/all_to_all | solution.py:50
  157.2 3.9 %copy-start.47 = (bf16[128,512]{1,0:T(8,128)(2,1)S(1)}, bf16[128,512]{1,0:T(8,128)(2,1)}, u32[]{:S(2)}) copy-start(bf16[128,512]{1,0:T(8,128)(2,1)} %get-tuple-element.335) | copy-start | bytes 393220
  157.2 3.9 %copy-start.48 = (bf16[128,512]{1,0:T(8,128)(2,1)S(1)}, bf16[128,512]{1,0:T(8,128)(2,1)}, u32[]{:S(2)}) copy-start(bf16[128,512]{1,0:T(8,128)(2,1)} %get-tuple-element.336) | copy-start | bytes 393220
  161.1 3.0 %copy-start.56 = (f32[512]{0:T(512)S(1)}, f32[512]{0:T(512)}, u32[]{:S(2)}) copy-start(f32[512]{0:T(512)} %get-tuple-element.349) | copy-start | bytes 6148
  161.1 3.0 %copy-start.57 = (f32[512]{0:T(512)S(1)}, f32[512]{0:T(512)}, u32[]{:S(2)}) copy-start(f32[512]{0:T(512)} %get-tuple-element.350) | copy-start | bytes 6148
  161.1 3.0 %copy-start.58 = (f32[512]{0:T(512)S(1)}, f32[512]{0:T(512)}, u32[]{:S(2)}) copy-start(f32[512]{0:T(512)} %get-tuple-element.351) | copy-start | bytes 6148
  161.1 5.0 %copy-start.29 = (f32[1,1536]{1,0:T(1,128)S(1)}, f32[1,1536]{1,0:T(1,128)}, u32[]{:S(2)}) copy-start(f32[1,1536]{1,0:T(1,128)} %copy-done.28) | copy-start | bytes 18436
  163.3 6.9 %collective-permute-start.20 = (bf16[128,1024]{1,0:T(8,128)(2,1)}, bf16[128,1024]{1,0:T(8,128)(2,1)}, u32[]{:S(2)}, u32[]{:S(2)}) collective-permute-start(bf16[128,1024]{1,0:T(8,128)(2,1)} %fusion.28), channel_id=1, source_target_pairs={{0,128},{128,0},{1,129},{129,1},{2,130},{130,2},{3,131},{131,3},{4... | collective-permute-start | bytes 786440 | tf_op jit(solution)/shard_map/ppermute | solution.py:27
  179.9 4.7 %copy-start.43 = (bf16[2048,512]{1,0:T(8,128)(2,1)S(1)}, bf16[2048,512]{1,0:T(8,128)(2,1)}, u32[]{:S(2)}) copy-start(bf16[2048,512]{1,0:T(8,128)(2,1)} %get-tuple-element.313) | copy-start | bytes 6291460
  181.0 2.1 collective-permute-start.21
  182.5 2.5 %collective-permute-start.23 = (bf16[128,1536]{1,0:T(8,128)(2,1)S(1)}, bf16[128,1536]{1,0:T(8,128)(2,1)S(1)}, u32[]{:S(2)}, u32[]{:S(2)}) collective-permute-start(bf16[128,1536]{1,0:T(8,128)(2,1)S(1)} %slice.345), channel_id=1, source_target_pairs={{0,128},{128,0},{1,129},{129,1},{2,130},{130,2},{3,131},{131,3},{4... | collective-permute-start | bytes 1179656 | tf_op jit(solution)/shard_map/ppermute | solution.py:27
  188.0 2.0 collective-permute-start.24
  189.4 9.2 %collective-permute-start.22 = (bf16[128,1024]{1,0:T(8,128)(2,1)S(1)}, bf16[128,1024]{1,0:T(8,128)(2,1)S(1)}, u32[]{:S(2)}, u32[]{:S(2)}) collective-permute-start(bf16[128,1024]{1,0:T(8,128)(2,1)S(1)} %fusion.30), channel_id=1, source_target_pairs={{0,128},{128,0},{1,129},{129,1},{2,130},{130,2},{3,131},{131,3},{4... | collective-permute-start | bytes 786440 | tf_op jit(solution)/shard_map/ppermute | solution.py:27
  193.8 4.8 %copy-start.38 = (bf16[128,1024]{1,0:T(8,128)(2,1)S(1)}, bf16[128,1024]{1,0:T(8,128)(2,1)}, u32[]{:S(2)}) copy-start(bf16[128,1024]{1,0:T(8,128)(2,1)} %copy-done.37) | copy-start | bytes 786436
  193.8 4.8 %copy-start.40 = (bf16[128,1024]{1,0:T(8,128)(2,1)S(1)}, bf16[128,1024]{1,0:T(8,128)(2,1)}, u32[]{:S(2)}) copy-start(bf16[128,1024]{1,0:T(8,128)(2,1)} %copy-done.39) | copy-start | bytes 786436
  198.0 1.7 collective-permute-start.25
  (36 other events, 57.7 us)
Sparse Core Ops, SparseCore 0:
  14.0 143.1 all-gather.1
where the time goes:
time: 209 us; the launch traced here: 208 us
  starting transfers between devices  58.1 us (28%)
  waiting for transfers between devices  49.1 us (23%)
  local copies, waits for them, and re-layouts  27.7 us (13%)
  other arithmetic  25.6 us (12%)
  Pallas kernels  19.2 us (9%)
  between operations  18.5 us (9%)
  matrix products  9.03 us (4%)
    ppermute x14, waiting for transfers between devices, shifted(): lax.ppermute(value, axis, [(one, (one + by) % size) for one in range(size)])  31.6 us
    all_to_all x3, starting transfers between devices, across(): lax.all_to_all(filled.reshape(-1, cap, cols), axes, split_axis=0, concat_...  18.4 us
    ppermute x9, starting transfers between devices, swap(): return lax.ppermute(value, 'pipe', [(0, 1), (1, 0)])  16.1 us
    ppermute x14, starting transfers between devices, shifted(): lax.ppermute(value, axis, [(one, (one + by) % size) for one in range(size)])  15.9 us
    select_n x18, other arithmetic, pick(): return jnp.where(first_core, a, b)  10 us
    pallas_call x4, Pallas kernels, call(): pl.pallas_call(kernel, out_shape=out_shape, in_specs=in_specs, out_specs=...  9.63 us
    pallas_call x2, Pallas kernels, project_whole(): pl.pallas_call(functools.partial(whole_kernel, with_context), grid=(width...  9.59 us
    dot_general x11, matrix products, mm(): return jnp.dot(a, b, preferred_element_type=F32)  9.03 us
  transfers between devices with their start and end apart: 30, of which 12 were waited for; matrix products, arithmetic and copies ran while one was open for 22% of the time, Pallas kernels for 9%

commit v1 on v0

--- a/solution.py
+++ b/solution.py
@@ -296,14 +296,14 @@
     return lax.ppermute(value, axis, [(one, (one + by) % size) for one in range(size)])
 
 
-def rings(blocks, axes, halves):
+def rings(blocks, axes, halves, later=()):
     size = lax.axis_size(axes[0])
     found = [{0: [block]} for block in blocks]
     ups = downs = list(blocks)
     for step in range(1, size // 2):
         ups = [shifted(up, axis, 1) for up, axis in zip(ups, axes)]
         downs = [shifted(down, axis, -1) for down, axis in zip(downs, axes)]
-        ups, downs = lax.optimization_barrier((ups, downs))
+        ups, downs, later = lax.optimization_barrier((ups, downs, later))
         for one, up, down in zip(found, ups, downs):
             one[size - step], one[step] = [up], [down]
     for one, up, down, axis in zip(found, ups, downs, axes):
@@ -312,10 +312,10 @@
             one[size // 2] = [shifted(up[:rows], axis, 1), shifted(down[rows:], axis, -1)]
         else:
             one[size // 2] = [shifted(up, axis, 1)]
-    return [[one[k] for k in range(size)] for one in found]
-
-
-def column_of(shard, later):
+    return [[one[k] for k in range(size)] for one in found], later
+
+
+def column_of(shard):
     size, index = lax.axis_size("z"), lax.axis_index("z")
     block, step = shard[None], size // 2
     while step:
@@ -323,21 +323,19 @@
         upper = (index // step) % 2 == 1
         both = [jnp.where(upper, got, block), jnp.where(upper, block, got)]
         block = jnp.stack(both, axis=1).reshape(-1, *shard.shape)
-        if step == size // 2:
-            block, later = lax.optimization_barrier((block, later))
         step //= 2
-    return block.reshape(-1, shard.shape[1]), later
-
-
-def pieces_of(ring):
+    return block.reshape(-1, shard.shape[1])
+
+
+def pieces_of(ring, later):
     half = ring.shape[1] // 2
-    pair = rings([ring[:, :half], ring[:, half:]], ["y", "x"], False)
+    pair, later = rings([ring[:, :half], ring[:, half:]], ["y", "x"], False, later)
     pair = [jnp.concatenate([one[0] for one in each], axis=0) for each in pair]
     pair = lax.optimization_barrier(pair)
     order = []
-    for each in rings(pair, ["x", "y"], True):
+    for each in rings(pair, ["x", "y"], True)[0]:
         order += [*each[0], *each[1], *each[3], *each[2]]
-    return order
+    return order, later
 
 
 def shards(
@@ -377,8 +375,8 @@
     shard0, shard1 = pick(kept, got), pick(got, kept)
     bulk = jnp.concatenate([shard1, shard0[:, 3 * part :]], axis=1)
     gathered = lax.all_gather(bulk, DP, axis=0, tiled=True)
-    column, (seg_ids, cache_row, ln_gain) = column_of(
-        shard0[:, : 3 * part], (seg_ids, cache_row, ln_gain)
+    pieces, (tokens, seg_ids, cache_row, ln_gain) = pieces_of(
+        column_of(shard0[:, : 3 * part]), (tokens, seg_ids, cache_row, ln_gain)
     )
 
     vectors = jnp.concatenate([ln_gain[0], ln_bias[0], qkv_bias[0], out_bias[0]])
@@ -436,11 +434,7 @@
     filled = flagged(mm(send_z, payload).astype(BF), out_z, flag_at)
     place = jnp.stack([lax.axis_index("x"), lax.axis_index("y")]).astype(jnp.int32)
     turns = turns_of(positions.astype(F32))
-    filled, column, turns, allowed, send_z, place, rows0 = lax.optimization_barrier(
-        (filled, column, turns, allowed, send_z, place, rows0)
-    )
     middle = across(filled, "z", CAP_Z)
-    pieces = pieces_of(column)
     slot_p, out_p = slots_of(
         middle[:, half_width + 2].astype(jnp.int32),
         middle[:, half_width] > 0,
@@ -458,7 +452,9 @@
     leg = mm(send_p, leg).astype(BF)
     wide = half_width + part
     arrived = across(leg, PLANE, CAP_P)
-    gathered, leg_mark = lax.optimization_barrier((gathered, leg[0, half_width]))
+    gathered, leg_mark, rows1, out_bias0, out_bias1 = lax.optimization_barrier(
+        (gathered, leg[0, half_width], rows1, out_bias0, out_bias1)
+    )
 
     def finish(half, context, out, out_b):
         done = jnp.concatenate([mm(context, one) for one in out], axis=1)
@@ -471,8 +467,8 @@
 
     out0, out1 = out_of(4 * part), out_of(3 * part)
     hidden0_half, hidden0 = finish(half_tokens, joined(context0), out0, out_bias0)
+    arrived, hidden0_half = lax.optimization_barrier((arrived, hidden0_half))
     context1 = project_whole(hidden0, rows1, turns, allowed, gathered)
-    arrived, context1 = lax.optimization_barrier((arrived, context1))
     _, hidden1 = finish(hidden0_half, joined(context1), out1, out_bias1)
 
     def places(came_meta):

time: 209 us -> 207 us (level)
  waiting for transfers between devices: 49.1 us -> 62.9 us
  local copies, waits for them, and re-layouts: 27.7 us -> 20.2 us
  other arithmetic: 25.6 us -> 20.4 us
    all_to_all x3, waiting for transfers between devices: 0.01 us -> 6.71 us  [across(): lax.all_to_all(filled.reshape(-1, cap, cols), axes, split_axis=0, concat_...]
    ppermute x3, waiting for transfers between devices: 8.84 us -> 13.3 us  [column_of(): got = lax.ppermute(block, 'z', [(one, one ^ step) for one in range(size)])]
    select_n x18 -> x16, other arithmetic: 10 us -> 5.95 us  [pick(): return jnp.where(first_core, a, b)]
    all_gather x1, waiting for transfers between devices: 6.92 us -> 9.84 us  [shards(): gathered = lax.all_gather(bulk, DP, axis=0, tiled=True)]
    unnamed x140 -> x124, local copies, waits for them, and re-layouts: 8.61 us -> 5.91 us
    all_to_all x3, starting transfers between devices: 18.4 us -> 16.3 us  [across(): lax.all_to_all(filled.reshape(-1, cap, cols), axes, split_axis=0, concat_...]
  transfers between devices with their start and end apart: 30 -> 30, of which waited for: 12 -> 13; matrix products, arithmetic and copies ran while one was open for 22% -> 19% of each run, Pallas kernels for 9% -> 9%
where the time goes in v1:
time: 207 us; the launch traced here: 206 us
  waiting for transfers between devices  62.9 us (30%)
  starting transfers between devices  56.8 us (27%)
  other arithmetic  20.4 us (10%)
  local copies, waits for them, and re-layouts  20.2 us (10%)
  Pallas kernels  19.2 us (9%)
  between operations  18.4 us (9%)
  matrix products  7.7 us (4%)
    ppermute x14, waiting for transfers between devices, shifted(): lax.ppermute(value, axis, [(one, (one + by) % size) for one in range(size)])  31.9 us
    ppermute x9, starting transfers between devices, swap(): return lax.ppermute(value, 'pipe', [(0, 1), (1, 0)])  17 us
    ppermute x14, starting transfers between devices, shifted(): lax.ppermute(value, axis, [(one, (one + by) % size) for one in range(size)])  16.8 us
    all_to_all x3, starting transfers between devices, across(): lax.all_to_all(filled.reshape(-1, cap, cols), axes, split_axis=0, concat_...  16.3 us
    ppermute x3, waiting for transfers between devices, column_of(): got = lax.ppermute(block, 'z', [(one, one ^ step) for one in range(size)])  13.3 us
    all_gather x1, waiting for transfers between devices, shards(): gathered = lax.all_gather(bulk, DP, axis=0, tiled=True)  9.84 us
    pallas_call x4, Pallas kernels, call(): pl.pallas_call(kernel, out_shape=out_shape, in_specs=in_specs, out_specs=...  9.65 us
    pallas_call x2, Pallas kernels, project_whole(): pl.pallas_call(functools.partial(whole_kernel, with_context), grid=(width...  9.59 us
  transfers between devices with their start and end apart: 30, of which 13 were waited for; matrix products, arithmetic and copies ran while one was open for 19% of the time, Pallas kernels for 9%

profile of v1, /device:TPU:1, one launch (start us, length us, event | category | flops | bytes accessed | tf_op | source)
XLA Modules:
  0.0 205.8 jit_solution(13294537350618680254)
XLA Ops:
  7.2 0.8 fusion.80
  8.0 0.8 fusion.77
  8.8 3.3 %collective-permute-start = (bf16[16,2048]{1,0:T(8,128)(2,1)S(1)}, bf16[16,2048]{1,0:T(8,128)(2,1)S(1)}, u32[]{:S(2)}, u32[]{:S(2)}) collective-permute-start(bf16[16,2048]{1,0:T(8,128)(2,1)S(1)} %broadcast_select_fusion.18), channel_id=1, source_target_pairs={{0,128},{128,0},{1,129},{129,1},{2,130},{130,2},{3,131},{131,3},{4... | collective-permute-start | bytes 196616 | tf_op jit(solution)/shard_map/ppermute | solution.py:27
  12.1 0.9 collective-permute-done
  13.1 0.6 pad_maximum_fusion.19
  13.8 5.3 %collective-permute-start.1 = (bf16[1,16,1536]{2,1,0:T(8,128)(2,1)S(1)}, bf16[1,16,1536]{2,1,0:T(8,128)(2,1)S(1)}, u32[]{:S(2)}, u32[]{:S(2)}) collective-permute-start(bf16[1,16,1536]{2,1,0:T(8,128)(2,1)S(1)} %slice_bitcast_fusion.10), channel_id=1, source_target_pairs={{0,4},{1,5},{2,6},{3,7},{4,0},{5,1},{6,2},{7,3},{8,12},{9,13},{10,... | collective-permute-start | bytes 147464 | tf_op jit(solution)/shard_map/ppermute | solution.py:322
  19.1 1.8 collective-permute-done.1
  20.9 1.2 collective-permute-start.2
  22.1 5.8 %collective-permute-done.2 = bf16[2,16,1536]{2,1,0:T(8,128)(2,1)S(1)} collective-permute-done((bf16[2,16,1536]{2,1,0:T(8,128)(2,1)S(1)}, bf16[2,16,1536]{2,1,0:T(8,128)(2,1)S(1)}, u32[]{:S(2)}, u32[]{:S(2)}) %collective-permute-start.2) | collective-permute-done | bytes 98336 | tf_op jit(solution)/shard_map/ppermute | solution.py:322
  28.2 5.8 %collective-permute-done.3 = bf16[4,16,1536]{2,1,0:T(8,128)(2,1)S(1)} collective-permute-done((bf16[4,16,1536]{2,1,0:T(8,128)(2,1)S(1)}, bf16[4,16,1536]{2,1,0:T(8,128)(2,1)S(1)}, u32[]{:S(2)}, u32[]{:S(2)}) %collective-permute-start.3) | collective-permute-done | bytes 196640 | tf_op jit(solution)/shard_map/ppermute | solution.py:322
  34.1 2.6 %collective-permute-start.7 = (bf16[128,768]{1,0:T(8,128)(2,1)S(1)}, bf16[128,768]{1,0:T(8,128)(2,1)S(1)}, u32[]{:S(2)}, u32[]{:S(2)}) collective-permute-start(bf16[128,768]{1,0:T(8,128)(2,1)S(1)} %get-tuple-element.317), channel_id=1, source_target_pairs={{0,96},{32,0},{64,32},{96,64},{1,97},{33,1},{65,33},{97,65},{2,98}... | collective-permute-start | bytes 589832 | tf_op jit(solution)/shard_map/ppermute | solution.py:296
  36.7 2.7 %collective-permute-start.6 = (bf16[128,768]{1,0:T(8,128)(2,1)S(1)}, bf16[128,768]{1,0:T(8,128)(2,1)S(1)}, u32[]{:S(2)}, u32[]{:S(2)}) collective-permute-start(bf16[128,768]{1,0:T(8,128)(2,1)S(1)} %get-tuple-element.318), channel_id=1, source_target_pairs={{0,24},{8,0},{16,8},{24,16},{1,25},{9,1},{17,9},{25,17},{2,26},{10... | collective-permute-start | bytes 589832 | tf_op jit(solution)/shard_map/ppermute | solution.py:296
  39.4 0.7 pad_add_fusion.place
  40.1 2.4 %collective-permute-done.5 = bf16[128,768]{1,0:T(8,128)(2,1)S(1)} collective-permute-done((bf16[128,768]{1,0:T(8,128)(2,1)S(1)}, bf16[128,768]{1,0:T(8,128)(2,1)S(1)}, u32[]{:S(2)}, u32[]{:S(2)}) %collective-permute-start.5) | collective-permute-done | bytes 196640 | tf_op jit(solution)/shard_map/ppermute | solution.py:296
  42.5 3.2 %collective-permute-done.4 = bf16[128,768]{1,0:T(8,128)(2,1)S(1)} collective-permute-done((bf16[128,768]{1,0:T(8,128)(2,1)S(1)}, bf16[128,768]{1,0:T(8,128)(2,1)S(1)}, u32[]{:S(2)}, u32[]{:S(2)}) %collective-permute-start.4) | collective-permute-done | bytes 196640 | tf_op jit(solution)/shard_map/ppermute | solution.py:296
  47.2 0.7 and_reduce_fusion
  48.6 3.2 %collective-permute-start.8 = (f32[9216]{0:T(1024)S(1)}, f32[9216]{0:T(1024)S(1)}, u32[]{:S(2)}, u32[]{:S(2)}) collective-permute-start(f32[9216]{0:T(1024)S(1)} %pad_maximum_fusion.20), channel_id=1, source_target_pairs={{0,128},{128,0},{1,129},{129,1},{2,130},{130,2},{3,131},{131,3},{4... | collective-permute-start | bytes 110600 | tf_op jit(solution)/shard_map/ppermute | solution.py:27
  53.2 0.7 copy-done.28
  53.9 1.4 fusion.12
  55.3 5.1 %all-to-all-start.1 = ((bf16[8,48,1152]{2,1,0:T(8,128)(2,1)}), bf16[8,48,1152]{2,1,0:T(8,128)(2,1)}, u32[]{:S(2)}, u32[]{:S(2)}) async-start(bf16[8,48,1152]{2,1,0:T(8,128)(2,1)} %bitcast.21), calls=%async_computation.1 | async-start | bytes 1769472 | tf_op jit(solution)/shard_map/all_to_all | solution.py:50
  60.9 2.7 %collective-permute-start.13 = (bf16[512,768]{1,0:T(8,128)(2,1)S(1)}, bf16[512,768]{1,0:T(8,128)(2,1)S(1)}, u32[]{:S(2)}, u32[]{:S(2)}) collective-permute-start(bf16[512,768]{1,0:T(8,128)(2,1)S(1)} %pad_maximum_fusion.1.rest_0_), channel_id=1, source_target_pairs={{0,96},{32,0},{64,32},{96,64},{1,97},{33,1},{65,33},{97,65},{2,98}... | collective-permute-start | bytes 2359304 | tf_op jit(solution)/shard_map/ppermute | solution.py:296
  63.7 2.7 %collective-permute-start.14 = (bf16[512,768]{1,0:T(8,128)(2,1)S(1)}, bf16[512,768]{1,0:T(8,128)(2,1)S(1)}, u32[]{:S(2)}, u32[]{:S(2)}) collective-permute-start(bf16[512,768]{1,0:T(8,128)(2,1)S(1)} %pad_maximum_fusion.2.rest_3_.rest_5_), channel_id=1, source_target_pairs={{0,24},{8,0},{16,8},{24,16},{1,25},{9,1},{17,9},{25,17},{2,26},{10... | collective-permute-start | bytes 2359304 | tf_op jit(solution)/shard_map/ppermute | solution.py:296
  66.4 0.7 and_convert_fusion
  67.2 19.8 %collective-permute-done.13.rest_1_ = bf16[512,768]{1,0:T(8,128)(2,1)S(1)} collective-permute-done((bf16[512,768]{1,0:T(8,128)(2,1)S(1)}, bf16[512,768]{1,0:T(8,128)(2,1)S(1)}, u32[]{:S(2)}, u32[]{:S(2)}) %collective-permute-start.13) | collective-permute-done | bytes 786464 | tf_op jit(solution)/shard_map/ppermute | solution.py:296
  87.0 3.2 %collective-permute-done.11.rest_2_ = bf16[512,768]{1,0:T(8,128)(2,1)S(1)} collective-permute-done((bf16[512,768]{1,0:T(8,128)(2,1)S(1)}, bf16[512,768]{1,0:T(8,128)(2,1)S(1)}, u32[]{:S(2)}, u32[]{:S(2)}) %collective-permute-start.11) | collective-permute-done | bytes 786464 | tf_op jit(solution)/shard_map/ppermute | solution.py:296
  90.4 2.9 %collective-permute-start.18 = (bf16[256,768]{1,0:T(8,128)(2,1)S(1)}, bf16[256,768]{1,0:T(8,128)(2,1)S(1)}, u32[]{:S(2)}, u32[]{:S(2)}) collective-permute-start(bf16[256,768]{1,0:T(8,128)(2,1)S(1)} %slice.259), channel_id=1, source_target_pairs={{0,24},{8,0},{16,8},{24,16},{1,25},{9,1},{17,9},{25,17},{2,26},{10... | collective-permute-start | bytes 1179656 | tf_op jit(solution)/shard_map/ppermute | solution.py:296
  93.4 2.7 %collective-permute-start.16 = (bf16[256,768]{1,0:T(8,128)(2,1)S(1)}, bf16[256,768]{1,0:T(8,128)(2,1)S(1)}, u32[]{:S(2)}, u32[]{:S(2)}) collective-permute-start(bf16[256,768]{1,0:T(8,128)(2,1)S(1)} %slice.257), channel_id=1, source_target_pairs={{0,96},{32,0},{64,32},{96,64},{1,97},{33,1},{65,33},{97,65},{2,98}... | collective-permute-start | bytes 1179656 | tf_op jit(solution)/shard_map/ppermute | solution.py:296
  97.3 2.7 %shard_map.104 = (f32[128,1536]{1,0:T(8,128)S(1)}, bf16[16,128,128]{2,1,0:T(8,128)(2,1)S(1)}) custom-call(s32[2]{0:T(128)S(1)} %copy-done.24, bf16[128,2048]{1,0:T(8,128)(2,1)S(1)} %bitcast.92, f32[1,2048]{1,0:T(1,128)S(1)} %bitcast.94, f32[1,2048]{1,0:T(1,128)S(1)} %bitcast.96, f32[1,1536]{1,0:T(1,128)S(1)} %broadcast_in_dim.171.bias, ...), custom_call_target="tpu_custom_call" | custom-call | flops 196608 | bytes 196608 | tf_op jit(solution)/shard_map/pallas_call | solution.py:220
  100.0 1.0 collective-permute-done.17.rest_2_.rest_8_
  101.1 2.3 %collective-permute-done.15.rest_0_.rest_3_ = bf16[256,768]{1,0:T(8,128)(2,1)S(1)} collective-permute-done((bf16[256,768]{1,0:T(8,128)(2,1)S(1)}, bf16[256,768]{1,0:T(8,128)(2,1)S(1)}, u32[]{:S(2)}, u32[]{:S(2)}) %collective-permute-start.15) | collective-permute-done | bytes 393248 | tf_op jit(solution)/shard_map/ppermute | solution.py:296
  103.4 3.3 %shard_map.105 = bf16[128,512]{1,0:T(8,128)(2,1)} custom-call(s32[2]{0:T(128)S(1)} %copy-done.24, bf16[16,128,128]{2,1,0:T(8,128)(2,1)S(1)} %get-tuple-element.252.normed, f32[128,1536]{1,0:T(8,128)S(1)} %get-tuple-element.253.near, f32[3,128,128]{2,1,0:T(8,128)S(1)} %pad_maximum_fusion.11.turns, f32[128,128]{1,0:T(8,128)S(1)} %get-tuple-element.362.allowed.rest_0_, ...), custom_call_target="tpu_custom_call" | custom-call | flops 196608 | bytes 196608 | tf_op jit(solution)/shard_map/pallas_call | solution.py:220
  106.7 0.7 copy-done.16
  107.4 1.7 fusion.37
  109.2 1.8 compare_reduce_fusion
  113.0 1.9 fusion.18
  115.0 6.3 %all-to-all-start.2 = ((bf16[8,48,512]{2,1,0:T(8,128)(2,1)}), bf16[8,48,512]{2,1,0:T(8,128)(2,1)S(1)}, u32[]{:S(2)}, u32[]{:S(2)}) async-start(bf16[8,48,512]{2,1,0:T(8,128)(2,1)} %bitcast.23), calls=%async_computation.2 | async-start | bytes 786432 | tf_op jit(solution)/shard_map/all_to_all | solution.py:50
  122.5 1.3 slice_select_fusion.1
  123.8 3.2 %collective-permute-start.19 = (bf16[128,512]{1,0:T(8,128)(2,1)}, bf16[128,512]{1,0:T(8,128)(2,1)}, u32[]{:S(2)}, u32[]{:S(2)}) collective-permute-start(bf16[128,512]{1,0:T(8,128)(2,1)} %shard_map.105), channel_id=1, source_target_pairs={{0,128},{128,0},{1,129},{129,1},{2,130},{130,2},{3,131},{131,3},{4... | collective-permute-start | bytes 393224 | tf_op jit(solution)/shard_map/ppermute | solution.py:27
  129.1 0.9 slice.329
  130.0 1.2 slice.327
  131.2 0.7 add_select_fusion
  131.9 6.7 %all-to-all-done.2 = bf16[8,48,512]{2,1,0:T(8,128)(2,1)S(1)} async-done(((bf16[8,48,512]{2,1,0:T(8,128)(2,1)}), bf16[8,48,512]{2,1,0:T(8,128)(2,1)S(1)}, u32[]{:S(2)}, u32[]{:S(2)}) %all-to-all-start.2) | async-done | bytes 393248 | tf_op jit(solution)/shard_map/all_to_all | solution.py:50
  138.6 2.2 %convolution_convert_fusion.2 = bf16[512,1664]{1,0:T(8,128)(2,1)} fusion(bf16[384,128]{1,0:T(8,128)(2,1)S(1)} %slice.329, bf16[384,512]{1,0:T(8,128)(2,1)S(1)} %bitcast.118, bf16[384,1024]{1,0:T(8,128)(2,1)S(1)} %slice.327, s32[384]{0:T(512)S(1)} %add_select_fusion), kind=kOutput, calls=%fused_computation.20 | convolution fusion | flops 659193856 | bytes 2983424 | tf_op jit(solution)/shard_map/dot_general | solution.py:31
  140.9 4.8 %all-to-all-start.3 = ((bf16[16,32,1664]{2,1,0:T(8,128)(2,1)}), bf16[16,32,1664]{2,1,0:T(8,128)(2,1)S(1)}, u32[]{:S(2)}, u32[]{:S(2)}) async-start(bf16[16,32,1664]{2,1,0:T(8,128)(2,1)} %bitcast.113), calls=%async_computation.3 | async-start | bytes 3407872 | tf_op jit(solution)/shard_map/all_to_all | solution.py:50
  145.7 1.7 broadcast_select_fusion.15
  147.4 1.2 slice.330
  148.6 9.8 %all-gather.2.cloned.1.call-done.rest_1_.rest_2_.rest_3_.rest_0_ = bf16[2048,2560]{1,0:T(8,128)(2,1)} async-done(((bf16[16,2560]{1,0:T(8,128)(2,1)}), bf16[2048,2560]{1,0:T(8,128)(2,1)}) %all-gather.2.cloned.1.call-update) | async-done | bytes 10485776 | tf_op jit(solution)/shard_map/all_gather | solution.py:377
  159.8 4.0 %fusion.73 = (bf16[2048,512]{1,0:T(8,128)(2,1)}, bf16[2048,512]{1,0:T(8,128)(2,1)S(1)}) fusion(bf16[2048,2560]{1,0:T(8,128)(2,1)} %all-gather.2.cloned.1.call-done.rest_1_.rest_2_.rest_3_.rest_0_), kind=kLoop, calls=%fused_computation.205 | loop fusion | bytes 8388608 | tf_op jit(solution)/shard_map/slice | solution.py:465
  164.4 0.7 copy-done.9
  165.1 0.8 fusion.28
  165.9 0.7 collective-permute-start.20
  166.6 1.3 shard_map.107
  168.2 0.9 convert_reduce_fusion.1
  169.2 1.0 slice.347
  170.2 5.3 %collective-permute-start.23 = (bf16[128,1536]{1,0:T(8,128)(2,1)S(1)}, bf16[128,1536]{1,0:T(8,128)(2,1)S(1)}, u32[]{:S(2)}, u32[]{:S(2)}) collective-permute-start(bf16[128,1536]{1,0:T(8,128)(2,1)S(1)} %slice.347), channel_id=1, source_target_pairs={{0,128},{128,0},{1,129},{129,1},{2,130},{130,2},{3,131},{131,3},{4... | collective-permute-start | bytes 1179656 | tf_op jit(solution)/shard_map/ppermute | solution.py:27
  175.9 1.1 broadcast_select_fusion.11
  177.0 5.5 %shard_map.106 = bf16[128,512]{1,0:T(8,128)(2,1)S(1)} custom-call(bf16[128,2048]{1,0:T(8,128)(2,1)S(1)} %pad_maximum_fusion.3.layer_in, f32[1,2048]{1,0:T(1,128)S(1)} %bitcast.100, f32[1,2048]{1,0:T(1,128)S(1)} %bitcast.98, f32[1,1536]{1,0:T(1,128)S(1)} %copy-done.22, f32[3,128,128]{2,1,0:T(8,128)S(1)} %pad_maximum_fusion.11.turns, ...), custom_call_target="tpu_custom_call" | custom-call | flops 196608 | bytes 196608 | tf_op jit(solution)/shard_map/pallas_call | solution.py:276
  182.8 1.3 copy-done.31
  184.8 0.9 copy-done.29
  186.6 1.1 fusion.30
  189.8 2.4 %shard_map.108 = bf16[128,1024]{1,0:T(8,128)(2,1)S(1)} custom-call(s32[2]{0:T(128)S(1)} %copy-done.25, bf16[128,2048]{1,0:T(8,128)(2,1)S(1)} %pad_maximum_fusion.4.layer_in, f32[1,2048]{1,0:T(1,128)S(1)} %bitcast.95, f32[1,2048]{1,0:T(1,128)S(1)} %bitcast.97, f32[1,1024]{1,0:T(1,128)S(1)} %copy-done.23, f32[3,128,128]{2,1,0:T(8,128)S(1)} %pad_maximum_fusion.12.turns, ...), custom_call_target="tpu_custom_call" | custom-call | flops 131072 | bytes 131072 | tf_op jit(solution)/shard_map/pallas_call | solution.py:220
  192.2 4.1 %shard_map.109 = bf16[128,1024]{1,0:T(8,128)(2,1)S(1)} custom-call(bf16[128,2048]{1,0:T(8,128)(2,1)S(1)} %pad_maximum_fusion.5.layer_in, f32[1,2048]{1,0:T(1,128)S(1)} %bitcast.101, f32[1,2048]{1,0:T(1,128)S(1)} %bitcast.99, f32[1,1024]{1,0:T(1,128)S(1)} %slice.294.bias, f32[3,128,128]{2,1,0:T(8,128)S(1)} %pad_maximum_fusion.12.turns, ...), custom_call_target="tpu_custom_call" | custom-call | flops 131072 | bytes 131072 | tf_op jit(solution)/shard_map/pallas_call | solution.py:276
  196.9 0.9 maximum_select_fusion
  198.1 0.8 maximum_bitcast_fusion
  (235 shorter events, 15.3 us)
Async XLA Ops:
  7.2 151.3 %all-gather.2.cloned.1.call-start = ((), (), s32[]{:S(2)}) async-start(), calls=%async_computation.4 | async-start | bytes 10567680 | tf_op jit(solution)/shard_map/all_gather | solution.py:377
  8.8 4.2 %collective-permute-start = (bf16[16,2048]{1,0:T(8,128)(2,1)S(1)}, bf16[16,2048]{1,0:T(8,128)(2,1)S(1)}, u32[]{:S(2)}, u32[]{:S(2)}) collective-permute-start(bf16[16,2048]{1,0:T(8,128)(2,1)S(1)} %broadcast_select_fusion.18), channel_id=1, source_target_pairs={{0,128},{128,0},{1,129},{129,1},{2,130},{130,2},{3,131},{131,3},{4... | collective-permute-start | bytes 196616 | tf_op jit(solution)/shard_map/ppermute | solution.py:27
  13.8 46.6 %copy-start.52 = (pred[128]{0:T(512)(128)(4,1)}, pred[128]{0:T(512)(128)(4,1)S(1)}, u32[]{:S(2)}) copy-start(pred[128]{0:T(512)(128)(4,1)S(1)} %iota_compare_fusion.19) | copy-start | bytes 388
  13.8 7.0 %collective-permute-start.1 = (bf16[1,16,1536]{2,1,0:T(8,128)(2,1)S(1)}, bf16[1,16,1536]{2,1,0:T(8,128)(2,1)S(1)}, u32[]{:S(2)}, u32[]{:S(2)}) collective-permute-start(bf16[1,16,1536]{2,1,0:T(8,128)(2,1)S(1)} %slice_bitcast_fusion.10), channel_id=1, source_target_pairs={{0,4},{1,5},{2,6},{3,7},{4,0},{5,1},{6,2},{7,3},{8,12},{9,13},{10,... | collective-permute-start | bytes 147464 | tf_op jit(solution)/shard_map/ppermute | solution.py:322
  19.1 41.3 %copy-start.54 = (f32[128]{0:T(128)}, f32[128]{0:T(128)S(1)}, u32[]{:S(2)}) copy-start(f32[128]{0:T(128)S(1)} %multiply_power_fusion) | copy-start | bytes 1540
  20.9 7.0 %collective-permute-start.2 = (bf16[2,16,1536]{2,1,0:T(8,128)(2,1)S(1)}, bf16[2,16,1536]{2,1,0:T(8,128)(2,1)S(1)}, u32[]{:S(2)}, u32[]{:S(2)}) collective-permute-start(bf16[2,16,1536]{2,1,0:T(8,128)(2,1)S(1)} %maximum_bitcast_fusion.1), channel_id=1, source_target_pairs={{0,2},{1,3},{2,0},{3,1},{4,6},{5,7},{6,4},{7,5},{8,10},{9,11},{10,... | collective-permute-start | bytes 294920 | tf_op jit(solution)/shard_map/ppermute | solution.py:322
  22.1 23.5 %copy-start.47 = (s32[4,32]{1,0:T(4,128)S(1)}, s32[4,32]{1,0:T(4,128)}, u32[]{:S(2)}) copy-start(s32[4,32]{1,0:T(4,128)} %param.15) | copy-start | bytes 1540
  22.1 23.6 %copy-start.62 = (s32[4,32]{1,0:T(4,128)S(1)}, s32[4,32]{1,0:T(4,128)}, u32[]{:S(2)}) copy-start(s32[4,32]{1,0:T(4,128)} %param.14) | copy-start | bytes 1540
  27.9 20.6 %copy-start.37 = (f32[1,3072]{1,0:T(1,128)S(1)}, f32[1,3072]{1,0:T(1,128)}, u32[]{:S(2)}) copy-start(f32[1,3072]{1,0:T(1,128)} %param.19) | copy-start | bytes 36868
  28.0 20.6 %copy-start.40 = (f32[1,2048]{1,0:T(1,128)S(1)}, f32[1,2048]{1,0:T(1,128)}, u32[]{:S(2)}) copy-start(f32[1,2048]{1,0:T(1,128)} %param.21) | copy-start | bytes 24580
  28.0 20.6 %copy-start.41 = (f32[1,2048]{1,0:T(1,128)S(1)}, f32[1,2048]{1,0:T(1,128)}, u32[]{:S(2)}) copy-start(f32[1,2048]{1,0:T(1,128)} %param.17) | copy-start | bytes 24580
  28.0 20.6 %copy-start.42 = (f32[1,2048]{1,0:T(1,128)S(1)}, f32[1,2048]{1,0:T(1,128)}, u32[]{:S(2)}) copy-start(f32[1,2048]{1,0:T(1,128)} %param.16) | copy-start | bytes 24580
  28.0 25.2 %copy-start.8 = (bf16[4,32,2048]{2,1,0:T(8,128)(2,1)S(1)}, bf16[4,32,2048]{2,1,0:T(8,128)(2,1)}, u32[]{:S(2)}) copy-start(bf16[4,32,2048]{2,1,0:T(8,128)(2,1)} %param.13) | copy-start | bytes 1572868
  28.1 5.9 %collective-permute-start.3 = (bf16[4,16,1536]{2,1,0:T(8,128)(2,1)S(1)}, bf16[4,16,1536]{2,1,0:T(8,128)(2,1)S(1)}, u32[]{:S(2)}, u32[]{:S(2)}) collective-permute-start(bf16[4,16,1536]{2,1,0:T(8,128)(2,1)S(1)} %bitcast.117), channel_id=1, source_target_pairs={{0,1},{1,0},{2,3},{3,2},{4,5},{5,4},{6,7},{7,6},{8,9},{9,8},{10,11... | collective-permute-start | bytes 589832 | tf_op jit(solution)/shard_map/ppermute | solution.py:322
  34.1 6.0 %collective-permute-start.7 = (bf16[128,768]{1,0:T(8,128)(2,1)S(1)}, bf16[128,768]{1,0:T(8,128)(2,1)S(1)}, u32[]{:S(2)}, u32[]{:S(2)}) collective-permute-start(bf16[128,768]{1,0:T(8,128)(2,1)S(1)} %get-tuple-element.317), channel_id=1, source_target_pairs={{0,96},{32,0},{64,32},{96,64},{1,97},{33,1},{65,33},{97,65},{2,98}... | collective-permute-start | bytes 589832 | tf_op jit(solution)/shard_map/ppermute | solution.py:296
  36.7 5.8 %collective-permute-start.5 = (bf16[128,768]{1,0:T(8,128)(2,1)S(1)}, bf16[128,768]{1,0:T(8,128)(2,1)S(1)}, u32[]{:S(2)}, u32[]{:S(2)}) collective-permute-start(bf16[128,768]{1,0:T(8,128)(2,1)S(1)} %get-tuple-element.317), channel_id=1, source_target_pairs={{0,32},{32,64},{64,96},{96,0},{1,33},{33,65},{65,97},{97,1},{2,34}... | collective-permute-start | bytes 589832 | tf_op jit(solution)/shard_map/ppermute | solution.py:296
  36.7 5.8 %collective-permute-start.6 = (bf16[128,768]{1,0:T(8,128)(2,1)S(1)}, bf16[128,768]{1,0:T(8,128)(2,1)S(1)}, u32[]{:S(2)}, u32[]{:S(2)}) collective-permute-start(bf16[128,768]{1,0:T(8,128)(2,1)S(1)} %get-tuple-element.318), channel_id=1, source_target_pairs={{0,24},{8,0},{16,8},{24,16},{1,25},{9,1},{17,9},{25,17},{2,26},{10... | collective-permute-start | bytes 589832 | tf_op jit(solution)/shard_map/ppermute | solution.py:296
  39.4 6.3 %collective-permute-start.4 = (bf16[128,768]{1,0:T(8,128)(2,1)S(1)}, bf16[128,768]{1,0:T(8,128)(2,1)S(1)}, u32[]{:S(2)}, u32[]{:S(2)}) collective-permute-start(bf16[128,768]{1,0:T(8,128)(2,1)S(1)} %get-tuple-element.318), channel_id=1, source_target_pairs={{0,8},{8,16},{16,24},{24,0},{1,9},{9,17},{17,25},{25,1},{2,10},{10... | collective-permute-start | bytes 589832 | tf_op jit(solution)/shard_map/ppermute | solution.py:296
  40.1 20.8 %copy-start.56 = (pred[128]{0:T(512)(128)(4,1)}, pred[128]{0:T(512)(128)(4,1)S(1)}, u32[]{:S(2)}) copy-start(pred[128]{0:T(512)(128)(4,1)S(1)} %get-tuple-element.379) | copy-start | bytes 388
  40.1 20.8 %copy-start.58 = (pred[128]{0:T(512)(128)(4,1)}, pred[128]{0:T(512)(128)(4,1)S(1)}, u32[]{:S(2)}) copy-start(pred[128]{0:T(512)(128)(4,1)S(1)} %get-tuple-element.380) | copy-start | bytes 388
  45.8 15.1 %copy-start.50 = (s32[128]{0:T(128)}, s32[128]{0:T(128)S(1)}, u32[]{:S(2)}) copy-start(s32[128]{0:T(128)S(1)} %reshape.854) | copy-start | bytes 1540
  48.6 18.6 %collective-permute-start.8 = (f32[9216]{0:T(1024)S(1)}, f32[9216]{0:T(1024)S(1)}, u32[]{:S(2)}, u32[]{:S(2)}) collective-permute-start(f32[9216]{0:T(1024)S(1)} %pad_maximum_fusion.20), channel_id=1, source_target_pairs={{0,128},{128,0},{1,129},{129,1},{2,130},{130,2},{3,131},{131,3},{4... | collective-permute-start | bytes 110600 | tf_op jit(solution)/shard_map/ppermute | solution.py:27
  51.8 8.9 %collective-permute-start.9 = (bf16[128,768]{1,0:T(8,128)(2,1)S(1)}, bf16[128,768]{1,0:T(8,128)(2,1)S(1)}, u32[]{:S(2)}, u32[]{:S(2)}) collective-permute-start(bf16[128,768]{1,0:T(8,128)(2,1)S(1)} %collective-permute-done.4), channel_id=1, source_target_pairs={{0,8},{8,16},{16,24},{24,0},{1,9},{9,17},{17,25},{25,1},{2,10},{10... | collective-permute-start | bytes 589832 | tf_op jit(solution)/shard_map/ppermute | solution.py:296
  51.8 9.1 %collective-permute-start.10 = (bf16[128,768]{1,0:T(8,128)(2,1)S(1)}, bf16[128,768]{1,0:T(8,128)(2,1)S(1)}, u32[]{:S(2)}, u32[]{:S(2)}) collective-permute-start(bf16[128,768]{1,0:T(8,128)(2,1)S(1)} %collective-permute-done.5), channel_id=1, source_target_pairs={{0,32},{32,64},{64,96},{96,0},{1,33},{33,65},{65,97},{97,1},{2,34}... | collective-permute-start | bytes 589832 | tf_op jit(solution)/shard_map/ppermute | solution.py:296
  53.0 7.8 %copy-start.60 = (s32[128]{0:T(128)}, s32[128]{0:T(128)S(1)}, u32[]{:S(2)}) copy-start(s32[128]{0:T(128)S(1)} %get-tuple-element.366) | copy-start | bytes 1540
  53.1 7.7 %copy-start.32 = (bf16[128,128]{1,0:T(8,128)(2,1)}, bf16[128,128]{1,0:T(8,128)(2,1)S(1)}, u32[]{:S(2)}) copy-start(bf16[128,128]{1,0:T(8,128)(2,1)S(1)} %select_convert_fusion) | copy-start | bytes 98308
  55.3 52.1 %all-to-all-start.1 = ((bf16[8,48,1152]{2,1,0:T(8,128)(2,1)}), bf16[8,48,1152]{2,1,0:T(8,128)(2,1)}, u32[]{:S(2)}, u32[]{:S(2)}) async-start(bf16[8,48,1152]{2,1,0:T(8,128)(2,1)} %bitcast.21), calls=%async_computation.1 | async-start | bytes 1769472 | tf_op jit(solution)/shard_map/all_to_all | solution.py:50
  60.9 36.3 %copy-start.24 = (s32[2]{0:T(128)S(1)}, s32[2]{0:T(128)}, u32[]{:S(2)}) copy-start(s32[2]{0:T(128)} %pad_add_fusion.place) | copy-start | bytes 28
  60.9 26.0 %collective-permute-start.13 = (bf16[512,768]{1,0:T(8,128)(2,1)S(1)}, bf16[512,768]{1,0:T(8,128)(2,1)S(1)}, u32[]{:S(2)}, u32[]{:S(2)}) collective-permute-start(bf16[512,768]{1,0:T(8,128)(2,1)S(1)} %pad_maximum_fusion.1.rest_0_), channel_id=1, source_target_pairs={{0,96},{32,0},{64,32},{96,64},{1,97},{33,1},{65,33},{97,65},{2,98}... | collective-permute-start | bytes 2359304 | tf_op jit(solution)/shard_map/ppermute | solution.py:296
  63.7 26.5 %collective-permute-start.11 = (bf16[512,768]{1,0:T(8,128)(2,1)S(1)}, bf16[512,768]{1,0:T(8,128)(2,1)S(1)}, u32[]{:S(2)}, u32[]{:S(2)}) collective-permute-start(bf16[512,768]{1,0:T(8,128)(2,1)S(1)} %pad_maximum_fusion.1.rest_0_), channel_id=1, source_target_pairs={{0,32},{32,64},{64,96},{96,0},{1,33},{33,65},{65,97},{97,1},{2,34}... | collective-permute-start | bytes 2359304 | tf_op jit(solution)/shard_map/ppermute | solution.py:296
  63.7 26.5 %collective-permute-start.14 = (bf16[512,768]{1,0:T(8,128)(2,1)S(1)}, bf16[512,768]{1,0:T(8,128)(2,1)S(1)}, u32[]{:S(2)}, u32[]{:S(2)}) collective-permute-start(bf16[512,768]{1,0:T(8,128)(2,1)S(1)} %pad_maximum_fusion.2.rest_3_.rest_5_), channel_id=1, source_target_pairs={{0,24},{8,0},{16,8},{24,16},{1,25},{9,1},{17,9},{25,17},{2,26},{10... | collective-permute-start | bytes 2359304 | tf_op jit(solution)/shard_map/ppermute | solution.py:296
  66.4 23.8 %collective-permute-start.12 = (bf16[512,768]{1,0:T(8,128)(2,1)S(1)}, bf16[512,768]{1,0:T(8,128)(2,1)S(1)}, u32[]{:S(2)}, u32[]{:S(2)}) collective-permute-start(bf16[512,768]{1,0:T(8,128)(2,1)S(1)} %pad_maximum_fusion.2.rest_3_.rest_5_), channel_id=1, source_target_pairs={{0,8},{8,16},{16,24},{24,0},{1,9},{9,17},{17,25},{25,1},{2,10},{10... | collective-permute-start | bytes 2359304 | tf_op jit(solution)/shard_map/ppermute | solution.py:296
  67.2 30.1 %copy-start.33 = (f32[9216]{0:T(1024)}, f32[9216]{0:T(1024)S(1)}, u32[]{:S(2)}) copy-start(f32[9216]{0:T(1024)S(1)} %get-tuple-element.339) | copy-start | bytes 110596
  67.2 30.1 %copy-start.34 = (f32[9216]{0:T(1024)}, f32[9216]{0:T(1024)S(1)}, u32[]{:S(2)}) copy-start(f32[9216]{0:T(1024)S(1)} %get-tuple-element.340) | copy-start | bytes 110596
  87.0 13.0 %copy-start = (bf16[512,768]{1,0:T(8,128)(2,1)}, bf16[512,768]{1,0:T(8,128)(2,1)S(1)}, u32[]{:S(2)}) copy-start(bf16[512,768]{1,0:T(8,128)(2,1)S(1)} %collective-permute-done.13.rest_1_) | copy-start | bytes 2359300
  90.2 9.8 %copy-start.2 = (bf16[512,768]{1,0:T(8,128)(2,1)}, bf16[512,768]{1,0:T(8,128)(2,1)S(1)}, u32[]{:S(2)}) copy-start(bf16[512,768]{1,0:T(8,128)(2,1)S(1)} %collective-permute-done.11.rest_2_) | copy-start | bytes 2359300
  90.2 9.8 %copy-start.4 = (bf16[512,768]{1,0:T(8,128)(2,1)}, bf16[512,768]{1,0:T(8,128)(2,1)S(1)}, u32[]{:S(2)}) copy-start(bf16[512,768]{1,0:T(8,128)(2,1)S(1)} %collective-permute-done.14.rest_4_.rest_6_) | copy-start | bytes 2359300
  90.2 9.8 %copy-start.6 = (bf16[512,768]{1,0:T(8,128)(2,1)}, bf16[512,768]{1,0:T(8,128)(2,1)S(1)}, u32[]{:S(2)}) copy-start(bf16[512,768]{1,0:T(8,128)(2,1)S(1)} %collective-permute-done.12.rest_5_.rest_7_) | copy-start | bytes 2359300
  90.3 10.7 %collective-permute-start.17 = (bf16[256,768]{1,0:T(8,128)(2,1)S(1)}, bf16[256,768]{1,0:T(8,128)(2,1)S(1)}, u32[]{:S(2)}, u32[]{:S(2)}) collective-permute-start(bf16[256,768]{1,0:T(8,128)(2,1)S(1)} %slice.258), channel_id=1, source_target_pairs={{0,8},{8,16},{16,24},{24,0},{1,9},{9,17},{17,25},{25,1},{2,10},{10... | collective-permute-start | bytes 1179656 | tf_op jit(solution)/shard_map/ppermute | solution.py:296
  90.4 10.7 %collective-permute-start.18 = (bf16[256,768]{1,0:T(8,128)(2,1)S(1)}, bf16[256,768]{1,0:T(8,128)(2,1)S(1)}, u32[]{:S(2)}, u32[]{:S(2)}) collective-permute-start(bf16[256,768]{1,0:T(8,128)(2,1)S(1)} %slice.259), channel_id=1, source_target_pairs={{0,24},{8,0},{16,8},{24,16},{1,25},{9,1},{17,9},{25,17},{2,26},{10... | collective-permute-start | bytes 1179656 | tf_op jit(solution)/shard_map/ppermute | solution.py:296
  93.4 10.0 %collective-permute-start.15 = (bf16[256,768]{1,0:T(8,128)(2,1)S(1)}, bf16[256,768]{1,0:T(8,128)(2,1)S(1)}, u32[]{:S(2)}, u32[]{:S(2)}) collective-permute-start(bf16[256,768]{1,0:T(8,128)(2,1)S(1)} %slice.256), channel_id=1, source_target_pairs={{0,32},{32,64},{64,96},{96,0},{1,33},{33,65},{65,97},{97,1},{2,34}... | collective-permute-start | bytes 1179656 | tf_op jit(solution)/shard_map/ppermute | solution.py:296
  93.4 10.0 %collective-permute-start.16 = (bf16[256,768]{1,0:T(8,128)(2,1)S(1)}, bf16[256,768]{1,0:T(8,128)(2,1)S(1)}, u32[]{:S(2)}, u32[]{:S(2)}) collective-permute-start(bf16[256,768]{1,0:T(8,128)(2,1)S(1)} %slice.257), channel_id=1, source_target_pairs={{0,96},{32,0},{64,32},{96,64},{1,97},{33,1},{65,33},{97,65},{2,98}... | collective-permute-start | bytes 1179656 | tf_op jit(solution)/shard_map/ppermute | solution.py:296
  100.0 13.0 %copy-start.61 = (s32[128]{0:T(128)S(1)}, s32[128]{0:T(128)}, u32[]{:S(2)}) copy-start(s32[128]{0:T(128)} %copy-done.60) | copy-start | bytes 1540
  101.1 13.9 %copy-start.10 = (bf16[256,768]{1,0:T(8,128)(2,1)}, bf16[256,768]{1,0:T(8,128)(2,1)S(1)}, u32[]{:S(2)}) copy-start(bf16[256,768]{1,0:T(8,128)(2,1)S(1)} %collective-permute-done.17.rest_2_.rest_8_) | copy-start | bytes 1179652
  101.1 13.9 %copy-start.12 = (bf16[256,768]{1,0:T(8,128)(2,1)}, bf16[256,768]{1,0:T(8,128)(2,1)S(1)}, u32[]{:S(2)}) copy-start(bf16[256,768]{1,0:T(8,128)(2,1)S(1)} %collective-permute-done.18.rest_3_.rest_9_) | copy-start | bytes 1179652
  103.4 11.6 %copy-start.14 = (bf16[256,768]{1,0:T(8,128)(2,1)}, bf16[256,768]{1,0:T(8,128)(2,1)S(1)}, u32[]{:S(2)}) copy-start(bf16[256,768]{1,0:T(8,128)(2,1)S(1)} %collective-permute-done.15.rest_0_.rest_3_) | copy-start | bytes 1179652
  103.4 17.9 %copy-start.21 = (f32[1,1536]{1,0:T(1,128)S(1)}, f32[1,1536]{1,0:T(1,128)}, u32[]{:S(2)}) copy-start(f32[1,1536]{1,0:T(1,128)} %copy-done.20) | copy-start | bytes 18436
  103.4 18.5 %copy-start.44 = (f32[512]{0:T(512)S(1)}, f32[512]{0:T(512)}, u32[]{:S(2)}) copy-start(f32[512]{0:T(512)} %get-tuple-element.341) | copy-start | bytes 6148
  103.4 18.5 %copy-start.45 = (f32[512]{0:T(512)S(1)}, f32[512]{0:T(512)}, u32[]{:S(2)}) copy-start(f32[512]{0:T(512)} %get-tuple-element.342) | copy-start | bytes 6148
  103.4 18.5 %copy-start.46 = (f32[512]{0:T(512)S(1)}, f32[512]{0:T(512)}, u32[]{:S(2)}) copy-start(f32[512]{0:T(512)} %get-tuple-element.343) | copy-start | bytes 6148
  111.0 18.1 %copy-start.51 = (pred[384]{0:T(512)(128)(4,1)}, pred[384]{0:T(512)(128)(4,1)S(1)}, u32[]{:S(2)}) copy-start(pred[384]{0:T(512)(128)(4,1)S(1)} %get-tuple-element.291) | copy-start | bytes 1156
  111.2 17.9 %copy-start.49 = (f32[384]{0:T(512)}, f32[384]{0:T(512)S(1)}, u32[]{:S(2)}) copy-start(f32[384]{0:T(512)S(1)} %fusion.19) | copy-start | bytes 4612
  115.0 16.3 %copy-start.48 = (s32[384]{0:T(512)S(1)}, s32[384]{0:T(512)}, u32[]{:S(2)}) copy-start(s32[384]{0:T(512)} %get-tuple-element.288) | copy-start | bytes 4612
  115.0 23.7 %all-to-all-start.2 = ((bf16[8,48,512]{2,1,0:T(8,128)(2,1)}), bf16[8,48,512]{2,1,0:T(8,128)(2,1)S(1)}, u32[]{:S(2)}, u32[]{:S(2)}) async-start(bf16[8,48,512]{2,1,0:T(8,128)(2,1)} %bitcast.23), calls=%async_computation.2 | async-start | bytes 786432 | tf_op jit(solution)/shard_map/all_to_all | solution.py:50
  123.8 21.9 %collective-permute-start.19 = (bf16[128,512]{1,0:T(8,128)(2,1)}, bf16[128,512]{1,0:T(8,128)(2,1)}, u32[]{:S(2)}, u32[]{:S(2)}) collective-permute-start(bf16[128,512]{1,0:T(8,128)(2,1)} %shard_map.105), channel_id=1, source_target_pairs={{0,128},{128,0},{1,129},{129,1},{2,130},{130,2},{3,131},{131,3},{4... | collective-permute-start | bytes 393224 | tf_op jit(solution)/shard_map/ppermute | solution.py:27
  140.9 25.7 %all-to-all-start.3 = ((bf16[16,32,1664]{2,1,0:T(8,128)(2,1)}), bf16[16,32,1664]{2,1,0:T(8,128)(2,1)S(1)}, u32[]{:S(2)}, u32[]{:S(2)}) async-start(bf16[16,32,1664]{2,1,0:T(8,128)(2,1)} %bitcast.113), calls=%async_computation.3 | async-start | bytes 3407872 | tf_op jit(solution)/shard_map/all_to_all | solution.py:50
  165.9 9.9 %collective-permute-start.20 = (bf16[128,1024]{1,0:T(8,128)(2,1)}, bf16[128,1024]{1,0:T(8,128)(2,1)}, u32[]{:S(2)}, u32[]{:S(2)}) collective-permute-start(bf16[128,1024]{1,0:T(8,128)(2,1)} %fusion.28), channel_id=1, source_target_pairs={{0,128},{128,0},{1,129},{129,1},{2,130},{130,2},{3,131},{131,3},{4... | collective-permute-start | bytes 786440 | tf_op jit(solution)/shard_map/ppermute | solution.py:27
  168.2 8.8 %copy-start.18 = (f32[2048]{0:T(1024)S(1)}, f32[2048]{0:T(1024)}, u32[]{:S(2)}) copy-start(f32[2048]{0:T(1024)} %get-tuple-element.344) | copy-start | bytes 24580
  168.2 8.8 %copy-start.19 = (f32[2048]{0:T(1024)S(1)}, f32[2048]{0:T(1024)}, u32[]{:S(2)}) copy-start(f32[2048]{0:T(1024)} %get-tuple-element.345) | copy-start | bytes 24580
  170.2 12.5 %collective-permute-start.23 = (bf16[128,1536]{1,0:T(8,128)(2,1)S(1)}, bf16[128,1536]{1,0:T(8,128)(2,1)S(1)}, u32[]{:S(2)}, u32[]{:S(2)}) collective-permute-start(bf16[128,1536]{1,0:T(8,128)(2,1)S(1)} %slice.347), channel_id=1, source_target_pairs={{0,128},{128,0},{1,129},{129,1},{2,130},{130,2},{3,131},{131,3},{4... | collective-permute-start | bytes 1179656 | tf_op jit(solution)/shard_map/ppermute | solution.py:27
  182.6 2.2 %collective-permute-start.21 = (bf16[128,512]{1,0:T(8,128)(2,1)S(1)}, bf16[128,512]{1,0:T(8,128)(2,1)S(1)}, u32[]{:S(2)}, u32[]{:S(2)}) collective-permute-start(bf16[128,512]{1,0:T(8,128)(2,1)S(1)} %shard_map.106), channel_id=1, source_target_pairs={{0,128},{128,0},{1,129},{129,1},{2,130},{130,2},{3,131},{131,3},{4... | collective-permute-start | bytes 393224 | tf_op jit(solution)/shard_map/ppermute | solution.py:27
  186.5 2.0 collective-permute-start.24
  187.8 9.0 %collective-permute-start.22 = (bf16[128,1024]{1,0:T(8,128)(2,1)S(1)}, bf16[128,1024]{1,0:T(8,128)(2,1)S(1)}, u32[]{:S(2)}, u32[]{:S(2)}) collective-permute-start(bf16[128,1024]{1,0:T(8,128)(2,1)S(1)} %fusion.30), channel_id=1, source_target_pairs={{0,128},{128,0},{1,129},{129,1},{2,130},{130,2},{3,131},{131,3},{4... | collective-permute-start | bytes 786440 | tf_op jit(solution)/shard_map/ppermute | solution.py:27
  196.3 1.7 collective-permute-start.25
  (28 other events, 79.5 us)
Sparse Core Ops, SparseCore 0:
  13.9 144.5 all-gather.1

commit v2 on v1

--- a/solution.py
+++ b/solution.py
@@ -205,6 +205,28 @@
     @pl.when(step == pl.num_programs(0) - 1)
     def _():
         conclude(total[...], turns, allowed, out_ref)
+
+
+def slots_kernel(cap, meta, choice, flag):
+    info = meta[...].astype(F32)
+    lane = lax.broadcasted_iota(jnp.int32, info.shape, 1)
+
+    def column(k):
+        return jnp.sum(jnp.where(lane == k, info, 0.0), axis=1, keepdims=True)
+
+    valid = jnp.where(column(0) > 0.0, 1.0, 0.0)
+    dest = column(2)
+    hits = jnp.where(lane.astype(F32) == dest, 1.0, 0.0) * valid
+    square = (info.shape[0], info.shape[0])
+    row = lax.broadcasted_iota(jnp.int32, square, 0)
+    earlier = jnp.where(lax.broadcasted_iota(jnp.int32, square, 1) < row, 1.0, 0.0)
+    before = mm(earlier.astype(BF), hits.astype(BF))
+    rank = jnp.sum(before * hits, axis=1, keepdims=True)
+    slot = jnp.where(rank < cap, dest * cap + rank, -1.0) * valid + (valid - 1.0)
+    place = lax.broadcasted_iota(jnp.int32, choice.shape, 1).astype(F32)
+    choice[...] = jnp.where(place == slot, 1.0, 0.0).astype(BF)
+    over = jnp.where(rank < cap, 0.0, 1.0) * valid + column(3)
+    flag[...] = jnp.broadcast_to(jnp.sum(over, axis=0, keepdims=True), flag.shape)
 
 
 def cost(rows, width, cols):
@@ -435,21 +457,27 @@
     place = jnp.stack([lax.axis_index("x"), lax.axis_index("y")]).astype(jnp.int32)
     turns = turns_of(positions.astype(F32))
     middle = across(filled, "z", CAP_Z)
-    slot_p, out_p = slots_of(
-        middle[:, half_width + 2].astype(jnp.int32),
-        middle[:, half_width] > 0,
-        device_count // depth,
-        CAP_P,
-    )
     slots_p = device_count // depth * CAP_P
-    send_p = chooser(slots_p, slot_p)
-    ran_out = out_p | jnp.any(middle[:, flag_at] > 0)
+    send_p, flags = pl.pallas_call(
+        functools.partial(slots_kernel, CAP_P),
+        grid=(1,),
+        out_shape=(of((middle.shape[0], slots_p), BF), of((1, LANES), F32)),
+        in_specs=[pl.BlockSpec((middle.shape[0], META), lambda k: (0, half_width // META))],
+        out_specs=(
+            pl.BlockSpec((middle.shape[0], slots_p), lambda k: (0, 0)),
+            pl.BlockSpec((1, LANES), lambda k: (0, 0)),
+        ),
+        cost_estimate=cost(128, 128, 128),
+    )(middle)
+    ran_out = flags[0, 0] > 0
 
     context0 = context_by_pieces(place, flat, rows0, turns, allowed, pieces)
     filled = jnp.where(ran_out, jnp.nan, mm(send_z, context0)).astype(BF)
     middle0 = across(filled, "z", CAP_Z)
     leg = jnp.concatenate([middle[:, :half_width], middle0, middle[:, half_width:]], axis=1)
-    leg = mm(send_p, leg).astype(BF)
+    leg = lax.dot_general(
+        send_p, leg, (((0,), (0,)), ((), ())), preferred_element_type=F32
+    ).astype(BF)
     wide = half_width + part
     arrived = across(leg, PLANE, CAP_P)
     gathered, leg_mark, rows1, out_bias0, out_bias1 = lax.optimization_barrier(

time: 207 us -> 204 us (0.986)
  other arithmetic: 20.4 us -> 15.5 us
  Pallas kernels: 19.2 us -> 21.4 us
    dot_general x11 -> x9, matrix products: 7.7 us -> 5.19 us  [mm(): return jnp.dot(a, b, preferred_element_type=F32)]
    dot_general x0 -> x1, matrix products: none -> 2.35 us  [shards(): lax.dot_general(send_p, leg, (((0,), (0,)), ((), ())), preferred_element_...]
    pallas_call x0 -> x1, Pallas kernels: none -> 2.17 us  [shards(): pl.pallas_call(functools.partial(slots_kernel, CAP_P), grid=(1,), out_sha...]
    unnamed x124 -> x120, local copies, waits for them, and re-layouts: 5.91 us -> 5.9 us
  transfers between devices with their start and end apart: 30 -> 30, of which waited for: 13 -> 13; matrix products, arithmetic and copies ran while one was open for 19% -> 16% of each run, Pallas kernels for 9% -> 11%
where the time goes in v2:
time: 204 us; the launch traced here: 203 us
  waiting for transfers between devices  64.6 us (32%)
  starting transfers between devices  55.9 us (27%)
  Pallas kernels  21.4 us (10%)
  local copies, waits for them, and re-layouts  20.2 us (10%)
  between operations  17.9 us (9%)
  other arithmetic  15.5 us (8%)
  matrix products  7.54 us (4%)
    ppermute x14, waiting for transfers between devices, shifted(): lax.ppermute(value, axis, [(one, (one + by) % size) for one in range(size)])  31.9 us
    all_to_all x3, starting transfers between devices, across(): lax.all_to_all(filled.reshape(-1, cap, cols), axes, split_axis=0, concat_...  16.8 us
    ppermute x14, starting transfers between devices, shifted(): lax.ppermute(value, axis, [(one, (one + by) % size) for one in range(size)])  16.8 us
    ppermute x9, starting transfers between devices, swap(): return lax.ppermute(value, 'pipe', [(0, 1), (1, 0)])  15.6 us
    ppermute x3, waiting for transfers between devices, column_of(): got = lax.ppermute(block, 'z', [(one, one ^ step) for one in range(size)])  13.3 us
    all_gather x1, waiting for transfers between devices, shards(): gathered = lax.all_gather(bulk, DP, axis=0, tiled=True)  11 us
    pallas_call x4, Pallas kernels, call(): pl.pallas_call(kernel, out_shape=out_shape, in_specs=in_specs, out_specs=...  9.63 us
    pallas_call x2, Pallas kernels, project_whole(): pl.pallas_call(functools.partial(whole_kernel, with_context), grid=(width...  9.59 us
  transfers between devices with their start and end apart: 30, of which 13 were waited for; matrix products, arithmetic and copies ran while one was open for 16% of the time, Pallas kernels for 11%

profile of v2, /device:TPU:1, one launch (start us, length us, event | category | flops | bytes accessed | tf_op | source)
XLA Modules:
  0.0 203.3 jit_solution(5604403932409041568)
XLA Ops:
  7.2 0.8 fusion.69
  8.0 0.8 fusion.66
  8.8 3.3 %collective-permute-start = (bf16[16,2048]{1,0:T(8,128)(2,1)S(1)}, bf16[16,2048]{1,0:T(8,128)(2,1)S(1)}, u32[]{:S(2)}, u32[]{:S(2)}) collective-permute-start(bf16[16,2048]{1,0:T(8,128)(2,1)S(1)} %broadcast_select_fusion.18), channel_id=1, source_target_pairs={{0,128},{128,0},{1,129},{129,1},{2,130},{130,2},{3,131},{131,3},{4... | collective-permute-start | bytes 196616 | tf_op jit(solution)/shard_map/ppermute | solution.py:27
  12.1 0.9 collective-permute-done
  13.1 0.6 pad_maximum_fusion.19
  13.8 5.3 %collective-permute-start.1 = (bf16[1,16,1536]{2,1,0:T(8,128)(2,1)S(1)}, bf16[1,16,1536]{2,1,0:T(8,128)(2,1)S(1)}, u32[]{:S(2)}, u32[]{:S(2)}) collective-permute-start(bf16[1,16,1536]{2,1,0:T(8,128)(2,1)S(1)} %slice_bitcast_fusion.10), channel_id=1, source_target_pairs={{0,4},{1,5},{2,6},{3,7},{4,0},{5,1},{6,2},{7,3},{8,12},{9,13},{10,... | collective-permute-start | bytes 147464 | tf_op jit(solution)/shard_map/ppermute | solution.py:344
  19.1 1.8 collective-permute-done.1
  20.9 1.2 collective-permute-start.2
  22.1 5.8 %collective-permute-done.2 = bf16[2,16,1536]{2,1,0:T(8,128)(2,1)S(1)} collective-permute-done((bf16[2,16,1536]{2,1,0:T(8,128)(2,1)S(1)}, bf16[2,16,1536]{2,1,0:T(8,128)(2,1)S(1)}, u32[]{:S(2)}, u32[]{:S(2)}) %collective-permute-start.2) | collective-permute-done | bytes 98336 | tf_op jit(solution)/shard_map/ppermute | solution.py:344
  28.2 5.8 %collective-permute-done.3 = bf16[4,16,1536]{2,1,0:T(8,128)(2,1)S(1)} collective-permute-done((bf16[4,16,1536]{2,1,0:T(8,128)(2,1)S(1)}, bf16[4,16,1536]{2,1,0:T(8,128)(2,1)S(1)}, u32[]{:S(2)}, u32[]{:S(2)}) %collective-permute-start.3) | collective-permute-done | bytes 196640 | tf_op jit(solution)/shard_map/ppermute | solution.py:344
  34.1 2.6 %collective-permute-start.7 = (bf16[128,768]{1,0:T(8,128)(2,1)S(1)}, bf16[128,768]{1,0:T(8,128)(2,1)S(1)}, u32[]{:S(2)}, u32[]{:S(2)}) collective-permute-start(bf16[128,768]{1,0:T(8,128)(2,1)S(1)} %get-tuple-element.317), channel_id=1, source_target_pairs={{0,96},{32,0},{64,32},{96,64},{1,97},{33,1},{65,33},{97,65},{2,98}... | collective-permute-start | bytes 589832 | tf_op jit(solution)/shard_map/ppermute | solution.py:318
  36.7 2.7 %collective-permute-start.6 = (bf16[128,768]{1,0:T(8,128)(2,1)S(1)}, bf16[128,768]{1,0:T(8,128)(2,1)S(1)}, u32[]{:S(2)}, u32[]{:S(2)}) collective-permute-start(bf16[128,768]{1,0:T(8,128)(2,1)S(1)} %get-tuple-element.318), channel_id=1, source_target_pairs={{0,24},{8,0},{16,8},{24,16},{1,25},{9,1},{17,9},{25,17},{2,26},{10... | collective-permute-start | bytes 589832 | tf_op jit(solution)/shard_map/ppermute | solution.py:318
  39.4 0.6 pad_add_fusion.place
  40.0 2.4 %collective-permute-done.5 = bf16[128,768]{1,0:T(8,128)(2,1)S(1)} collective-permute-done((bf16[128,768]{1,0:T(8,128)(2,1)S(1)}, bf16[128,768]{1,0:T(8,128)(2,1)S(1)}, u32[]{:S(2)}, u32[]{:S(2)}) %collective-permute-start.5) | collective-permute-done | bytes 196640 | tf_op jit(solution)/shard_map/ppermute | solution.py:318
  42.5 3.2 %collective-permute-done.4 = bf16[128,768]{1,0:T(8,128)(2,1)S(1)} collective-permute-done((bf16[128,768]{1,0:T(8,128)(2,1)S(1)}, bf16[128,768]{1,0:T(8,128)(2,1)S(1)}, u32[]{:S(2)}, u32[]{:S(2)}) %collective-permute-start.4) | collective-permute-done | bytes 196640 | tf_op jit(solution)/shard_map/ppermute | solution.py:318
  45.8 0.6 and_select_fusion.2
  47.2 0.7 and_reduce_fusion
  48.6 3.2 %collective-permute-start.8 = (f32[9216]{0:T(1024)S(1)}, f32[9216]{0:T(1024)S(1)}, u32[]{:S(2)}, u32[]{:S(2)}) collective-permute-start(f32[9216]{0:T(1024)S(1)} %pad_maximum_fusion.20), channel_id=1, source_target_pairs={{0,128},{128,0},{1,129},{129,1},{2,130},{130,2},{3,131},{131,3},{4... | collective-permute-start | bytes 110600 | tf_op jit(solution)/shard_map/ppermute | solution.py:27
  52.5 0.6 broadcast_and_fusion
  53.3 0.7 copy-done.28
  53.9 1.3 fusion.12
  55.3 5.1 %all-to-all-start.1 = ((bf16[8,48,1152]{2,1,0:T(8,128)(2,1)}), bf16[8,48,1152]{2,1,0:T(8,128)(2,1)}, u32[]{:S(2)}, u32[]{:S(2)}) async-start(bf16[8,48,1152]{2,1,0:T(8,128)(2,1)} %bitcast.21), calls=%async_computation.1 | async-start | bytes 1769472 | tf_op jit(solution)/shard_map/all_to_all | solution.py:50
  60.9 2.7 %collective-permute-start.13 = (bf16[512,768]{1,0:T(8,128)(2,1)S(1)}, bf16[512,768]{1,0:T(8,128)(2,1)S(1)}, u32[]{:S(2)}, u32[]{:S(2)}) collective-permute-start(bf16[512,768]{1,0:T(8,128)(2,1)S(1)} %pad_maximum_fusion.1.rest_0_), channel_id=1, source_target_pairs={{0,96},{32,0},{64,32},{96,64},{1,97},{33,1},{65,33},{97,65},{2,98}... | collective-permute-start | bytes 2359304 | tf_op jit(solution)/shard_map/ppermute | solution.py:318
  63.7 2.7 %collective-permute-start.14 = (bf16[512,768]{1,0:T(8,128)(2,1)S(1)}, bf16[512,768]{1,0:T(8,128)(2,1)S(1)}, u32[]{:S(2)}, u32[]{:S(2)}) collective-permute-start(bf16[512,768]{1,0:T(8,128)(2,1)S(1)} %pad_maximum_fusion.2.rest_3_.rest_5_), channel_id=1, source_target_pairs={{0,24},{8,0},{16,8},{24,16},{1,25},{9,1},{17,9},{25,17},{2,26},{10... | collective-permute-start | bytes 2359304 | tf_op jit(solution)/shard_map/ppermute | solution.py:318
  66.4 0.7 and_convert_fusion
  67.2 19.8 %collective-permute-done.13.rest_1_ = bf16[512,768]{1,0:T(8,128)(2,1)S(1)} collective-permute-done((bf16[512,768]{1,0:T(8,128)(2,1)S(1)}, bf16[512,768]{1,0:T(8,128)(2,1)S(1)}, u32[]{:S(2)}, u32[]{:S(2)}) %collective-permute-start.13) | collective-permute-done | bytes 786464 | tf_op jit(solution)/shard_map/ppermute | solution.py:318
  86.9 3.2 %collective-permute-done.11.rest_2_ = bf16[512,768]{1,0:T(8,128)(2,1)S(1)} collective-permute-done((bf16[512,768]{1,0:T(8,128)(2,1)S(1)}, bf16[512,768]{1,0:T(8,128)(2,1)S(1)}, u32[]{:S(2)}, u32[]{:S(2)}) %collective-permute-start.11) | collective-permute-done | bytes 786464 | tf_op jit(solution)/shard_map/ppermute | solution.py:318
  90.4 2.9 %collective-permute-start.18 = (bf16[256,768]{1,0:T(8,128)(2,1)S(1)}, bf16[256,768]{1,0:T(8,128)(2,1)S(1)}, u32[]{:S(2)}, u32[]{:S(2)}) collective-permute-start(bf16[256,768]{1,0:T(8,128)(2,1)S(1)} %slice.253), channel_id=1, source_target_pairs={{0,24},{8,0},{16,8},{24,16},{1,25},{9,1},{17,9},{25,17},{2,26},{10... | collective-permute-start | bytes 1179656 | tf_op jit(solution)/shard_map/ppermute | solution.py:318
  93.3 2.7 %collective-permute-start.16 = (bf16[256,768]{1,0:T(8,128)(2,1)S(1)}, bf16[256,768]{1,0:T(8,128)(2,1)S(1)}, u32[]{:S(2)}, u32[]{:S(2)}) collective-permute-start(bf16[256,768]{1,0:T(8,128)(2,1)S(1)} %slice.251), channel_id=1, source_target_pairs={{0,96},{32,0},{64,32},{96,64},{1,97},{33,1},{65,33},{97,65},{2,98}... | collective-permute-start | bytes 1179656 | tf_op jit(solution)/shard_map/ppermute | solution.py:318
  96.6 0.6 fusion.67
  97.2 2.7 %shard_map.104 = (f32[128,1536]{1,0:T(8,128)S(1)}, bf16[16,128,128]{2,1,0:T(8,128)(2,1)S(1)}) custom-call(s32[2]{0:T(128)S(1)} %copy-done.24, bf16[128,2048]{1,0:T(8,128)(2,1)S(1)} %bitcast.95, f32[1,2048]{1,0:T(1,128)S(1)} %bitcast.97, f32[1,2048]{1,0:T(1,128)S(1)} %bitcast.99, f32[1,1536]{1,0:T(1,128)S(1)} %broadcast_in_dim.160.bias, ...), custom_call_target="tpu_custom_call" | custom-call | flops 196608 | bytes 196608 | tf_op jit(solution)/shard_map/pallas_call | solution.py:242
  100.0 1.0 collective-permute-done.17.rest_2_.rest_8_
  101.0 2.3 %collective-permute-done.15.rest_0_.rest_3_ = bf16[256,768]{1,0:T(8,128)(2,1)S(1)} collective-permute-done((bf16[256,768]{1,0:T(8,128)(2,1)S(1)}, bf16[256,768]{1,0:T(8,128)(2,1)S(1)}, u32[]{:S(2)}, u32[]{:S(2)}) %collective-permute-start.15) | collective-permute-done | bytes 393248 | tf_op jit(solution)/shard_map/ppermute | solution.py:318
  103.3 3.3 %shard_map.105 = bf16[128,512]{1,0:T(8,128)(2,1)} custom-call(s32[2]{0:T(128)S(1)} %copy-done.24, bf16[16,128,128]{2,1,0:T(8,128)(2,1)S(1)} %get-tuple-element.254.normed, f32[128,1536]{1,0:T(8,128)S(1)} %get-tuple-element.255.near, f32[3,128,128]{2,1,0:T(8,128)S(1)} %pad_maximum_fusion.11.turns, f32[128,128]{1,0:T(8,128)S(1)} %get-tuple-element.362.allowed.rest_0_, ...), custom_call_target="tpu_custom_call" | custom-call | flops 196608 | bytes 196608 | tf_op jit(solution)/shard_map/pallas_call | solution.py:242
  106.6 0.7 copy-done.16
  107.3 2.2 %shard_map.106 = (bf16[384,512]{1,0:T(8,128)(2,1)}, f32[1,128]{1,0:T(1,128)}) custom-call(bf16[384,1152]{1,0:T(8,128)(2,1)} %bitcast.22.meta), custom_call_target="tpu_custom_call" | custom-call | flops 16384 | bytes 16384 | tf_op jit(solution)/shard_map/pallas_call | solution.py:461
  110.2 1.9 fusion.18
  112.1 6.6 %all-to-all-start.2 = ((bf16[8,48,512]{2,1,0:T(8,128)(2,1)}), bf16[8,48,512]{2,1,0:T(8,128)(2,1)S(1)}, u32[]{:S(2)}, u32[]{:S(2)}) async-start(bf16[8,48,512]{2,1,0:T(8,128)(2,1)} %bitcast.24), calls=%async_computation.2 | async-start | bytes 786432 | tf_op jit(solution)/shard_map/all_to_all | solution.py:50
  119.9 1.3 slice_select_fusion.1
  121.2 3.1 %collective-permute-start.19 = (bf16[128,512]{1,0:T(8,128)(2,1)}, bf16[128,512]{1,0:T(8,128)(2,1)}, u32[]{:S(2)}, u32[]{:S(2)}) collective-permute-start(bf16[128,512]{1,0:T(8,128)(2,1)} %shard_map.105), channel_id=1, source_target_pairs={{0,128},{128,0},{1,129},{129,1},{2,130},{130,2},{3,131},{131,3},{4... | collective-permute-start | bytes 393224 | tf_op jit(solution)/shard_map/ppermute | solution.py:27
  126.4 0.9 slice.318
  127.3 1.2 slice.317
  128.5 7.3 %all-to-all-done.2 = bf16[8,48,512]{2,1,0:T(8,128)(2,1)S(1)} async-done(((bf16[8,48,512]{2,1,0:T(8,128)(2,1)}), bf16[8,48,512]{2,1,0:T(8,128)(2,1)S(1)}, u32[]{:S(2)}, u32[]{:S(2)}) %all-to-all-start.2) | async-done | bytes 393248 | tf_op jit(solution)/shard_map/all_to_all | solution.py:50
  135.8 2.4 %convolution_convert_fusion.2 = bf16[512,1664]{1,0:T(8,128)(2,1)} fusion(bf16[384,512]{1,0:T(8,128)(2,1)S(1)} %copy-done.60, bf16[384,128]{1,0:T(8,128)(2,1)S(1)} %slice.318, bf16[384,512]{1,0:T(8,128)(2,1)S(1)} %bitcast.121, bf16[384,1024]{1,0:T(8,128)(2,1)S(1)} %slice.317), kind=kOutput, calls=%fused_computation.20 | convolution fusion | flops 658997248 | bytes 3375104 | tf_op jit(solution)/shard_map/dot_general | solution.py:478
  138.2 5.2 %all-to-all-start.3 = ((bf16[16,32,1664]{2,1,0:T(8,128)(2,1)}), bf16[16,32,1664]{2,1,0:T(8,128)(2,1)S(1)}, u32[]{:S(2)}, u32[]{:S(2)}) async-start(bf16[16,32,1664]{2,1,0:T(8,128)(2,1)} %bitcast.116), calls=%async_computation.3 | async-start | bytes 3407872 | tf_op jit(solution)/shard_map/all_to_all | solution.py:50
  143.4 1.7 broadcast_select_fusion.15
  145.1 1.2 slice.319
  146.3 11.0 %all-gather.2.cloned.1.call-done.rest_1_.rest_2_.rest_3_.rest_0_ = bf16[2048,2560]{1,0:T(8,128)(2,1)} async-done(((bf16[16,2560]{1,0:T(8,128)(2,1)}), bf16[2048,2560]{1,0:T(8,128)(2,1)}) %all-gather.2.cloned.1.call-update) | async-done | bytes 10485776 | tf_op jit(solution)/shard_map/all_gather | solution.py:399
  158.7 3.9 %fusion.62 = (bf16[2048,512]{1,0:T(8,128)(2,1)}, bf16[2048,512]{1,0:T(8,128)(2,1)S(1)}) fusion(bf16[2048,2560]{1,0:T(8,128)(2,1)} %all-gather.2.cloned.1.call-done.rest_1_.rest_2_.rest_3_.rest_0_), kind=kLoop, calls=%fused_computation.184 | loop fusion | bytes 8388608 | tf_op jit(solution)/shard_map/slice | solution.py:493
  163.3 0.8 copy-done.9
  164.0 0.8 fusion.27
  165.3 1.3 shard_map.108
  166.9 0.9 convert_reduce_fusion
  167.9 1.0 slice.336
  168.9 4.1 %collective-permute-start.23 = (bf16[128,1536]{1,0:T(8,128)(2,1)S(1)}, bf16[128,1536]{1,0:T(8,128)(2,1)S(1)}, u32[]{:S(2)}, u32[]{:S(2)}) collective-permute-start(bf16[128,1536]{1,0:T(8,128)(2,1)S(1)} %slice.336), channel_id=1, source_target_pairs={{0,128},{128,0},{1,129},{129,1},{2,130},{130,2},{3,131},{131,3},{4... | collective-permute-start | bytes 1179656 | tf_op jit(solution)/shard_map/ppermute | solution.py:27
  173.4 1.1 broadcast_select_fusion.11
  174.6 5.5 %shard_map.107 = bf16[128,512]{1,0:T(8,128)(2,1)S(1)} custom-call(bf16[128,2048]{1,0:T(8,128)(2,1)S(1)} %pad_maximum_fusion.3.layer_in, f32[1,2048]{1,0:T(1,128)S(1)} %bitcast.103, f32[1,2048]{1,0:T(1,128)S(1)} %bitcast.101, f32[1,1536]{1,0:T(1,128)S(1)} %copy-done.22, f32[3,128,128]{2,1,0:T(8,128)S(1)} %pad_maximum_fusion.11.turns, ...), custom_call_target="tpu_custom_call" | custom-call | flops 196608 | bytes 196608 | tf_op jit(solution)/shard_map/pallas_call | solution.py:298
  180.3 1.3 copy-done.31
  182.4 0.9 copy-done.29
  184.1 1.1 fusion.29
  187.3 2.4 %shard_map.109 = bf16[128,1024]{1,0:T(8,128)(2,1)S(1)} custom-call(s32[2]{0:T(128)S(1)} %copy-done.25, bf16[128,2048]{1,0:T(8,128)(2,1)S(1)} %pad_maximum_fusion.4.layer_in, f32[1,2048]{1,0:T(1,128)S(1)} %bitcast.98, f32[1,2048]{1,0:T(1,128)S(1)} %bitcast.100, f32[1,1024]{1,0:T(1,128)S(1)} %copy-done.23, f32[3,128,128]{2,1,0:T(8,128)S(1)} %pad_maximum_fusion.12.turns, ...), custom_call_target="tpu_custom_call" | custom-call | flops 131072 | bytes 131072 | tf_op jit(solution)/shard_map/pallas_call | solution.py:242
  189.7 4.1 %shard_map.110 = bf16[128,1024]{1,0:T(8,128)(2,1)S(1)} custom-call(bf16[128,2048]{1,0:T(8,128)(2,1)S(1)} %pad_maximum_fusion.5.layer_in, f32[1,2048]{1,0:T(1,128)S(1)} %bitcast.104, f32[1,2048]{1,0:T(1,128)S(1)} %bitcast.102, f32[1,1024]{1,0:T(1,128)S(1)} %slice.286.bias, f32[3,128,128]{2,1,0:T(8,128)S(1)} %pad_maximum_fusion.12.turns, ...), custom_call_target="tpu_custom_call" | custom-call | flops 131072 | bytes 131072 | tf_op jit(solution)/shard_map/pallas_call | solution.py:298
  194.4 0.9 maximum_select_fusion
  195.7 0.8 maximum_bitcast_fusion
  (227 shorter events, 13.2 us)
Async XLA Ops:
  7.2 150.1 %all-gather.2.cloned.1.call-start = ((), (), s32[]{:S(2)}) async-start(), calls=%async_computation.4 | async-start | bytes 10567680 | tf_op jit(solution)/shard_map/all_gather | solution.py:399
  8.8 4.2 %collective-permute-start = (bf16[16,2048]{1,0:T(8,128)(2,1)S(1)}, bf16[16,2048]{1,0:T(8,128)(2,1)S(1)}, u32[]{:S(2)}, u32[]{:S(2)}) collective-permute-start(bf16[16,2048]{1,0:T(8,128)(2,1)S(1)} %broadcast_select_fusion.18), channel_id=1, source_target_pairs={{0,128},{128,0},{1,129},{129,1},{2,130},{130,2},{3,131},{131,3},{4... | collective-permute-start | bytes 196616 | tf_op jit(solution)/shard_map/ppermute | solution.py:27
  13.8 46.6 %copy-start.49 = (pred[128]{0:T(512)(128)(4,1)}, pred[128]{0:T(512)(128)(4,1)S(1)}, u32[]{:S(2)}) copy-start(pred[128]{0:T(512)(128)(4,1)S(1)} %iota_compare_fusion.14) | copy-start | bytes 388
  13.8 7.0 %collective-permute-start.1 = (bf16[1,16,1536]{2,1,0:T(8,128)(2,1)S(1)}, bf16[1,16,1536]{2,1,0:T(8,128)(2,1)S(1)}, u32[]{:S(2)}, u32[]{:S(2)}) collective-permute-start(bf16[1,16,1536]{2,1,0:T(8,128)(2,1)S(1)} %slice_bitcast_fusion.10), channel_id=1, source_target_pairs={{0,4},{1,5},{2,6},{3,7},{4,0},{5,1},{6,2},{7,3},{8,12},{9,13},{10,... | collective-permute-start | bytes 147464 | tf_op jit(solution)/shard_map/ppermute | solution.py:344
  19.1 41.3 %copy-start.51 = (f32[128]{0:T(128)}, f32[128]{0:T(128)S(1)}, u32[]{:S(2)}) copy-start(f32[128]{0:T(128)S(1)} %multiply_power_fusion) | copy-start | bytes 1540
  20.9 7.0 %collective-permute-start.2 = (bf16[2,16,1536]{2,1,0:T(8,128)(2,1)S(1)}, bf16[2,16,1536]{2,1,0:T(8,128)(2,1)S(1)}, u32[]{:S(2)}, u32[]{:S(2)}) collective-permute-start(bf16[2,16,1536]{2,1,0:T(8,128)(2,1)S(1)} %maximum_bitcast_fusion.1), channel_id=1, source_target_pairs={{0,2},{1,3},{2,0},{3,1},{4,6},{5,7},{6,4},{7,5},{8,10},{9,11},{10,... | collective-permute-start | bytes 294920 | tf_op jit(solution)/shard_map/ppermute | solution.py:344
  22.1 23.5 %copy-start.47 = (s32[4,32]{1,0:T(4,128)S(1)}, s32[4,32]{1,0:T(4,128)}, u32[]{:S(2)}) copy-start(s32[4,32]{1,0:T(4,128)} %param.15) | copy-start | bytes 1540
  22.1 23.6 %copy-start.59 = (s32[4,32]{1,0:T(4,128)S(1)}, s32[4,32]{1,0:T(4,128)}, u32[]{:S(2)}) copy-start(s32[4,32]{1,0:T(4,128)} %param.14) | copy-start | bytes 1540
  27.9 20.6 %copy-start.37 = (f32[1,3072]{1,0:T(1,128)S(1)}, f32[1,3072]{1,0:T(1,128)}, u32[]{:S(2)}) copy-start(f32[1,3072]{1,0:T(1,128)} %param.19) | copy-start | bytes 36868
  28.0 20.6 %copy-start.40 = (f32[1,2048]{1,0:T(1,128)S(1)}, f32[1,2048]{1,0:T(1,128)}, u32[]{:S(2)}) copy-start(f32[1,2048]{1,0:T(1,128)} %param.21) | copy-start | bytes 24580
  28.0 20.6 %copy-start.41 = (f32[1,2048]{1,0:T(1,128)S(1)}, f32[1,2048]{1,0:T(1,128)}, u32[]{:S(2)}) copy-start(f32[1,2048]{1,0:T(1,128)} %param.17) | copy-start | bytes 24580
  28.0 20.6 %copy-start.42 = (f32[1,2048]{1,0:T(1,128)S(1)}, f32[1,2048]{1,0:T(1,128)}, u32[]{:S(2)}) copy-start(f32[1,2048]{1,0:T(1,128)} %param.16) | copy-start | bytes 24580
  28.0 25.2 %copy-start.8 = (bf16[4,32,2048]{2,1,0:T(8,128)(2,1)S(1)}, bf16[4,32,2048]{2,1,0:T(8,128)(2,1)}, u32[]{:S(2)}) copy-start(bf16[4,32,2048]{2,1,0:T(8,128)(2,1)} %param.13) | copy-start | bytes 1572868
  28.1 5.9 %collective-permute-start.3 = (bf16[4,16,1536]{2,1,0:T(8,128)(2,1)S(1)}, bf16[4,16,1536]{2,1,0:T(8,128)(2,1)S(1)}, u32[]{:S(2)}, u32[]{:S(2)}) collective-permute-start(bf16[4,16,1536]{2,1,0:T(8,128)(2,1)S(1)} %bitcast.120), channel_id=1, source_target_pairs={{0,1},{1,0},{2,3},{3,2},{4,5},{5,4},{6,7},{7,6},{8,9},{9,8},{10,11... | collective-permute-start | bytes 589832 | tf_op jit(solution)/shard_map/ppermute | solution.py:344
  34.1 5.9 %collective-permute-start.7 = (bf16[128,768]{1,0:T(8,128)(2,1)S(1)}, bf16[128,768]{1,0:T(8,128)(2,1)S(1)}, u32[]{:S(2)}, u32[]{:S(2)}) collective-permute-start(bf16[128,768]{1,0:T(8,128)(2,1)S(1)} %get-tuple-element.317), channel_id=1, source_target_pairs={{0,96},{32,0},{64,32},{96,64},{1,97},{33,1},{65,33},{97,65},{2,98}... | collective-permute-start | bytes 589832 | tf_op jit(solution)/shard_map/ppermute | solution.py:318
  36.7 5.8 %collective-permute-start.5 = (bf16[128,768]{1,0:T(8,128)(2,1)S(1)}, bf16[128,768]{1,0:T(8,128)(2,1)S(1)}, u32[]{:S(2)}, u32[]{:S(2)}) collective-permute-start(bf16[128,768]{1,0:T(8,128)(2,1)S(1)} %get-tuple-element.317), channel_id=1, source_target_pairs={{0,32},{32,64},{64,96},{96,0},{1,33},{33,65},{65,97},{97,1},{2,34}... | collective-permute-start | bytes 589832 | tf_op jit(solution)/shard_map/ppermute | solution.py:318
  36.7 5.8 %collective-permute-start.6 = (bf16[128,768]{1,0:T(8,128)(2,1)S(1)}, bf16[128,768]{1,0:T(8,128)(2,1)S(1)}, u32[]{:S(2)}, u32[]{:S(2)}) collective-permute-start(bf16[128,768]{1,0:T(8,128)(2,1)S(1)} %get-tuple-element.318), channel_id=1, source_target_pairs={{0,24},{8,0},{16,8},{24,16},{1,25},{9,1},{17,9},{25,17},{2,26},{10... | collective-permute-start | bytes 589832 | tf_op jit(solution)/shard_map/ppermute | solution.py:318
  39.4 6.3 %collective-permute-start.4 = (bf16[128,768]{1,0:T(8,128)(2,1)S(1)}, bf16[128,768]{1,0:T(8,128)(2,1)S(1)}, u32[]{:S(2)}, u32[]{:S(2)}) collective-permute-start(bf16[128,768]{1,0:T(8,128)(2,1)S(1)} %get-tuple-element.318), channel_id=1, source_target_pairs={{0,8},{8,16},{16,24},{24,0},{1,9},{9,17},{17,25},{25,1},{2,10},{10... | collective-permute-start | bytes 589832 | tf_op jit(solution)/shard_map/ppermute | solution.py:318
  40.0 20.8 %copy-start.53 = (pred[128]{0:T(512)(128)(4,1)}, pred[128]{0:T(512)(128)(4,1)S(1)}, u32[]{:S(2)}) copy-start(pred[128]{0:T(512)(128)(4,1)S(1)} %get-tuple-element.379) | copy-start | bytes 388
  40.0 20.8 %copy-start.55 = (pred[128]{0:T(512)(128)(4,1)}, pred[128]{0:T(512)(128)(4,1)S(1)}, u32[]{:S(2)}) copy-start(pred[128]{0:T(512)(128)(4,1)S(1)} %get-tuple-element.380) | copy-start | bytes 388
  45.8 15.1 %copy-start.48 = (s32[128]{0:T(128)}, s32[128]{0:T(128)S(1)}, u32[]{:S(2)}) copy-start(s32[128]{0:T(128)S(1)} %reshape.831) | copy-start | bytes 1540
  48.6 18.5 %collective-permute-start.8 = (f32[9216]{0:T(1024)S(1)}, f32[9216]{0:T(1024)S(1)}, u32[]{:S(2)}, u32[]{:S(2)}) collective-permute-start(f32[9216]{0:T(1024)S(1)} %pad_maximum_fusion.20), channel_id=1, source_target_pairs={{0,128},{128,0},{1,129},{129,1},{2,130},{130,2},{3,131},{131,3},{4... | collective-permute-start | bytes 110600 | tf_op jit(solution)/shard_map/ppermute | solution.py:27
  51.9 8.9 %collective-permute-start.9 = (bf16[128,768]{1,0:T(8,128)(2,1)S(1)}, bf16[128,768]{1,0:T(8,128)(2,1)S(1)}, u32[]{:S(2)}, u32[]{:S(2)}) collective-permute-start(bf16[128,768]{1,0:T(8,128)(2,1)S(1)} %collective-permute-done.4), channel_id=1, source_target_pairs={{0,8},{8,16},{16,24},{24,0},{1,9},{9,17},{17,25},{25,1},{2,10},{10... | collective-permute-start | bytes 589832 | tf_op jit(solution)/shard_map/ppermute | solution.py:318
  51.9 9.0 %collective-permute-start.10 = (bf16[128,768]{1,0:T(8,128)(2,1)S(1)}, bf16[128,768]{1,0:T(8,128)(2,1)S(1)}, u32[]{:S(2)}, u32[]{:S(2)}) collective-permute-start(bf16[128,768]{1,0:T(8,128)(2,1)S(1)} %collective-permute-done.5), channel_id=1, source_target_pairs={{0,32},{32,64},{64,96},{96,0},{1,33},{33,65},{65,97},{97,1},{2,34}... | collective-permute-start | bytes 589832 | tf_op jit(solution)/shard_map/ppermute | solution.py:318
  53.1 7.8 %copy-start.57 = (s32[128]{0:T(128)}, s32[128]{0:T(128)S(1)}, u32[]{:S(2)}) copy-start(s32[128]{0:T(128)S(1)} %get-tuple-element.366) | copy-start | bytes 1540
  53.2 7.6 %copy-start.32 = (bf16[128,128]{1,0:T(8,128)(2,1)}, bf16[128,128]{1,0:T(8,128)(2,1)S(1)}, u32[]{:S(2)}) copy-start(bf16[128,128]{1,0:T(8,128)(2,1)S(1)} %select_convert_fusion) | copy-start | bytes 98308
  55.3 52.1 %all-to-all-start.1 = ((bf16[8,48,1152]{2,1,0:T(8,128)(2,1)}), bf16[8,48,1152]{2,1,0:T(8,128)(2,1)}, u32[]{:S(2)}, u32[]{:S(2)}) async-start(bf16[8,48,1152]{2,1,0:T(8,128)(2,1)} %bitcast.21), calls=%async_computation.1 | async-start | bytes 1769472 | tf_op jit(solution)/shard_map/all_to_all | solution.py:50
  60.9 36.3 %copy-start.24 = (s32[2]{0:T(128)S(1)}, s32[2]{0:T(128)}, u32[]{:S(2)}) copy-start(s32[2]{0:T(128)} %pad_add_fusion.place) | copy-start | bytes 28
  60.9 26.0 %collective-permute-start.13 = (bf16[512,768]{1,0:T(8,128)(2,1)S(1)}, bf16[512,768]{1,0:T(8,128)(2,1)S(1)}, u32[]{:S(2)}, u32[]{:S(2)}) collective-permute-start(bf16[512,768]{1,0:T(8,128)(2,1)S(1)} %pad_maximum_fusion.1.rest_0_), channel_id=1, source_target_pairs={{0,96},{32,0},{64,32},{96,64},{1,97},{33,1},{65,33},{97,65},{2,98}... | collective-permute-start | bytes 2359304 | tf_op jit(solution)/shard_map/ppermute | solution.py:318
  63.7 26.5 %collective-permute-start.11 = (bf16[512,768]{1,0:T(8,128)(2,1)S(1)}, bf16[512,768]{1,0:T(8,128)(2,1)S(1)}, u32[]{:S(2)}, u32[]{:S(2)}) collective-permute-start(bf16[512,768]{1,0:T(8,128)(2,1)S(1)} %pad_maximum_fusion.1.rest_0_), channel_id=1, source_target_pairs={{0,32},{32,64},{64,96},{96,0},{1,33},{33,65},{65,97},{97,1},{2,34}... | collective-permute-start | bytes 2359304 | tf_op jit(solution)/shard_map/ppermute | solution.py:318
  63.7 26.5 %collective-permute-start.14 = (bf16[512,768]{1,0:T(8,128)(2,1)S(1)}, bf16[512,768]{1,0:T(8,128)(2,1)S(1)}, u32[]{:S(2)}, u32[]{:S(2)}) collective-permute-start(bf16[512,768]{1,0:T(8,128)(2,1)S(1)} %pad_maximum_fusion.2.rest_3_.rest_5_), channel_id=1, source_target_pairs={{0,24},{8,0},{16,8},{24,16},{1,25},{9,1},{17,9},{25,17},{2,26},{10... | collective-permute-start | bytes 2359304 | tf_op jit(solution)/shard_map/ppermute | solution.py:318
  66.4 23.8 %collective-permute-start.12 = (bf16[512,768]{1,0:T(8,128)(2,1)S(1)}, bf16[512,768]{1,0:T(8,128)(2,1)S(1)}, u32[]{:S(2)}, u32[]{:S(2)}) collective-permute-start(bf16[512,768]{1,0:T(8,128)(2,1)S(1)} %pad_maximum_fusion.2.rest_3_.rest_5_), channel_id=1, source_target_pairs={{0,8},{8,16},{16,24},{24,0},{1,9},{9,17},{17,25},{25,1},{2,10},{10... | collective-permute-start | bytes 2359304 | tf_op jit(solution)/shard_map/ppermute | solution.py:318
  67.1 30.1 %copy-start.33 = (f32[9216]{0:T(1024)}, f32[9216]{0:T(1024)S(1)}, u32[]{:S(2)}) copy-start(f32[9216]{0:T(1024)S(1)} %get-tuple-element.339) | copy-start | bytes 110596
  67.2 30.1 %copy-start.34 = (f32[9216]{0:T(1024)}, f32[9216]{0:T(1024)S(1)}, u32[]{:S(2)}) copy-start(f32[9216]{0:T(1024)S(1)} %get-tuple-element.340) | copy-start | bytes 110596
  86.9 13.0 %copy-start = (bf16[512,768]{1,0:T(8,128)(2,1)}, bf16[512,768]{1,0:T(8,128)(2,1)S(1)}, u32[]{:S(2)}) copy-start(bf16[512,768]{1,0:T(8,128)(2,1)S(1)} %collective-permute-done.13.rest_1_) | copy-start | bytes 2359300
  90.1 9.8 %copy-start.2 = (bf16[512,768]{1,0:T(8,128)(2,1)}, bf16[512,768]{1,0:T(8,128)(2,1)S(1)}, u32[]{:S(2)}) copy-start(bf16[512,768]{1,0:T(8,128)(2,1)S(1)} %collective-permute-done.11.rest_2_) | copy-start | bytes 2359300
  90.1 9.8 %copy-start.4 = (bf16[512,768]{1,0:T(8,128)(2,1)}, bf16[512,768]{1,0:T(8,128)(2,1)S(1)}, u32[]{:S(2)}) copy-start(bf16[512,768]{1,0:T(8,128)(2,1)S(1)} %collective-permute-done.14.rest_4_.rest_6_) | copy-start | bytes 2359300
  90.2 9.8 %copy-start.6 = (bf16[512,768]{1,0:T(8,128)(2,1)}, bf16[512,768]{1,0:T(8,128)(2,1)S(1)}, u32[]{:S(2)}) copy-start(bf16[512,768]{1,0:T(8,128)(2,1)S(1)} %collective-permute-done.12.rest_5_.rest_7_) | copy-start | bytes 2359300
  90.3 10.7 %collective-permute-start.17 = (bf16[256,768]{1,0:T(8,128)(2,1)S(1)}, bf16[256,768]{1,0:T(8,128)(2,1)S(1)}, u32[]{:S(2)}, u32[]{:S(2)}) collective-permute-start(bf16[256,768]{1,0:T(8,128)(2,1)S(1)} %slice.252), channel_id=1, source_target_pairs={{0,8},{8,16},{16,24},{24,0},{1,9},{9,17},{17,25},{25,1},{2,10},{10... | collective-permute-start | bytes 1179656 | tf_op jit(solution)/shard_map/ppermute | solution.py:318
  90.4 10.6 %collective-permute-start.18 = (bf16[256,768]{1,0:T(8,128)(2,1)S(1)}, bf16[256,768]{1,0:T(8,128)(2,1)S(1)}, u32[]{:S(2)}, u32[]{:S(2)}) collective-permute-start(bf16[256,768]{1,0:T(8,128)(2,1)S(1)} %slice.253), channel_id=1, source_target_pairs={{0,24},{8,0},{16,8},{24,16},{1,25},{9,1},{17,9},{25,17},{2,26},{10... | collective-permute-start | bytes 1179656 | tf_op jit(solution)/shard_map/ppermute | solution.py:318
  93.3 10.0 %collective-permute-start.15 = (bf16[256,768]{1,0:T(8,128)(2,1)S(1)}, bf16[256,768]{1,0:T(8,128)(2,1)S(1)}, u32[]{:S(2)}, u32[]{:S(2)}) collective-permute-start(bf16[256,768]{1,0:T(8,128)(2,1)S(1)} %slice.250), channel_id=1, source_target_pairs={{0,32},{32,64},{64,96},{96,0},{1,33},{33,65},{65,97},{97,1},{2,34}... | collective-permute-start | bytes 1179656 | tf_op jit(solution)/shard_map/ppermute | solution.py:318
  93.3 10.0 %collective-permute-start.16 = (bf16[256,768]{1,0:T(8,128)(2,1)S(1)}, bf16[256,768]{1,0:T(8,128)(2,1)S(1)}, u32[]{:S(2)}, u32[]{:S(2)}) collective-permute-start(bf16[256,768]{1,0:T(8,128)(2,1)S(1)} %slice.251), channel_id=1, source_target_pairs={{0,96},{32,0},{64,32},{96,64},{1,97},{33,1},{65,33},{97,65},{2,98}... | collective-permute-start | bytes 1179656 | tf_op jit(solution)/shard_map/ppermute | solution.py:318
  100.0 10.2 %copy-start.58 = (s32[128]{0:T(128)S(1)}, s32[128]{0:T(128)}, u32[]{:S(2)}) copy-start(s32[128]{0:T(128)} %copy-done.57) | copy-start | bytes 1540
  101.0 11.1 %copy-start.10 = (bf16[256,768]{1,0:T(8,128)(2,1)}, bf16[256,768]{1,0:T(8,128)(2,1)S(1)}, u32[]{:S(2)}) copy-start(bf16[256,768]{1,0:T(8,128)(2,1)S(1)} %collective-permute-done.17.rest_2_.rest_8_) | copy-start | bytes 1179652
  101.0 11.1 %copy-start.12 = (bf16[256,768]{1,0:T(8,128)(2,1)}, bf16[256,768]{1,0:T(8,128)(2,1)S(1)}, u32[]{:S(2)}) copy-start(bf16[256,768]{1,0:T(8,128)(2,1)S(1)} %collective-permute-done.18.rest_3_.rest_9_) | copy-start | bytes 1179652
  103.3 8.8 %copy-start.14 = (bf16[256,768]{1,0:T(8,128)(2,1)}, bf16[256,768]{1,0:T(8,128)(2,1)S(1)}, u32[]{:S(2)}) copy-start(bf16[256,768]{1,0:T(8,128)(2,1)S(1)} %collective-permute-done.15.rest_0_.rest_3_) | copy-start | bytes 1179652
  103.3 15.4 %copy-start.21 = (f32[1,1536]{1,0:T(1,128)S(1)}, f32[1,1536]{1,0:T(1,128)}, u32[]{:S(2)}) copy-start(f32[1,1536]{1,0:T(1,128)} %copy-done.20) | copy-start | bytes 18436
  103.3 16.0 %copy-start.44 = (f32[512]{0:T(512)S(1)}, f32[512]{0:T(512)}, u32[]{:S(2)}) copy-start(f32[512]{0:T(512)} %get-tuple-element.341) | copy-start | bytes 6148
  103.3 16.0 %copy-start.45 = (f32[512]{0:T(512)S(1)}, f32[512]{0:T(512)}, u32[]{:S(2)}) copy-start(f32[512]{0:T(512)} %get-tuple-element.342) | copy-start | bytes 6148
  103.3 16.0 %copy-start.46 = (f32[512]{0:T(512)S(1)}, f32[512]{0:T(512)}, u32[]{:S(2)}) copy-start(f32[512]{0:T(512)} %get-tuple-element.343) | copy-start | bytes 6148
  112.1 23.8 %copy-start.60 = (bf16[384,512]{1,0:T(8,128)(2,1)S(1)}, bf16[384,512]{1,0:T(8,128)(2,1)}, u32[]{:S(2)}) copy-start(bf16[384,512]{1,0:T(8,128)(2,1)} %get-tuple-element.258) | copy-start | bytes 1179652
  112.1 23.7 %all-to-all-start.2 = ((bf16[8,48,512]{2,1,0:T(8,128)(2,1)}), bf16[8,48,512]{2,1,0:T(8,128)(2,1)S(1)}, u32[]{:S(2)}, u32[]{:S(2)}) async-start(bf16[8,48,512]{2,1,0:T(8,128)(2,1)} %bitcast.24), calls=%async_computation.2 | async-start | bytes 786432 | tf_op jit(solution)/shard_map/all_to_all | solution.py:50
  121.2 22.2 %collective-permute-start.19 = (bf16[128,512]{1,0:T(8,128)(2,1)}, bf16[128,512]{1,0:T(8,128)(2,1)}, u32[]{:S(2)}, u32[]{:S(2)}) collective-permute-start(bf16[128,512]{1,0:T(8,128)(2,1)} %shard_map.105), channel_id=1, source_target_pairs={{0,128},{128,0},{1,129},{129,1},{2,130},{130,2},{3,131},{131,3},{4... | collective-permute-start | bytes 393224 | tf_op jit(solution)/shard_map/ppermute | solution.py:27
  138.2 27.1 %all-to-all-start.3 = ((bf16[16,32,1664]{2,1,0:T(8,128)(2,1)}), bf16[16,32,1664]{2,1,0:T(8,128)(2,1)S(1)}, u32[]{:S(2)}, u32[]{:S(2)}) async-start(bf16[16,32,1664]{2,1,0:T(8,128)(2,1)} %bitcast.116), calls=%async_computation.3 | async-start | bytes 3407872 | tf_op jit(solution)/shard_map/all_to_all | solution.py:50
  164.8 8.6 %collective-permute-start.20 = (bf16[128,1024]{1,0:T(8,128)(2,1)}, bf16[128,1024]{1,0:T(8,128)(2,1)}, u32[]{:S(2)}, u32[]{:S(2)}) collective-permute-start(bf16[128,1024]{1,0:T(8,128)(2,1)} %fusion.27), channel_id=1, source_target_pairs={{0,128},{128,0},{1,129},{129,1},{2,130},{130,2},{3,131},{131,3},{4... | collective-permute-start | bytes 786440 | tf_op jit(solution)/shard_map/ppermute | solution.py:27
  166.6 6.4 %copy-start.50 = (pred[128]{0:T(512)(128)(4,1)S(1)}, pred[128]{0:T(512)(128)(4,1)}, u32[]{:S(2)}) copy-start(pred[128]{0:T(512)(128)(4,1)} %copy-done.49) | copy-start | bytes 388
  166.6 6.4 %copy-start.52 = (f32[128]{0:T(128)S(1)}, f32[128]{0:T(128)}, u32[]{:S(2)}) copy-start(f32[128]{0:T(128)} %copy-done.51) | copy-start | bytes 1540
  166.9 7.6 %copy-start.18 = (f32[2048]{0:T(1024)S(1)}, f32[2048]{0:T(1024)}, u32[]{:S(2)}) copy-start(f32[2048]{0:T(1024)} %get-tuple-element.344) | copy-start | bytes 24580
  166.9 7.6 %copy-start.19 = (f32[2048]{0:T(1024)S(1)}, f32[2048]{0:T(1024)}, u32[]{:S(2)}) copy-start(f32[2048]{0:T(1024)} %get-tuple-element.345) | copy-start | bytes 24580
  168.9 11.3 %collective-permute-start.23 = (bf16[128,1536]{1,0:T(8,128)(2,1)S(1)}, bf16[128,1536]{1,0:T(8,128)(2,1)S(1)}, u32[]{:S(2)}, u32[]{:S(2)}) collective-permute-start(bf16[128,1536]{1,0:T(8,128)(2,1)S(1)} %slice.336), channel_id=1, source_target_pairs={{0,128},{128,0},{1,129},{129,1},{2,130},{130,2},{3,131},{131,3},{4... | collective-permute-start | bytes 1179656 | tf_op jit(solution)/shard_map/ppermute | solution.py:27
  180.1 2.2 %collective-permute-start.21 = (bf16[128,512]{1,0:T(8,128)(2,1)S(1)}, bf16[128,512]{1,0:T(8,128)(2,1)S(1)}, u32[]{:S(2)}, u32[]{:S(2)}) collective-permute-start(bf16[128,512]{1,0:T(8,128)(2,1)S(1)} %shard_map.107), channel_id=1, source_target_pairs={{0,128},{128,0},{1,129},{129,1},{2,130},{130,2},{3,131},{131,3},{4... | collective-permute-start | bytes 393224 | tf_op jit(solution)/shard_map/ppermute | solution.py:27
  184.0 2.0 collective-permute-start.24
  185.4 9.0 %collective-permute-start.22 = (bf16[128,1024]{1,0:T(8,128)(2,1)S(1)}, bf16[128,1024]{1,0:T(8,128)(2,1)S(1)}, u32[]{:S(2)}, u32[]{:S(2)}) collective-permute-start(bf16[128,1024]{1,0:T(8,128)(2,1)S(1)} %fusion.29), channel_id=1, source_target_pairs={{0,128},{128,0},{1,129},{129,1},{2,130},{130,2},{3,131},{131,3},{4... | collective-permute-start | bytes 786440 | tf_op jit(solution)/shard_map/ppermute | solution.py:27
  193.8 1.7 collective-permute-start.25
  (26 other events, 62.0 us)
Sparse Core Ops, SparseCore 0:
  13.9 143.3 all-gather.1

commit v3 on v2

--- a/solution.py
+++ b/solution.py
@@ -207,7 +207,7 @@
         conclude(total[...], turns, allowed, out_ref)
 
 
-def slots_kernel(cap, meta, choice, flag):
+def slots_kernel(cap, meta, send, context, choice, filled, flag):
     info = meta[...].astype(F32)
     lane = lax.broadcasted_iota(jnp.int32, info.shape, 1)
 
@@ -226,7 +226,9 @@
     place = lax.broadcasted_iota(jnp.int32, choice.shape, 1).astype(F32)
     choice[...] = jnp.where(place == slot, 1.0, 0.0).astype(BF)
     over = jnp.where(rank < cap, 0.0, 1.0) * valid + column(3)
-    flag[...] = jnp.broadcast_to(jnp.sum(over, axis=0, keepdims=True), flag.shape)
+    total = jnp.sum(over, axis=0, keepdims=True)
+    flag[...] = jnp.broadcast_to(total, flag.shape)
+    filled[...] = (mm(send[...], context[...]) + jnp.where(total > 0.0, jnp.nan, 0.0)).astype(BF)
 
 
 def cost(rows, width, cols):
@@ -458,21 +460,20 @@
     turns = turns_of(positions.astype(F32))
     middle = across(filled, "z", CAP_Z)
     slots_p = device_count // depth * CAP_P
-    send_p, flags = pl.pallas_call(
+    context0 = context_by_pieces(place, flat, rows0, turns, allowed, pieces)
+    whole = [(middle.shape[0], slots_p), (middle.shape[0], context0.shape[1]), (1, LANES)]
+    send_p, filled, _ = pl.pallas_call(
         functools.partial(slots_kernel, CAP_P),
         grid=(1,),
-        out_shape=(of((middle.shape[0], slots_p), BF), of((1, LANES), F32)),
-        in_specs=[pl.BlockSpec((middle.shape[0], META), lambda k: (0, half_width // META))],
-        out_specs=(
-            pl.BlockSpec((middle.shape[0], slots_p), lambda k: (0, 0)),
-            pl.BlockSpec((1, LANES), lambda k: (0, 0)),
-        ),
+        out_shape=(of(whole[0], BF), of(whole[1], BF), of(whole[2], F32)),
+        in_specs=[
+            pl.BlockSpec((middle.shape[0], META), lambda k: (0, half_width // META)),
+            pl.BlockSpec(send_z.shape, lambda k: (0, 0)),
+            pl.BlockSpec(context0.shape, lambda k: (0, 0)),
+        ],
+        out_specs=tuple(pl.BlockSpec(one, lambda k: (0, 0)) for one in whole),
         cost_estimate=cost(128, 128, 128),
-    )(middle)
-    ran_out = flags[0, 0] > 0
-
-    context0 = context_by_pieces(place, flat, rows0, turns, allowed, pieces)
-    filled = jnp.where(ran_out, jnp.nan, mm(send_z, context0)).astype(BF)
+    )(middle, send_z, context0)
     middle0 = across(filled, "z", CAP_Z)
     leg = jnp.concatenate([middle[:, :half_width], middle0, middle[:, half_width:]], axis=1)
     leg = lax.dot_general(

time: 204 us -> 203 us (level)
    dot_general x9 -> x8, matrix products: 5.19 us -> 3.29 us  [mm(): return jnp.dot(a, b, preferred_element_type=F32)]
    unnamed x120 -> x116, local copies, waits for them, and re-layouts: 5.9 us -> 5.9 us
where the time goes in v3:
time: 203 us; the launch traced here: 202 us
  waiting for transfers between devices  66.1 us (33%)
  starting transfers between devices  55.4 us (27%)
  Pallas kernels  21.7 us (11%)
  local copies, waits for them, and re-layouts  20.2 us (10%)
  between operations  17 us (8%)
  other arithmetic  16.3 us (8%)
  matrix products  5.63 us (3%)
    ppermute x14, waiting for transfers between devices, shifted(): lax.ppermute(value, axis, [(one, (one + by) % size) for one in range(size)])  33.1 us
    ppermute x14, starting transfers between devices, shifted(): lax.ppermute(value, axis, [(one, (one + by) % size) for one in range(size)])  16.8 us
    all_to_all x3, starting transfers between devices, across(): lax.all_to_all(filled.reshape(-1, cap, cols), axes, split_axis=0, concat_...  16.3 us
    ppermute x9, starting transfers between devices, swap(): return lax.ppermute(value, 'pipe', [(0, 1), (1, 0)])  15.6 us
    ppermute x3, waiting for transfers between devices, column_of(): got = lax.ppermute(block, 'z', [(one, one ^ step) for one in range(size)])  13.3 us
    all_gather x1, waiting for transfers between devices, shards(): gathered = lax.all_gather(bulk, DP, axis=0, tiled=True)  10.5 us
    pallas_call x4, Pallas kernels, call(): pl.pallas_call(kernel, out_shape=out_shape, in_specs=in_specs, out_specs=...  9.65 us
    pallas_call x2, Pallas kernels, project_whole(): pl.pallas_call(functools.partial(whole_kernel, with_context), grid=(width...  9.58 us
  transfers between devices with their start and end apart: 30, of which 13 were waited for; matrix products, arithmetic and copies ran while one was open for 16% of the time, Pallas kernels for 11%

profile of v3, /device:TPU:1, one launch (start us, length us, event | category | flops | bytes accessed | tf_op | source)
XLA Modules:
  0.0 202.5 jit_solution(10787043327734708545)
XLA Ops:
  7.2 0.8 fusion.68
  8.0 0.8 fusion.65
  8.8 3.3 %collective-permute-start = (bf16[16,2048]{1,0:T(8,128)(2,1)S(1)}, bf16[16,2048]{1,0:T(8,128)(2,1)S(1)}, u32[]{:S(2)}, u32[]{:S(2)}) collective-permute-start(bf16[16,2048]{1,0:T(8,128)(2,1)S(1)} %broadcast_select_fusion.18), channel_id=1, source_target_pairs={{0,128},{128,0},{1,129},{129,1},{2,130},{130,2},{3,131},{131,3},{4... | collective-permute-start | bytes 196616 | tf_op jit(solution)/shard_map/ppermute | solution.py:27
  12.1 0.9 collective-permute-done
  13.1 0.6 pad_maximum_fusion.19
  13.8 5.3 %collective-permute-start.1 = (bf16[1,16,1536]{2,1,0:T(8,128)(2,1)S(1)}, bf16[1,16,1536]{2,1,0:T(8,128)(2,1)S(1)}, u32[]{:S(2)}, u32[]{:S(2)}) collective-permute-start(bf16[1,16,1536]{2,1,0:T(8,128)(2,1)S(1)} %slice_bitcast_fusion.10), channel_id=1, source_target_pairs={{0,4},{1,5},{2,6},{3,7},{4,0},{5,1},{6,2},{7,3},{8,12},{9,13},{10,... | collective-permute-start | bytes 147464 | tf_op jit(solution)/shard_map/ppermute | solution.py:346
  19.1 1.8 collective-permute-done.1
  20.9 1.2 collective-permute-start.2
  22.1 5.8 %collective-permute-done.2 = bf16[2,16,1536]{2,1,0:T(8,128)(2,1)S(1)} collective-permute-done((bf16[2,16,1536]{2,1,0:T(8,128)(2,1)S(1)}, bf16[2,16,1536]{2,1,0:T(8,128)(2,1)S(1)}, u32[]{:S(2)}, u32[]{:S(2)}) %collective-permute-start.2) | collective-permute-done | bytes 98336 | tf_op jit(solution)/shard_map/ppermute | solution.py:346
  28.2 5.8 %collective-permute-done.3 = bf16[4,16,1536]{2,1,0:T(8,128)(2,1)S(1)} collective-permute-done((bf16[4,16,1536]{2,1,0:T(8,128)(2,1)S(1)}, bf16[4,16,1536]{2,1,0:T(8,128)(2,1)S(1)}, u32[]{:S(2)}, u32[]{:S(2)}) %collective-permute-start.3) | collective-permute-done | bytes 196640 | tf_op jit(solution)/shard_map/ppermute | solution.py:346
  34.1 2.6 %collective-permute-start.7 = (bf16[128,768]{1,0:T(8,128)(2,1)S(1)}, bf16[128,768]{1,0:T(8,128)(2,1)S(1)}, u32[]{:S(2)}, u32[]{:S(2)}) collective-permute-start(bf16[128,768]{1,0:T(8,128)(2,1)S(1)} %get-tuple-element.317), channel_id=1, source_target_pairs={{0,96},{32,0},{64,32},{96,64},{1,97},{33,1},{65,33},{97,65},{2,98}... | collective-permute-start | bytes 589832 | tf_op jit(solution)/shard_map/ppermute | solution.py:320
  36.7 2.7 %collective-permute-start.6 = (bf16[128,768]{1,0:T(8,128)(2,1)S(1)}, bf16[128,768]{1,0:T(8,128)(2,1)S(1)}, u32[]{:S(2)}, u32[]{:S(2)}) collective-permute-start(bf16[128,768]{1,0:T(8,128)(2,1)S(1)} %get-tuple-element.318), channel_id=1, source_target_pairs={{0,24},{8,0},{16,8},{24,16},{1,25},{9,1},{17,9},{25,17},{2,26},{10... | collective-permute-start | bytes 589832 | tf_op jit(solution)/shard_map/ppermute | solution.py:320
  39.4 0.7 pad_add_fusion.place
  40.1 2.4 %collective-permute-done.5 = bf16[128,768]{1,0:T(8,128)(2,1)S(1)} collective-permute-done((bf16[128,768]{1,0:T(8,128)(2,1)S(1)}, bf16[128,768]{1,0:T(8,128)(2,1)S(1)}, u32[]{:S(2)}, u32[]{:S(2)}) %collective-permute-start.5) | collective-permute-done | bytes 196640 | tf_op jit(solution)/shard_map/ppermute | solution.py:320
  42.5 3.2 %collective-permute-done.4 = bf16[128,768]{1,0:T(8,128)(2,1)S(1)} collective-permute-done((bf16[128,768]{1,0:T(8,128)(2,1)S(1)}, bf16[128,768]{1,0:T(8,128)(2,1)S(1)}, u32[]{:S(2)}, u32[]{:S(2)}) %collective-permute-start.4) | collective-permute-done | bytes 196640 | tf_op jit(solution)/shard_map/ppermute | solution.py:320
  47.3 0.7 and_reduce_fusion
  48.6 3.2 %collective-permute-start.8 = (f32[9216]{0:T(1024)S(1)}, f32[9216]{0:T(1024)S(1)}, u32[]{:S(2)}, u32[]{:S(2)}) collective-permute-start(f32[9216]{0:T(1024)S(1)} %pad_maximum_fusion.20), channel_id=1, source_target_pairs={{0,128},{128,0},{1,129},{129,1},{2,130},{130,2},{3,131},{131,3},{4... | collective-permute-start | bytes 110600 | tf_op jit(solution)/shard_map/ppermute | solution.py:27
  53.3 0.7 copy-done.28
  54.0 1.3 fusion.12
  55.3 5.1 %all-to-all-start.1 = ((bf16[8,48,1152]{2,1,0:T(8,128)(2,1)}), bf16[8,48,1152]{2,1,0:T(8,128)(2,1)}, u32[]{:S(2)}, u32[]{:S(2)}) async-start(bf16[8,48,1152]{2,1,0:T(8,128)(2,1)} %bitcast.21), calls=%async_computation.1 | async-start | bytes 1769472 | tf_op jit(solution)/shard_map/all_to_all | solution.py:50
  60.8 0.7 and_convert_fusion
  61.7 2.7 %collective-permute-start.13 = (bf16[512,768]{1,0:T(8,128)(2,1)S(1)}, bf16[512,768]{1,0:T(8,128)(2,1)S(1)}, u32[]{:S(2)}, u32[]{:S(2)}) collective-permute-start(bf16[512,768]{1,0:T(8,128)(2,1)S(1)} %pad_maximum_fusion.1.rest_0_), channel_id=1, source_target_pairs={{0,96},{32,0},{64,32},{96,64},{1,97},{33,1},{65,33},{97,65},{2,98}... | collective-permute-start | bytes 2359304 | tf_op jit(solution)/shard_map/ppermute | solution.py:320
  64.4 2.7 %collective-permute-start.14 = (bf16[512,768]{1,0:T(8,128)(2,1)S(1)}, bf16[512,768]{1,0:T(8,128)(2,1)S(1)}, u32[]{:S(2)}, u32[]{:S(2)}) collective-permute-start(bf16[512,768]{1,0:T(8,128)(2,1)S(1)} %pad_maximum_fusion.2.rest_3_.rest_5_), channel_id=1, source_target_pairs={{0,24},{8,0},{16,8},{24,16},{1,25},{9,1},{17,9},{25,17},{2,26},{10... | collective-permute-start | bytes 2359304 | tf_op jit(solution)/shard_map/ppermute | solution.py:320
  67.1 0.7 fusion.34.send
  67.8 20.2 %collective-permute-done.13.rest_1_ = bf16[512,768]{1,0:T(8,128)(2,1)S(1)} collective-permute-done((bf16[512,768]{1,0:T(8,128)(2,1)S(1)}, bf16[512,768]{1,0:T(8,128)(2,1)S(1)}, u32[]{:S(2)}, u32[]{:S(2)}) %collective-permute-start.13) | collective-permute-done | bytes 786464 | tf_op jit(solution)/shard_map/ppermute | solution.py:320
  88.1 3.4 %collective-permute-done.11.rest_2_ = bf16[512,768]{1,0:T(8,128)(2,1)S(1)} collective-permute-done((bf16[512,768]{1,0:T(8,128)(2,1)S(1)}, bf16[512,768]{1,0:T(8,128)(2,1)S(1)}, u32[]{:S(2)}, u32[]{:S(2)}) %collective-permute-start.11) | collective-permute-done | bytes 786464 | tf_op jit(solution)/shard_map/ppermute | solution.py:320
  91.7 2.9 %collective-permute-start.18 = (bf16[256,768]{1,0:T(8,128)(2,1)S(1)}, bf16[256,768]{1,0:T(8,128)(2,1)S(1)}, u32[]{:S(2)}, u32[]{:S(2)}) collective-permute-start(bf16[256,768]{1,0:T(8,128)(2,1)S(1)} %slice.250), channel_id=1, source_target_pairs={{0,24},{8,0},{16,8},{24,16},{1,25},{9,1},{17,9},{25,17},{2,26},{10... | collective-permute-start | bytes 1179656 | tf_op jit(solution)/shard_map/ppermute | solution.py:320
  94.6 2.7 %collective-permute-start.16 = (bf16[256,768]{1,0:T(8,128)(2,1)S(1)}, bf16[256,768]{1,0:T(8,128)(2,1)S(1)}, u32[]{:S(2)}, u32[]{:S(2)}) collective-permute-start(bf16[256,768]{1,0:T(8,128)(2,1)S(1)} %slice.248), channel_id=1, source_target_pairs={{0,96},{32,0},{64,32},{96,64},{1,97},{33,1},{65,33},{97,65},{2,98}... | collective-permute-start | bytes 1179656 | tf_op jit(solution)/shard_map/ppermute | solution.py:320
  97.9 0.6 fusion.66
  98.5 2.7 %shard_map.104 = (f32[128,1536]{1,0:T(8,128)S(1)}, bf16[16,128,128]{2,1,0:T(8,128)(2,1)S(1)}) custom-call(s32[2]{0:T(128)S(1)} %copy-done.24, bf16[128,2048]{1,0:T(8,128)(2,1)S(1)} %bitcast.92, f32[1,2048]{1,0:T(1,128)S(1)} %bitcast.94, f32[1,2048]{1,0:T(1,128)S(1)} %bitcast.96, f32[1,1536]{1,0:T(1,128)S(1)} %broadcast_in_dim.156.bias, ...), custom_call_target="tpu_custom_call" | custom-call | flops 196608 | bytes 196608 | tf_op jit(solution)/shard_map/pallas_call | solution.py:244
  101.3 1.6 collective-permute-done.17.rest_2_.rest_8_
  102.9 2.2 %collective-permute-done.15.rest_0_.rest_3_ = bf16[256,768]{1,0:T(8,128)(2,1)S(1)} collective-permute-done((bf16[256,768]{1,0:T(8,128)(2,1)S(1)}, bf16[256,768]{1,0:T(8,128)(2,1)S(1)}, u32[]{:S(2)}, u32[]{:S(2)}) %collective-permute-start.15) | collective-permute-done | bytes 393248 | tf_op jit(solution)/shard_map/ppermute | solution.py:320
  105.2 3.3 %shard_map.105.context = bf16[128,512]{1,0:T(8,128)(2,1)} custom-call(s32[2]{0:T(128)S(1)} %copy-done.24, bf16[16,128,128]{2,1,0:T(8,128)(2,1)S(1)} %get-tuple-element.254.normed, f32[128,1536]{1,0:T(8,128)S(1)} %get-tuple-element.255.near, f32[3,128,128]{2,1,0:T(8,128)S(1)} %pad_maximum_fusion.11.turns, f32[128,128]{1,0:T(8,128)S(1)} %get-tuple-element.362.allowed.rest_0_, ...), custom_call_target="tpu_custom_call" | custom-call | flops 196608 | bytes 196608 | tf_op jit(solution)/shard_map/pallas_call | solution.py:244
  108.4 0.8 copy-done.16
  109.2 2.5 %shard_map.106 = (bf16[384,512]{1,0:T(8,128)(2,1)}, bf16[384,512]{1,0:T(8,128)(2,1)}, f32[1,128]{1,0:T(1,128)}) custom-call(bf16[384,1152]{1,0:T(8,128)(2,1)} %bitcast.22.meta, bf16[384,128]{1,0:T(8,128)(2,1)} %fusion.34.send, bf16[128,512]{1,0:T(8,128)(2,1)} %shard_map.105.context), custom_call_target="tpu_custom_call" | custom-call | flops 16384 | bytes 16384 | tf_op jit(solution)/shard_map/pallas_call | solution.py:465
  111.7 6.6 %all-to-all-start.2 = ((bf16[8,48,512]{2,1,0:T(8,128)(2,1)}), bf16[8,48,512]{2,1,0:T(8,128)(2,1)S(1)}, u32[]{:S(2)}, u32[]{:S(2)}) async-start(bf16[8,48,512]{2,1,0:T(8,128)(2,1)} %bitcast.119), calls=%async_computation.2 | async-start | bytes 786432 | tf_op jit(solution)/shard_map/all_to_all | solution.py:50
  118.9 0.6 broadcast_in_dim.171.bias
  119.5 1.3 slice_select_fusion.1
  120.8 2.5 %collective-permute-start.19 = (bf16[128,512]{1,0:T(8,128)(2,1)}, bf16[128,512]{1,0:T(8,128)(2,1)}, u32[]{:S(2)}, u32[]{:S(2)}) collective-permute-start(bf16[128,512]{1,0:T(8,128)(2,1)} %shard_map.105.context), channel_id=1, source_target_pairs={{0,128},{128,0},{1,129},{129,1},{2,130},{130,2},{3,131},{131,3},{4... | collective-permute-start | bytes 393224 | tf_op jit(solution)/shard_map/ppermute | solution.py:27
  125.4 0.9 slice.314
  126.3 1.2 slice.313
  127.5 8.1 %all-to-all-done.2 = bf16[8,48,512]{2,1,0:T(8,128)(2,1)S(1)} async-done(((bf16[8,48,512]{2,1,0:T(8,128)(2,1)}), bf16[8,48,512]{2,1,0:T(8,128)(2,1)S(1)}, u32[]{:S(2)}, u32[]{:S(2)}) %all-to-all-start.2) | async-done | bytes 393248 | tf_op jit(solution)/shard_map/all_to_all | solution.py:50
  135.7 2.3 %convolution_convert_fusion.2 = bf16[512,1664]{1,0:T(8,128)(2,1)} fusion(bf16[384,512]{1,0:T(8,128)(2,1)S(1)} %copy-done.58, bf16[384,128]{1,0:T(8,128)(2,1)S(1)} %slice.314, bf16[384,512]{1,0:T(8,128)(2,1)S(1)} %bitcast.118, bf16[384,1024]{1,0:T(8,128)(2,1)S(1)} %slice.313), kind=kOutput, calls=%fused_computation.20 | convolution fusion | flops 658997248 | bytes 3375104 | tf_op jit(solution)/shard_map/dot_general | solution.py:479
  138.0 4.7 %all-to-all-start.3 = ((bf16[16,32,1664]{2,1,0:T(8,128)(2,1)}), bf16[16,32,1664]{2,1,0:T(8,128)(2,1)S(1)}, u32[]{:S(2)}, u32[]{:S(2)}) async-start(bf16[16,32,1664]{2,1,0:T(8,128)(2,1)} %bitcast.113), calls=%async_computation.3 | async-start | bytes 3407872 | tf_op jit(solution)/shard_map/all_to_all | solution.py:50
  142.7 1.7 broadcast_select_fusion.15
  144.4 1.2 slice.315
  145.6 10.5 %all-gather.2.cloned.1.call-done.rest_1_.rest_2_.rest_3_.rest_0_ = bf16[2048,2560]{1,0:T(8,128)(2,1)} async-done(((bf16[16,2560]{1,0:T(8,128)(2,1)}), bf16[2048,2560]{1,0:T(8,128)(2,1)}) %all-gather.2.cloned.1.call-update) | async-done | bytes 10485776 | tf_op jit(solution)/shard_map/all_gather | solution.py:401
  157.2 3.9 %fusion.61 = (bf16[2048,512]{1,0:T(8,128)(2,1)}, bf16[2048,512]{1,0:T(8,128)(2,1)S(1)}) fusion(bf16[2048,2560]{1,0:T(8,128)(2,1)} %all-gather.2.cloned.1.call-done.rest_1_.rest_2_.rest_3_.rest_0_), kind=kLoop, calls=%fused_computation.182 | loop fusion | bytes 8388608 | tf_op jit(solution)/shard_map/slice | solution.py:494
  161.8 0.8 copy-done.9
  162.5 0.8 fusion.26
  163.3 2.2 %collective-permute-start.20 = (bf16[128,1024]{1,0:T(8,128)(2,1)}, bf16[128,1024]{1,0:T(8,128)(2,1)}, u32[]{:S(2)}, u32[]{:S(2)}) collective-permute-start(bf16[128,1024]{1,0:T(8,128)(2,1)} %fusion.26), channel_id=1, source_target_pairs={{0,128},{128,0},{1,129},{129,1},{2,130},{130,2},{3,131},{131,3},{4... | collective-permute-start | bytes 786440 | tf_op jit(solution)/shard_map/ppermute | solution.py:27
  165.6 1.3 shard_map.108
  167.2 0.9 convert_reduce_fusion
  168.2 1.0 slice.332
  169.2 3.0 %collective-permute-start.23 = (bf16[128,1536]{1,0:T(8,128)(2,1)S(1)}, bf16[128,1536]{1,0:T(8,128)(2,1)S(1)}, u32[]{:S(2)}, u32[]{:S(2)}) collective-permute-start(bf16[128,1536]{1,0:T(8,128)(2,1)S(1)} %slice.332), channel_id=1, source_target_pairs={{0,128},{128,0},{1,129},{129,1},{2,130},{130,2},{3,131},{131,3},{4... | collective-permute-start | bytes 1179656 | tf_op jit(solution)/shard_map/ppermute | solution.py:27
  172.6 1.1 broadcast_select_fusion.11
  173.7 5.5 %shard_map.107 = bf16[128,512]{1,0:T(8,128)(2,1)S(1)} custom-call(bf16[128,2048]{1,0:T(8,128)(2,1)S(1)} %pad_maximum_fusion.3.layer_in, f32[1,2048]{1,0:T(1,128)S(1)} %bitcast.100, f32[1,2048]{1,0:T(1,128)S(1)} %bitcast.98, f32[1,1536]{1,0:T(1,128)S(1)} %copy-done.22, f32[3,128,128]{2,1,0:T(8,128)S(1)} %pad_maximum_fusion.11.turns, ...), custom_call_target="tpu_custom_call" | custom-call | flops 196608 | bytes 196608 | tf_op jit(solution)/shard_map/pallas_call | solution.py:300
  179.5 1.3 copy-done.31
  181.5 0.9 copy-done.29
  183.3 1.1 fusion.28
  186.5 2.4 %shard_map.109 = bf16[128,1024]{1,0:T(8,128)(2,1)S(1)} custom-call(s32[2]{0:T(128)S(1)} %copy-done.25, bf16[128,2048]{1,0:T(8,128)(2,1)S(1)} %pad_maximum_fusion.4.layer_in, f32[1,2048]{1,0:T(1,128)S(1)} %bitcast.95, f32[1,2048]{1,0:T(1,128)S(1)} %bitcast.97, f32[1,1024]{1,0:T(1,128)S(1)} %copy-done.23, f32[3,128,128]{2,1,0:T(8,128)S(1)} %pad_maximum_fusion.12.turns, ...), custom_call_target="tpu_custom_call" | custom-call | flops 131072 | bytes 131072 | tf_op jit(solution)/shard_map/pallas_call | solution.py:244
  188.9 4.1 %shard_map.110 = bf16[128,1024]{1,0:T(8,128)(2,1)S(1)} custom-call(bf16[128,2048]{1,0:T(8,128)(2,1)S(1)} %pad_maximum_fusion.5.layer_in, f32[1,2048]{1,0:T(1,128)S(1)} %bitcast.101, f32[1,2048]{1,0:T(1,128)S(1)} %bitcast.99, f32[1,1024]{1,0:T(1,128)S(1)} %slice.282.bias, f32[3,128,128]{2,1,0:T(8,128)S(1)} %pad_maximum_fusion.12.turns, ...), custom_call_target="tpu_custom_call" | custom-call | flops 131072 | bytes 131072 | tf_op jit(solution)/shard_map/pallas_call | solution.py:300
  193.6 0.9 maximum_select_fusion
  194.8 0.8 maximum_bitcast_fusion
  (223 shorter events, 13.4 us)
Async XLA Ops:
  7.2 148.9 %all-gather.2.cloned.1.call-start = ((), (), s32[]{:S(2)}) async-start(), calls=%async_computation.4 | async-start | bytes 10567680 | tf_op jit(solution)/shard_map/all_gather | solution.py:401
  8.8 4.2 %collective-permute-start = (bf16[16,2048]{1,0:T(8,128)(2,1)S(1)}, bf16[16,2048]{1,0:T(8,128)(2,1)S(1)}, u32[]{:S(2)}, u32[]{:S(2)}) collective-permute-start(bf16[16,2048]{1,0:T(8,128)(2,1)S(1)} %broadcast_select_fusion.18), channel_id=1, source_target_pairs={{0,128},{128,0},{1,129},{129,1},{2,130},{130,2},{3,131},{131,3},{4... | collective-permute-start | bytes 196616 | tf_op jit(solution)/shard_map/ppermute | solution.py:27
  13.8 46.6 %copy-start.49 = (pred[128]{0:T(512)(128)(4,1)}, pred[128]{0:T(512)(128)(4,1)S(1)}, u32[]{:S(2)}) copy-start(pred[128]{0:T(512)(128)(4,1)S(1)} %iota_compare_fusion.13) | copy-start | bytes 388
  13.8 7.0 %collective-permute-start.1 = (bf16[1,16,1536]{2,1,0:T(8,128)(2,1)S(1)}, bf16[1,16,1536]{2,1,0:T(8,128)(2,1)S(1)}, u32[]{:S(2)}, u32[]{:S(2)}) collective-permute-start(bf16[1,16,1536]{2,1,0:T(8,128)(2,1)S(1)} %slice_bitcast_fusion.10), channel_id=1, source_target_pairs={{0,4},{1,5},{2,6},{3,7},{4,0},{5,1},{6,2},{7,3},{8,12},{9,13},{10,... | collective-permute-start | bytes 147464 | tf_op jit(solution)/shard_map/ppermute | solution.py:346
  19.1 41.3 %copy-start.51 = (f32[128]{0:T(128)}, f32[128]{0:T(128)S(1)}, u32[]{:S(2)}) copy-start(f32[128]{0:T(128)S(1)} %multiply_power_fusion) | copy-start | bytes 1540
  20.9 7.0 %collective-permute-start.2 = (bf16[2,16,1536]{2,1,0:T(8,128)(2,1)S(1)}, bf16[2,16,1536]{2,1,0:T(8,128)(2,1)S(1)}, u32[]{:S(2)}, u32[]{:S(2)}) collective-permute-start(bf16[2,16,1536]{2,1,0:T(8,128)(2,1)S(1)} %maximum_bitcast_fusion.1), channel_id=1, source_target_pairs={{0,2},{1,3},{2,0},{3,1},{4,6},{5,7},{6,4},{7,5},{8,10},{9,11},{10,... | collective-permute-start | bytes 294920 | tf_op jit(solution)/shard_map/ppermute | solution.py:346
  22.1 23.5 %copy-start.47 = (s32[4,32]{1,0:T(4,128)S(1)}, s32[4,32]{1,0:T(4,128)}, u32[]{:S(2)}) copy-start(s32[4,32]{1,0:T(4,128)} %param.15) | copy-start | bytes 1540
  22.1 23.6 %copy-start.57 = (s32[4,32]{1,0:T(4,128)S(1)}, s32[4,32]{1,0:T(4,128)}, u32[]{:S(2)}) copy-start(s32[4,32]{1,0:T(4,128)} %param.14) | copy-start | bytes 1540
  27.9 20.7 %copy-start.37 = (f32[1,3072]{1,0:T(1,128)S(1)}, f32[1,3072]{1,0:T(1,128)}, u32[]{:S(2)}) copy-start(f32[1,3072]{1,0:T(1,128)} %param.19) | copy-start | bytes 36868
  27.9 20.7 %copy-start.40 = (f32[1,2048]{1,0:T(1,128)S(1)}, f32[1,2048]{1,0:T(1,128)}, u32[]{:S(2)}) copy-start(f32[1,2048]{1,0:T(1,128)} %param.21) | copy-start | bytes 24580
  28.0 20.7 %copy-start.41 = (f32[1,2048]{1,0:T(1,128)S(1)}, f32[1,2048]{1,0:T(1,128)}, u32[]{:S(2)}) copy-start(f32[1,2048]{1,0:T(1,128)} %param.17) | copy-start | bytes 24580
  28.0 20.7 %copy-start.42 = (f32[1,2048]{1,0:T(1,128)S(1)}, f32[1,2048]{1,0:T(1,128)}, u32[]{:S(2)}) copy-start(f32[1,2048]{1,0:T(1,128)} %param.16) | copy-start | bytes 24580
  28.0 25.3 %copy-start.8 = (bf16[4,32,2048]{2,1,0:T(8,128)(2,1)S(1)}, bf16[4,32,2048]{2,1,0:T(8,128)(2,1)}, u32[]{:S(2)}) copy-start(bf16[4,32,2048]{2,1,0:T(8,128)(2,1)} %param.13) | copy-start | bytes 1572868
  28.0 5.9 %collective-permute-start.3 = (bf16[4,16,1536]{2,1,0:T(8,128)(2,1)S(1)}, bf16[4,16,1536]{2,1,0:T(8,128)(2,1)S(1)}, u32[]{:S(2)}, u32[]{:S(2)}) collective-permute-start(bf16[4,16,1536]{2,1,0:T(8,128)(2,1)S(1)} %bitcast.117), channel_id=1, source_target_pairs={{0,1},{1,0},{2,3},{3,2},{4,5},{5,4},{6,7},{7,6},{8,9},{9,8},{10,11... | collective-permute-start | bytes 589832 | tf_op jit(solution)/shard_map/ppermute | solution.py:346
  34.1 6.0 %collective-permute-start.7 = (bf16[128,768]{1,0:T(8,128)(2,1)S(1)}, bf16[128,768]{1,0:T(8,128)(2,1)S(1)}, u32[]{:S(2)}, u32[]{:S(2)}) collective-permute-start(bf16[128,768]{1,0:T(8,128)(2,1)S(1)} %get-tuple-element.317), channel_id=1, source_target_pairs={{0,96},{32,0},{64,32},{96,64},{1,97},{33,1},{65,33},{97,65},{2,98}... | collective-permute-start | bytes 589832 | tf_op jit(solution)/shard_map/ppermute | solution.py:320
  36.7 5.8 %collective-permute-start.5 = (bf16[128,768]{1,0:T(8,128)(2,1)S(1)}, bf16[128,768]{1,0:T(8,128)(2,1)S(1)}, u32[]{:S(2)}, u32[]{:S(2)}) collective-permute-start(bf16[128,768]{1,0:T(8,128)(2,1)S(1)} %get-tuple-element.317), channel_id=1, source_target_pairs={{0,32},{32,64},{64,96},{96,0},{1,33},{33,65},{65,97},{97,1},{2,34}... | collective-permute-start | bytes 589832 | tf_op jit(solution)/shard_map/ppermute | solution.py:320
  36.7 5.8 %collective-permute-start.6 = (bf16[128,768]{1,0:T(8,128)(2,1)S(1)}, bf16[128,768]{1,0:T(8,128)(2,1)S(1)}, u32[]{:S(2)}, u32[]{:S(2)}) collective-permute-start(bf16[128,768]{1,0:T(8,128)(2,1)S(1)} %get-tuple-element.318), channel_id=1, source_target_pairs={{0,24},{8,0},{16,8},{24,16},{1,25},{9,1},{17,9},{25,17},{2,26},{10... | collective-permute-start | bytes 589832 | tf_op jit(solution)/shard_map/ppermute | solution.py:320
  39.4 6.3 %collective-permute-start.4 = (bf16[128,768]{1,0:T(8,128)(2,1)S(1)}, bf16[128,768]{1,0:T(8,128)(2,1)S(1)}, u32[]{:S(2)}, u32[]{:S(2)}) collective-permute-start(bf16[128,768]{1,0:T(8,128)(2,1)S(1)} %get-tuple-element.318), channel_id=1, source_target_pairs={{0,8},{8,16},{16,24},{24,0},{1,9},{9,17},{17,25},{25,1},{2,10},{10... | collective-permute-start | bytes 589832 | tf_op jit(solution)/shard_map/ppermute | solution.py:320
  40.1 21.4 %copy-start.53 = (pred[128]{0:T(512)(128)(4,1)}, pred[128]{0:T(512)(128)(4,1)S(1)}, u32[]{:S(2)}) copy-start(pred[128]{0:T(512)(128)(4,1)S(1)} %get-tuple-element.379) | copy-start | bytes 388
  40.1 21.4 %copy-start.55 = (pred[128]{0:T(512)(128)(4,1)}, pred[128]{0:T(512)(128)(4,1)S(1)}, u32[]{:S(2)}) copy-start(pred[128]{0:T(512)(128)(4,1)S(1)} %get-tuple-element.380) | copy-start | bytes 388
  45.7 7.4 %copy-start.48 = (s32[128]{0:T(128)}, s32[128]{0:T(128)S(1)}, u32[]{:S(2)}) copy-start(s32[128]{0:T(128)S(1)} %reshape.829) | copy-start | bytes 1540
  48.6 19.1 %collective-permute-start.8 = (f32[9216]{0:T(1024)S(1)}, f32[9216]{0:T(1024)S(1)}, u32[]{:S(2)}, u32[]{:S(2)}) collective-permute-start(f32[9216]{0:T(1024)S(1)} %pad_maximum_fusion.20), channel_id=1, source_target_pairs={{0,128},{128,0},{1,129},{129,1},{2,130},{130,2},{3,131},{131,3},{4... | collective-permute-start | bytes 110600 | tf_op jit(solution)/shard_map/ppermute | solution.py:27
  51.9 9.6 %collective-permute-start.9 = (bf16[128,768]{1,0:T(8,128)(2,1)S(1)}, bf16[128,768]{1,0:T(8,128)(2,1)S(1)}, u32[]{:S(2)}, u32[]{:S(2)}) collective-permute-start(bf16[128,768]{1,0:T(8,128)(2,1)S(1)} %collective-permute-done.4), channel_id=1, source_target_pairs={{0,8},{8,16},{16,24},{24,0},{1,9},{9,17},{17,25},{25,1},{2,10},{10... | collective-permute-start | bytes 589832 | tf_op jit(solution)/shard_map/ppermute | solution.py:320
  51.9 9.7 %collective-permute-start.10 = (bf16[128,768]{1,0:T(8,128)(2,1)S(1)}, bf16[128,768]{1,0:T(8,128)(2,1)S(1)}, u32[]{:S(2)}, u32[]{:S(2)}) collective-permute-start(bf16[128,768]{1,0:T(8,128)(2,1)S(1)} %collective-permute-done.5), channel_id=1, source_target_pairs={{0,32},{32,64},{64,96},{96,0},{1,33},{33,65},{65,97},{97,1},{2,34}... | collective-permute-start | bytes 589832 | tf_op jit(solution)/shard_map/ppermute | solution.py:320
  53.2 8.3 %copy-start.32 = (bf16[128,128]{1,0:T(8,128)(2,1)}, bf16[128,128]{1,0:T(8,128)(2,1)S(1)}, u32[]{:S(2)}) copy-start(bf16[128,128]{1,0:T(8,128)(2,1)S(1)} %select_convert_fusion) | copy-start | bytes 98308
  55.3 53.9 %all-to-all-start.1 = ((bf16[8,48,1152]{2,1,0:T(8,128)(2,1)}), bf16[8,48,1152]{2,1,0:T(8,128)(2,1)}, u32[]{:S(2)}, u32[]{:S(2)}) async-start(bf16[8,48,1152]{2,1,0:T(8,128)(2,1)} %bitcast.21), calls=%async_computation.1 | async-start | bytes 1769472 | tf_op jit(solution)/shard_map/all_to_all | solution.py:50
  61.7 36.9 %copy-start.24 = (s32[2]{0:T(128)S(1)}, s32[2]{0:T(128)}, u32[]{:S(2)}) copy-start(s32[2]{0:T(128)} %pad_add_fusion.place) | copy-start | bytes 28
  61.7 26.4 %collective-permute-start.13 = (bf16[512,768]{1,0:T(8,128)(2,1)S(1)}, bf16[512,768]{1,0:T(8,128)(2,1)S(1)}, u32[]{:S(2)}, u32[]{:S(2)}) collective-permute-start(bf16[512,768]{1,0:T(8,128)(2,1)S(1)} %pad_maximum_fusion.1.rest_0_), channel_id=1, source_target_pairs={{0,96},{32,0},{64,32},{96,64},{1,97},{33,1},{65,33},{97,65},{2,98}... | collective-permute-start | bytes 2359304 | tf_op jit(solution)/shard_map/ppermute | solution.py:320
  64.4 27.1 %collective-permute-start.11 = (bf16[512,768]{1,0:T(8,128)(2,1)S(1)}, bf16[512,768]{1,0:T(8,128)(2,1)S(1)}, u32[]{:S(2)}, u32[]{:S(2)}) collective-permute-start(bf16[512,768]{1,0:T(8,128)(2,1)S(1)} %pad_maximum_fusion.1.rest_0_), channel_id=1, source_target_pairs={{0,32},{32,64},{64,96},{96,0},{1,33},{33,65},{65,97},{97,1},{2,34}... | collective-permute-start | bytes 2359304 | tf_op jit(solution)/shard_map/ppermute | solution.py:320
  64.4 27.1 %collective-permute-start.14 = (bf16[512,768]{1,0:T(8,128)(2,1)S(1)}, bf16[512,768]{1,0:T(8,128)(2,1)S(1)}, u32[]{:S(2)}, u32[]{:S(2)}) collective-permute-start(bf16[512,768]{1,0:T(8,128)(2,1)S(1)} %pad_maximum_fusion.2.rest_3_.rest_5_), channel_id=1, source_target_pairs={{0,24},{8,0},{16,8},{24,16},{1,25},{9,1},{17,9},{25,17},{2,26},{10... | collective-permute-start | bytes 2359304 | tf_op jit(solution)/shard_map/ppermute | solution.py:320
  67.1 24.4 %collective-permute-start.12 = (bf16[512,768]{1,0:T(8,128)(2,1)S(1)}, bf16[512,768]{1,0:T(8,128)(2,1)S(1)}, u32[]{:S(2)}, u32[]{:S(2)}) collective-permute-start(bf16[512,768]{1,0:T(8,128)(2,1)S(1)} %pad_maximum_fusion.2.rest_3_.rest_5_), channel_id=1, source_target_pairs={{0,8},{8,16},{16,24},{24,0},{1,9},{9,17},{17,25},{25,1},{2,10},{10... | collective-permute-start | bytes 2359304 | tf_op jit(solution)/shard_map/ppermute | solution.py:320
  67.8 30.7 %copy-start.33 = (f32[9216]{0:T(1024)}, f32[9216]{0:T(1024)S(1)}, u32[]{:S(2)}) copy-start(f32[9216]{0:T(1024)S(1)} %get-tuple-element.339) | copy-start | bytes 110596
  67.8 30.7 %copy-start.34 = (f32[9216]{0:T(1024)}, f32[9216]{0:T(1024)S(1)}, u32[]{:S(2)}) copy-start(f32[9216]{0:T(1024)S(1)} %get-tuple-element.340) | copy-start | bytes 110596
  88.1 13.2 %copy-start = (bf16[512,768]{1,0:T(8,128)(2,1)}, bf16[512,768]{1,0:T(8,128)(2,1)S(1)}, u32[]{:S(2)}) copy-start(bf16[512,768]{1,0:T(8,128)(2,1)S(1)} %collective-permute-done.13.rest_1_) | copy-start | bytes 2359300
  91.5 9.8 %copy-start.2 = (bf16[512,768]{1,0:T(8,128)(2,1)}, bf16[512,768]{1,0:T(8,128)(2,1)S(1)}, u32[]{:S(2)}) copy-start(bf16[512,768]{1,0:T(8,128)(2,1)S(1)} %collective-permute-done.11.rest_2_) | copy-start | bytes 2359300
  91.5 9.8 %copy-start.4 = (bf16[512,768]{1,0:T(8,128)(2,1)}, bf16[512,768]{1,0:T(8,128)(2,1)S(1)}, u32[]{:S(2)}) copy-start(bf16[512,768]{1,0:T(8,128)(2,1)S(1)} %collective-permute-done.14.rest_4_.rest_6_) | copy-start | bytes 2359300
  91.5 9.8 %copy-start.6 = (bf16[512,768]{1,0:T(8,128)(2,1)}, bf16[512,768]{1,0:T(8,128)(2,1)S(1)}, u32[]{:S(2)}) copy-start(bf16[512,768]{1,0:T(8,128)(2,1)S(1)} %collective-permute-done.12.rest_5_.rest_7_) | copy-start | bytes 2359300
  91.6 11.2 %collective-permute-start.17 = (bf16[256,768]{1,0:T(8,128)(2,1)S(1)}, bf16[256,768]{1,0:T(8,128)(2,1)S(1)}, u32[]{:S(2)}, u32[]{:S(2)}) collective-permute-start(bf16[256,768]{1,0:T(8,128)(2,1)S(1)} %slice.249), channel_id=1, source_target_pairs={{0,8},{8,16},{16,24},{24,0},{1,9},{9,17},{17,25},{25,1},{2,10},{10... | collective-permute-start | bytes 1179656 | tf_op jit(solution)/shard_map/ppermute | solution.py:320
  91.7 11.2 %collective-permute-start.18 = (bf16[256,768]{1,0:T(8,128)(2,1)S(1)}, bf16[256,768]{1,0:T(8,128)(2,1)S(1)}, u32[]{:S(2)}, u32[]{:S(2)}) collective-permute-start(bf16[256,768]{1,0:T(8,128)(2,1)S(1)} %slice.250), channel_id=1, source_target_pairs={{0,24},{8,0},{16,8},{24,16},{1,25},{9,1},{17,9},{25,17},{2,26},{10... | collective-permute-start | bytes 1179656 | tf_op jit(solution)/shard_map/ppermute | solution.py:320
  94.6 10.5 %collective-permute-start.15 = (bf16[256,768]{1,0:T(8,128)(2,1)S(1)}, bf16[256,768]{1,0:T(8,128)(2,1)S(1)}, u32[]{:S(2)}, u32[]{:S(2)}) collective-permute-start(bf16[256,768]{1,0:T(8,128)(2,1)S(1)} %slice.247), channel_id=1, source_target_pairs={{0,32},{32,64},{64,96},{96,0},{1,33},{33,65},{65,97},{97,1},{2,34}... | collective-permute-start | bytes 1179656 | tf_op jit(solution)/shard_map/ppermute | solution.py:320
  94.6 10.5 %collective-permute-start.16 = (bf16[256,768]{1,0:T(8,128)(2,1)S(1)}, bf16[256,768]{1,0:T(8,128)(2,1)S(1)}, u32[]{:S(2)}, u32[]{:S(2)}) collective-permute-start(bf16[256,768]{1,0:T(8,128)(2,1)S(1)} %slice.248), channel_id=1, source_target_pairs={{0,96},{32,0},{64,32},{96,64},{1,97},{33,1},{65,33},{97,65},{2,98}... | collective-permute-start | bytes 1179656 | tf_op jit(solution)/shard_map/ppermute | solution.py:320
  102.9 8.8 %copy-start.10 = (bf16[256,768]{1,0:T(8,128)(2,1)}, bf16[256,768]{1,0:T(8,128)(2,1)S(1)}, u32[]{:S(2)}) copy-start(bf16[256,768]{1,0:T(8,128)(2,1)S(1)} %collective-permute-done.17.rest_2_.rest_8_) | copy-start | bytes 1179652
  102.9 8.8 %copy-start.12 = (bf16[256,768]{1,0:T(8,128)(2,1)}, bf16[256,768]{1,0:T(8,128)(2,1)S(1)}, u32[]{:S(2)}) copy-start(bf16[256,768]{1,0:T(8,128)(2,1)S(1)} %collective-permute-done.18.rest_3_.rest_9_) | copy-start | bytes 1179652
  105.1 6.6 %copy-start.14 = (bf16[256,768]{1,0:T(8,128)(2,1)}, bf16[256,768]{1,0:T(8,128)(2,1)S(1)}, u32[]{:S(2)}) copy-start(bf16[256,768]{1,0:T(8,128)(2,1)S(1)} %collective-permute-done.15.rest_0_.rest_3_) | copy-start | bytes 1179652
  105.1 13.1 %copy-start.21 = (f32[1,1536]{1,0:T(1,128)S(1)}, f32[1,1536]{1,0:T(1,128)}, u32[]{:S(2)}) copy-start(f32[1,1536]{1,0:T(1,128)} %copy-done.20) | copy-start | bytes 18436
  105.1 13.7 %copy-start.44 = (f32[512]{0:T(512)S(1)}, f32[512]{0:T(512)}, u32[]{:S(2)}) copy-start(f32[512]{0:T(512)} %get-tuple-element.341) | copy-start | bytes 6148
  105.1 13.7 %copy-start.45 = (f32[512]{0:T(512)S(1)}, f32[512]{0:T(512)}, u32[]{:S(2)}) copy-start(f32[512]{0:T(512)} %get-tuple-element.342) | copy-start | bytes 6148
  105.2 13.7 %copy-start.46 = (f32[512]{0:T(512)S(1)}, f32[512]{0:T(512)}, u32[]{:S(2)}) copy-start(f32[512]{0:T(512)} %get-tuple-element.343) | copy-start | bytes 6148
  111.7 24.0 %copy-start.58 = (bf16[384,512]{1,0:T(8,128)(2,1)S(1)}, bf16[384,512]{1,0:T(8,128)(2,1)}, u32[]{:S(2)}) copy-start(bf16[384,512]{1,0:T(8,128)(2,1)} %get-tuple-element.258) | copy-start | bytes 1179652
  111.7 24.0 %all-to-all-start.2 = ((bf16[8,48,512]{2,1,0:T(8,128)(2,1)}), bf16[8,48,512]{2,1,0:T(8,128)(2,1)S(1)}, u32[]{:S(2)}, u32[]{:S(2)}) async-start(bf16[8,48,512]{2,1,0:T(8,128)(2,1)} %bitcast.119), calls=%async_computation.2 | async-start | bytes 786432 | tf_op jit(solution)/shard_map/all_to_all | solution.py:50
  120.8 21.9 %collective-permute-start.19 = (bf16[128,512]{1,0:T(8,128)(2,1)}, bf16[128,512]{1,0:T(8,128)(2,1)}, u32[]{:S(2)}, u32[]{:S(2)}) collective-permute-start(bf16[128,512]{1,0:T(8,128)(2,1)} %shard_map.105.context), channel_id=1, source_target_pairs={{0,128},{128,0},{1,129},{129,1},{2,130},{130,2},{3,131},{131,3},{4... | collective-permute-start | bytes 393224 | tf_op jit(solution)/shard_map/ppermute | solution.py:27
  138.0 27.6 %all-to-all-start.3 = ((bf16[16,32,1664]{2,1,0:T(8,128)(2,1)}), bf16[16,32,1664]{2,1,0:T(8,128)(2,1)S(1)}, u32[]{:S(2)}, u32[]{:S(2)}) async-start(bf16[16,32,1664]{2,1,0:T(8,128)(2,1)} %bitcast.113), calls=%async_computation.3 | async-start | bytes 3407872 | tf_op jit(solution)/shard_map/all_to_all | solution.py:50
  163.3 9.2 %collective-permute-start.20 = (bf16[128,1024]{1,0:T(8,128)(2,1)}, bf16[128,1024]{1,0:T(8,128)(2,1)}, u32[]{:S(2)}, u32[]{:S(2)}) collective-permute-start(bf16[128,1024]{1,0:T(8,128)(2,1)} %fusion.26), channel_id=1, source_target_pairs={{0,128},{128,0},{1,129},{129,1},{2,130},{130,2},{3,131},{131,3},{4... | collective-permute-start | bytes 786440 | tf_op jit(solution)/shard_map/ppermute | solution.py:27
  166.9 5.3 %copy-start.50 = (pred[128]{0:T(512)(128)(4,1)S(1)}, pred[128]{0:T(512)(128)(4,1)}, u32[]{:S(2)}) copy-start(pred[128]{0:T(512)(128)(4,1)} %copy-done.49) | copy-start | bytes 388
  167.0 5.3 %copy-start.52 = (f32[128]{0:T(128)S(1)}, f32[128]{0:T(128)}, u32[]{:S(2)}) copy-start(f32[128]{0:T(128)} %copy-done.51) | copy-start | bytes 1540
  167.0 5.3 %copy-start.54 = (pred[128]{0:T(512)(128)(4,1)S(1)}, pred[128]{0:T(512)(128)(4,1)}, u32[]{:S(2)}) copy-start(pred[128]{0:T(512)(128)(4,1)} %copy-done.53) | copy-start | bytes 388
  167.2 6.5 %copy-start.18 = (f32[2048]{0:T(1024)S(1)}, f32[2048]{0:T(1024)}, u32[]{:S(2)}) copy-start(f32[2048]{0:T(1024)} %get-tuple-element.344) | copy-start | bytes 24580
  167.2 6.5 %copy-start.19 = (f32[2048]{0:T(1024)S(1)}, f32[2048]{0:T(1024)}, u32[]{:S(2)}) copy-start(f32[2048]{0:T(1024)} %get-tuple-element.345) | copy-start | bytes 24580
  169.2 10.2 %collective-permute-start.23 = (bf16[128,1536]{1,0:T(8,128)(2,1)S(1)}, bf16[128,1536]{1,0:T(8,128)(2,1)S(1)}, u32[]{:S(2)}, u32[]{:S(2)}) collective-permute-start(bf16[128,1536]{1,0:T(8,128)(2,1)S(1)} %slice.332), channel_id=1, source_target_pairs={{0,128},{128,0},{1,129},{129,1},{2,130},{130,2},{3,131},{131,3},{4... | collective-permute-start | bytes 1179656 | tf_op jit(solution)/shard_map/ppermute | solution.py:27
  173.7 5.7 %copy-start.27 = (bf16[128,1664]{1,0:T(8,128)(2,1)S(1)}, bf16[128,1664]{1,0:T(8,128)(2,1)}, u32[]{:S(2)}) copy-start(bf16[128,1664]{1,0:T(8,128)(2,1)} %get-tuple-element.443) | copy-start | bytes 1277956
  179.3 2.2 %collective-permute-start.21 = (bf16[128,512]{1,0:T(8,128)(2,1)S(1)}, bf16[128,512]{1,0:T(8,128)(2,1)S(1)}, u32[]{:S(2)}, u32[]{:S(2)}) collective-permute-start(bf16[128,512]{1,0:T(8,128)(2,1)S(1)} %shard_map.107), channel_id=1, source_target_pairs={{0,128},{128,0},{1,129},{129,1},{2,130},{130,2},{3,131},{131,3},{4... | collective-permute-start | bytes 393224 | tf_op jit(solution)/shard_map/ppermute | solution.py:27
  183.2 2.0 collective-permute-start.24
  184.5 9.0 %collective-permute-start.22 = (bf16[128,1024]{1,0:T(8,128)(2,1)S(1)}, bf16[128,1024]{1,0:T(8,128)(2,1)S(1)}, u32[]{:S(2)}, u32[]{:S(2)}) collective-permute-start(bf16[128,1024]{1,0:T(8,128)(2,1)S(1)} %fusion.28), channel_id=1, source_target_pairs={{0,128},{128,0},{1,129},{129,1},{2,130},{130,2},{3,131},{131,3},{4... | collective-permute-start | bytes 786440 | tf_op jit(solution)/shard_map/ppermute | solution.py:27
  193.0 1.7 collective-permute-start.25
  (24 other events, 48.7 us)
Sparse Core Ops, SparseCore 0:
  13.9 142.1 all-gather.1
